TPU v7x, 32 devices: a whole 2x2x4 slice. The times are simulated.
32 devices in a mesh: track: 16 (over z, x, core), head: 2 (over y).
Axes of the slice: x: 2, y: 2, z: 4, core: 2. Of those that a mesh axis runs over, the one named last changes fastest.
Arguments:
- residual_in: bfloat16 [16, 256, 2048], P('track', None, 'head')
- queries: bfloat16 [16, 256, 2048], P('track', None, 'head')
- key_vectors: bfloat16 [16, 256, 2048], P('track', None, 'head')
- values: bfloat16 [16, 256, 2048], P('track', None, 'head'), may hold values from -24 to 24
- bar_index: int32 [16, 256], replicated, may hold values from 0 to 31, as said below
- pair_offset: int32 [16, 16, 4], replicated, may hold values from 0 to 14, all different within a row; in each aligned block of 16 rows (0 to 15, 16 to 31, ..., all dimensions but the last counted through in order) at most 8 rows name the same one
- out_proj: bfloat16 [2048, 2048], P('head'), may hold values from -0.125 to 0.125
- norm_gain: bfloat16 [2048], P('head'), may hold values from 0.099609375 to 1.8984375
- router: bfloat16 [2048, 16], P('head'), may hold values from -0.125 to 0.125
- expert_route: int32 [16, 256, 2], P('track'), may hold values from 0 to 15, all different within a row; in each aligned block of 256 rows (0 to 255, 256 to 511, ..., all dimensions but the last counted through in order) at most 64 rows name the same one
- w_gate: bfloat16 [16, 2048, 1408], P('track', None, 'head'), may hold values from -0.125 to 0.125
- w_up: bfloat16 [16, 2048, 1408], P('track', None, 'head'), may hold values from -0.125 to 0.125
- w_down: bfloat16 [16, 1408, 2048], P('track', 'head'), may hold values from -0.15625 to 0.15625
Outputs:
- layer_out: bfloat16 [16, 256, 2048], P('track', None, 'head')
Inputs may be any that keep to these rules, and one draw needn't show every extreme that they name: bar_index[t, 0] = 0, and along a track each event's bar equals the one before or exceeds it by 1; the largest value is reached in every draw. `pair_offset`: the 4 entries of one query block differ; among the 16 query blocks of one track no value appears more than 8 times, and in every draw some track has a value that appears exactly 8 times. `expert_route`: the 2 entries of an event differ; among the 256 events of one track no expert appears more than 64 times, and in every draw some track has an expert that appears exactly 64 times.
All inputs are finite; a program needn't handle non-finite values.
Results may differ from a plain program's by a relative error of at most 0.0054.
Values may be sent and summed in bfloat16 or wider, within the bound.
No kernel may reach another device: no remote copies, remote signals or barrier semaphores. Data moves between devices by JAX's collectives and lax.ppermute only.
A program may use at most 256 MiB of HBM per device.

v0:
```python
import math

import jax
import jax.numpy as jnp
from jax import lax
from jax.sharding import PartitionSpec as P

D = 2048
QB = 16
PAIRS = 4
BAND = 2
TOP = 2
EXP_DEV = 1
HEAD_DIM = 128


MASKED_SCORE = -1e30
NORM_EPSILON = 1e-06


def masked_softmax_parts(scores, allowed):
    ceiling = jnp.max(jnp.where(allowed, scores, MASKED_SCORE), axis=-1)
    weights = jnp.where(allowed, jnp.exp(scores - ceiling[..., None]), 0.0)
    return (ceiling, jnp.sum(weights, axis=-1), weights.astype(jnp.bfloat16))


def merge_sets(self_peak, self_mass, self_value, pair_peak, pair_mass, pair_value):
    ceiling = jnp.maximum(self_peak, jnp.max(pair_peak, axis=1))
    self_scale = jnp.exp(self_peak - ceiling)
    pair_scale = jnp.exp(pair_peak - ceiling[:, None])
    numerator = self_scale[..., None] * self_value + jnp.sum(
        pair_scale[..., None] * pair_value, axis=1
    )
    denominator = self_scale * self_mass + jnp.sum(pair_scale * pair_mass, axis=1)
    return numerator / denominator[..., None]


def pair_tables(pair_offset, tracks):
    item_count = pair_offset.shape[1] * pair_offset.shape[2]
    source = jnp.arange(tracks, dtype=jnp.int32)[:, None]
    target = (source + 1 + pair_offset.reshape(tracks, item_count)) % tracks
    matches = (target[:, :, None] == jnp.arange(tracks, dtype=jnp.int32)).astype(jnp.int32)
    earlier = jnp.sum((jnp.cumsum(matches, axis=1) - matches) * matches, axis=2)
    return (target, earlier)


def local(
    residual_in,
    queries,
    key_vectors,
    values,
    bar_index,
    pair_offset,
    out_proj,
    norm_gain,
    router,
    expert_route,
    w_gate,
    w_up,
    w_down,
):
    tracks = lax.axis_size("track")
    my_track = lax.axis_index("track")
    events = queries.shape[1]
    feature_width = queries.shape[2]
    local_heads = feature_width // HEAD_DIM
    blocks = events // QB
    item_count = blocks * PAIRS
    score_scale = 1.0 / math.sqrt(HEAD_DIM)
    pair_capacity = min(blocks, max(2, 2 * item_count // (tracks - 1)))
    own_query = queries[0].reshape(events, local_heads, HEAD_DIM)
    own_keys = key_vectors[0].reshape(events, local_heads, HEAD_DIM)
    own_values = values[0].reshape(events, local_heads, HEAD_DIM)
    own_bars = lax.dynamic_index_in_dim(bar_index, my_track, 0, keepdims=False)
    position = jnp.arange(events, dtype=jnp.int32)
    self_allowed = (
        (own_bars[None, :] <= own_bars[:, None])
        & (own_bars[None, :] >= own_bars[:, None] - BAND)
        & (position[None, :] <= position[:, None])
    )
    scores = (
        jnp.einsum("qhd,khd->hqk", own_query, own_keys, preferred_element_type=jnp.float32)
        * score_scale
    )
    self_peak, self_mass, self_weights = masked_softmax_parts(scores, self_allowed[None])
    self_value = jnp.einsum(
        "hqk,khd->qhd", self_weights, own_values, preferred_element_type=jnp.float32
    )
    self_peak = jnp.moveaxis(self_peak, 0, -1).reshape(blocks, QB, local_heads)
    self_mass = jnp.moveaxis(self_mass, 0, -1).reshape(blocks, QB, local_heads)
    self_value = self_value.reshape(blocks, QB, local_heads, HEAD_DIM)
    target, earlier = pair_tables(pair_offset, tracks)
    my_target = lax.dynamic_index_in_dim(target, my_track, 0, keepdims=False)
    my_earlier = lax.dynamic_index_in_dim(earlier, my_track, 0, keepdims=False)
    query_bars = own_bars.reshape(blocks, QB)
    block_query = own_query.reshape(blocks, QB, local_heads, HEAD_DIM)
    item_numbers = jnp.arange(item_count, dtype=jnp.int32)
    slot_match = (
        my_target[None, None, :] == jnp.arange(tracks, dtype=jnp.int32)[:, None, None]
    ) & (my_earlier[None, None, :] == jnp.arange(pair_capacity, dtype=jnp.int32)[None, :, None])
    slot_of = jnp.where(
        jnp.any(slot_match, axis=2),
        jnp.sum(jnp.where(slot_match, item_numbers[None, None, :], 0), axis=2),
        item_count,
    )
    starting = (
        jnp.full((item_count, local_heads, QB), MASKED_SCORE, jnp.float32),
        jnp.zeros((item_count, local_heads, QB), jnp.float32),
        jnp.zeros((item_count, QB, local_heads, HEAD_DIM), jnp.float32),
    )
    block_piece = (
        lax.all_gather(key_vectors, "track", axis=0, tiled=True),
        lax.all_gather(values, "track", axis=0, tiled=True),
    )
    amount = block_piece[0].shape[0]
    slots = slot_of.reshape(amount * pair_capacity)
    safe_slots = jnp.minimum(slots, item_count - 1)
    slot_blocks = safe_slots // PAIRS
    slot_query = block_query[slot_blocks]
    slot_bars = query_bars[slot_blocks]
    piece_bars = jnp.repeat(bar_index, pair_capacity, axis=0)
    slot_keys = jnp.repeat(
        block_piece[0].reshape(amount, events, local_heads, HEAD_DIM), pair_capacity, axis=0
    )
    slot_values = jnp.repeat(
        block_piece[1].reshape(amount, events, local_heads, HEAD_DIM), pair_capacity, axis=0
    )
    slot_allowed = (piece_bars[:, None, :] <= slot_bars[:, :, None]) & (
        piece_bars[:, None, :] >= slot_bars[:, :, None] - BAND
    )
    slot_scores = (
        jnp.einsum("iqhd,ikhd->ihqk", slot_query, slot_keys, preferred_element_type=jnp.float32)
        * score_scale
    )
    new_peak, new_mass, new_weights = masked_softmax_parts(slot_scores, slot_allowed[:, None])
    new_value = jnp.einsum(
        "ihqk,ikhd->iqhd", new_weights, slot_values, preferred_element_type=jnp.float32
    )
    item_peak = starting[0].at[slots].set(new_peak, mode="drop")
    item_mass = starting[1].at[slots].set(new_mass, mode="drop")
    pair_value = starting[2].at[slots].set(new_value, mode="drop")
    pair_peak = jnp.moveaxis(item_peak, 1, -1)
    pair_mass = jnp.moveaxis(item_mass, 1, -1)
    merged = merge_sets(
        self_peak,
        self_mass,
        self_value,
        pair_peak.reshape(blocks, PAIRS, QB, local_heads),
        pair_mass.reshape(blocks, PAIRS, QB, local_heads),
        pair_value.reshape(blocks, PAIRS, QB, local_heads, HEAD_DIM),
    )
    attended = merged.reshape(events, feature_width).astype(jnp.bfloat16)
    projected = jnp.dot(attended, out_proj, preferred_element_type=jnp.float32)
    summed = lax.psum_scatter(projected, "head", scatter_dimension=1, tiled=True)
    hidden = (residual_in[0].astype(jnp.float32) + summed).astype(jnp.bfloat16)
    hidden_wide = lax.optimization_barrier(hidden).astype(jnp.float32)
    square = lax.psum(jnp.sum(hidden_wide * hidden_wide, axis=1), "head")
    normed = (
        hidden_wide * lax.rsqrt(square / D + NORM_EPSILON)[:, None] * norm_gain.astype(jnp.float32)
    ).astype(jnp.bfloat16)
    logits = lax.psum(
        jnp.dot(normed, router, preferred_element_type=jnp.float32).astype(jnp.bfloat16), "head"
    ).astype(jnp.float32)
    experts = tracks * EXP_DEV
    capacity = 2 * events * TOP // experts
    own_route = expert_route[0]
    matches = own_route[:, :, None] == jnp.arange(experts, dtype=jnp.int32)
    chosen = jnp.sum(jnp.where(matches, logits[:, None, :], 0.0), axis=2)
    sigmoid_vals = jax.nn.sigmoid(chosen)
    gate_share = sigmoid_vals / jnp.sum(sigmoid_vals, axis=1, keepdims=True)
    flat_route = own_route.reshape(-1)
    route_hits = (flat_route[:, None] == jnp.arange(experts, dtype=jnp.int32)).astype(jnp.int32)
    slot_rank = jnp.sum((jnp.cumsum(route_hits, axis=0) - route_hits) * route_hits, axis=1)
    slot_index = flat_route * capacity + slot_rank
    token_of = jnp.arange(events * TOP, dtype=jnp.int32) // TOP
    full_rows = lax.all_gather(normed, "head", axis=1, tiled=True)
    outgoing = (
        jnp.zeros((experts * capacity, full_rows.shape[1]), jnp.bfloat16)
        .at[slot_index]
        .set(full_rows[token_of])
    )
    expert_rows = lax.all_to_all(
        outgoing.reshape(tracks, capacity, full_rows.shape[1]),
        "track",
        split_axis=0,
        concat_axis=0,
        tiled=True,
    )
    expert_rows = expert_rows.reshape(tracks * capacity, full_rows.shape[1])
    gate_pre = jnp.dot(expert_rows, w_gate[0], preferred_element_type=jnp.float32)
    up_pre = jnp.dot(expert_rows, w_up[0], preferred_element_type=jnp.float32)
    activated = (jax.nn.silu(gate_pre) * up_pre).astype(jnp.bfloat16)
    down_terms = lax.optimization_barrier(
        jnp.dot(activated, w_down[0], preferred_element_type=jnp.float32).astype(jnp.bfloat16)
    ).astype(jnp.float32)
    expert_out = lax.psum_scatter(
        down_terms.astype(jnp.bfloat16), "head", scatter_dimension=1, tiled=True
    )
    returned = lax.all_to_all(
        expert_out.reshape(tracks, capacity, feature_width),
        "track",
        split_axis=0,
        concat_axis=0,
        tiled=True,
    )
    picked = (
        returned.reshape(tracks * capacity, feature_width)[slot_index]
        .reshape(events, TOP, feature_width)
        .astype(jnp.float32)
    )
    layer_out = (hidden_wide + jnp.sum(gate_share[:, :, None] * picked, axis=1)).astype(
        jnp.bfloat16
    )
    return layer_out[None]


def solution(mesh):
    in_specs = (
        P("track", None, "head"),
        P("track", None, "head"),
        P("track", None, "head"),
        P("track", None, "head"),
        P(),
        P(),
        P("head", None),
        P("head"),
        P("head", None),
        P("track", None, None),
        P("track", None, "head"),
        P("track", None, "head"),
        P("track", "head", None),
    )
    out_specs = P("track", None, "head")
    return jax.shard_map(local, mesh=mesh, in_specs=in_specs, out_specs=out_specs, check_vma=False)
```

profile of v0, /device:TPU:0, one launch (start us, length us, event | category | flops | bytes accessed | tf_op | source)
XLA Modules:
  0.0 624.5 jit_solution(18046244713905716611)
XLA Ops:
  8.1 2.0 copy.128
  11.0 1.4 select_reduce_fusion.2
  13.9 1.3 fusion.67
  16.5 1.2 gather_fusion
  17.7 3.0 gather_fusion.1
  20.7 1.2 copy.133
  22.1 1.9 select_reduce_fusion.1
  24.1 2.0 fusion.23
  26.8 3.4 fusion.29
  30.2 2.5 copy.116
  32.8 2.8 compare_and_fusion
  35.6 51.6 %all-gather.4.cloned.1.call-done = bf16[16,256,1024]{2,1,0:T(8,128)(2,1)} async-done(((bf16[1,256,1024]{2,1,0:T(8,128)(2,1)}), bf16[16,256,1024]{2,1,0:T(8,128)(2,1)}) %all-gather.4.cloned.1.call-update) | async-done | bytes 8388624 | tf_op jit(solution)/shard_map/all_gather | solution.py:112
  87.1 8.9 %copy_bitcast_fusion.1 = bf16[16,256,8,128]{3,1,2,0:T(8,128)(2,1)} fusion(bf16[16,256,1024]{2,1,0:T(8,128)(2,1)} %all-gather.4.cloned.1.call-done), kind=kLoop, calls=%fused_computation.14 | loop fusion | bytes 16777216 | tf_op jit(solution)/shard_map/reshape | solution.py:123
  96.1 24.6 %broadcast_in_dim.138 = bf16[16,8,256,8,128]{4,2,3,1,0:T(8,128)(2,1)} broadcast(bf16[16,256,8,128]{3,1,2,0:T(8,128)(2,1)} %copy_bitcast_fusion.1), dimensions={0,2,3,4} | broadcast | bytes 75497472 | tf_op jit(solution)/shard_map/broadcast_in_dim | solution.py:122
  120.6 44.4 %select_reduce_fusion = (f32[128,8,16]{2,1,0:T(8,128)}, f32[128,8,16,256]{3,2,1,0:T(8,128)}) fusion(pred[128,16,256]{2,1,0:T(8,128)(4,1)S(1)} %compare_and_fusion, bf16[128,256,8,128]{3,1,2,0:T(8,128)(2,1)} %bitcast.7, bf16[128,16,8,128]{3,2,1,0:T(8,128)(2,1)} %gather_fusion.1), kind=kOutput, calls=%fused_computation.9 | convolution fusion | flops 1086308352 | bytes 88670208 | tf_op jit(solution)/shard_map/iqhd,ikhd->ihqk/dot_general | solution.py:132
  165.0 9.9 %fusion = f32[128,8,16]{2,1,0:T(8,128)} fusion(f32[128,8,16,256]{3,2,1,0:T(8,128)} %get-tuple-element.14, f32[128,8,16]{2,1,0:T(8,128)} %get-tuple-element.13, pred[128,16,256]{2,1,0:T(8,128)(4,1)S(1)} %compare_and_fusion), kind=kLoop, calls=%fused_computation.10 | loop fusion | flops 16760832 | bytes 17432576 | tf_op jit(solution)/shard_map/reduce_sum | solution.py:24
  174.9 9.0 %copy_bitcast_fusion = bf16[16,256,8,128]{3,1,2,0:T(8,128)(2,1)} fusion(bf16[16,256,1024]{2,1,0:T(8,128)(2,1)} %all-gather.6.cloned.1.call-done), kind=kLoop, calls=%fused_computation.13 | loop fusion | bytes 16777216 | tf_op jit(solution)/shard_map/reshape | solution.py:126
  183.9 24.3 %broadcast_in_dim.143 = bf16[16,8,256,8,128]{4,2,3,1,0:T(8,128)(2,1)} broadcast(bf16[16,256,8,128]{3,1,2,0:T(8,128)(2,1)} %copy_bitcast_fusion), dimensions={0,2,3,4} | broadcast | bytes 75497472 | tf_op jit(solution)/shard_map/broadcast_in_dim | solution.py:125
  208.2 31.7 %fusion.10 = f32[128,16,8,128]{3,1,2,0:T(8,128)} fusion(bf16[128,256,8,128]{3,1,2,0:T(8,128)(2,1)} %bitcast.14, f32[128,8,16,256]{3,2,1,0:T(8,128)} %get-tuple-element.14, f32[128,8,16]{2,1,0:T(8,128)} %get-tuple-element.13, pred[128,16,256]{2,1,0:T(8,128)(4,1)S(1)} %compare_and_fusion), kind=kOutput, calls=%fused_computation.23 | convolution fusion | flops 1090519040 | bytes 92864512 | tf_op jit(solution)/shard_map/ihqk,ikhd->iqhd/dot_general | solution.py:136
  240.0 10.8 %copy.119 = f32[128,16,8,128]{3,2,1,0:T(8,128)} copy(f32[128,16,8,128]{3,1,2,0:T(8,128)} %fusion.10) | data formatting | bytes 16777216 | tf_op jit(solution)/shard_map/ihqk,ikhd->iqhd/transpose | solution.py:136
  251.5 13.7 %scatter_fusion = f32[64,8,16]{2,1,0:T(8,128)} fusion(f32[64,8,16]{2,1,0:T(8,128)} %broadcast_in_dim.131, s32[128]{0:T(128)S(1)} %get-tuple-element.12, f32[128,8,16]{2,1,0:T(8,128)S(1)} %copy-done.1), kind=kCustom, calls=%fused_computation.4 | custom fusion | bytes 197120 | tf_op jit(solution)/shard_map/scatter | solution.py:139
  266.2 8.2 %scatter_fusion.2 = f32[64,8,16]{2,1,0:T(8,128)S(1)} fusion(f32[64,8,16]{2,1,0:T(8,128)S(1)} %broadcast_in_dim.144, s32[128]{0:T(128)S(1)} %get-tuple-element.12, f32[128,8,16]{2,1,0:T(8,128)} %fusion), kind=kCustom, calls=%fused_computation.6 | custom fusion | bytes 197120 | tf_op jit(solution)/shard_map/scatter | solution.py:140
  274.4 2.3 multiply_reduce_fusion.2
  276.7 1.2 copy.117
  277.9 1.6 fusion.53
  280.4 1.6 copy.121
  282.0 2.5 broadcast_in_dim.141
  284.5 22.7 %scatter_fusion.1 = f32[64,16,8,128]{3,2,1,0:T(8,128)} fusion(f32[64,16,8,128]{3,2,1,0:T(8,128)} %broadcast_in_dim.141, s32[128]{0:T(128)S(1)} %get-tuple-element.12, f32[128,16,8,128]{3,2,1,0:T(8,128)} %copy.119), kind=kCustom, calls=%fused_computation.5 | custom fusion | bytes 25166336 | tf_op jit(solution)/shard_map/scatter | solution.py:141
  307.2 3.1 multiply_reduce_fusion
  311.0 3.0 fusion.43
  314.5 30.1 %reduce-scatter.3.cloned.1.call-done = f32[256,1024]{1,0:T(8,128)} async-done(((f32[256,2048]{1,0:T(8,128)}), f32[256,1024]{1,0:T(8,128)}) %reduce-scatter.3.cloned.1.call-update) | async-done | bytes 1048592 | tf_op jit(solution)/shard_map/reduce_scatter | solution.py:154
  344.6 1.5 fusion.32
  346.3 5.2 psum.14
  352.6 1.2 reduce-window.6
  355.5 18.4 %all-gather.8.cloned.1.call-done = bf16[256,2048]{1,0:T(8,128)(2,1)} async-done(((bf16[256,1024]{1,0:T(8,128)(2,1)}), bf16[256,2048]{1,0:T(8,128)(2,1)}) %all-gather.8.cloned.1.call-update) | async-done | bytes 1048592 | tf_op jit(solution)/shard_map/all_gather | solution.py:176
  373.9 12.1 %scatter_custom_fusion.3 = bf16[1024,2048]{1,0:T(8,128)(2,1)} fusion(s32[512]{0:T(512)S(1)} %bitcast.150, bf16[256,2048]{1,0:T(8,128)(2,1)} %all-gather.8.cloned.1.call-done, s32[1024]{0:T(1024)S(1)} %pad_clamp_fusion.1, bf16[]{:T(256)} %constant.111.clone.1), kind=kCustom, calls=%fused_computation.30 | custom fusion | bytes 4194816 | tf_op jit(solution)/shard_map/scatter | solution.py:180
  386.0 98.4 %all_to_all.10 = bf16[16,64,2048]{2,1,0:T(8,128)(2,1)S(1)} all-to-all(bf16[16,64,2048]{2,1,0:T(8,128)(2,1)} %bitcast.132), channel_id=1, replica_groups=mesh['track'=16,'head'=2] {'track'}, dimensions={0} | all-to-all | bytes 8388608 | tf_op jit(solution)/shard_map/all_to_all | solution.py:182
  484.4 2.0 copy-done.2
  486.4 4.8 fusion.14
  491.2 11.3 %convolution_convert_fusion = bf16[1024,2048]{1,0:T(8,128)(2,1)} fusion(bf16[1,704,2048]{2,1,0:T(8,128)(2,1)S(1)} %copy-done, f32[1024,704]{0,1:T(8,128)} %fusion.14, bf16[1024,2048]{1,0:T(8,128)(2,1)} %bitcast.135, bf16[1,2048,704]{1,2,0:T(8,128)(2,1)} %param.23), kind=kOutput, calls=%fused_computation.22 | convolution fusion | flops 5912002560 | bytes 17039360 | tf_op jit(solution)/shard_map/dot_general | solution.py:194
  502.5 54.1 %reduce-scatter.5.cloned.1.call-done = bf16[1024,1024]{1,0:T(8,128)(2,1)} async-done(((bf16[1024,2048]{1,0:T(8,128)(2,1)}), bf16[1024,1024]{1,0:T(8,128)(2,1)}) %reduce-scatter.5.cloned.1.call-update) | async-done | bytes 2097168 | tf_op jit(solution)/shard_map/reduce_scatter | solution.py:196
  556.6 5.7 all-to-all-start.1
  562.3 1.3 convolution_convert_fusion.1
  563.6 5.0 psum.15
  568.9 34.6 %all-to-all-done.1 = bf16[16,64,1024]{2,1,0:T(8,128)(2,1)} async-done(((bf16[16,64,1024]{2,1,0:T(8,128)(2,1)}), bf16[16,64,1024]{2,1,0:T(8,128)(2,1)}, u32[]{:S(2)}, u32[]{:S(2)}) %all-to-all-start.1) | async-done | bytes 2097184 | tf_op jit(solution)/shard_map/all_to_all | solution.py:199
  603.5 5.3 gather_fusion.2
  608.8 3.4 reshape.506
  612.2 4.3 multiply_reduce_fusion.1
  (89 shorter events, 14.1 us)
Async XLA Ops:
  6.5 484.7 %copy-start = (bf16[1,704,2048]{2,1,0:T(8,128)(2,1)S(1)}, bf16[1,704,2048]{2,1,0:T(8,128)(2,1)}, u32[]{:S(2)}) copy-start(bf16[1,704,2048]{2,1,0:T(8,128)(2,1)} %param.25) | copy-start | bytes 8650756
  6.5 80.6 %all-gather.4.cloned.1.call-start = ((), (), s32[]{:S(2)}) async-start(), calls=%async_computation.4 | async-start | bytes 8912896 | tf_op jit(solution)/shard_map/all_gather | solution.py:112
  7.3 167.7 %all-gather.6.cloned.1.call-start = ((), (), s32[]{:S(2)}) async-start(), calls=%async_computation.5 | async-start | bytes 8912896 | tf_op jit(solution)/shard_map/all_gather | solution.py:113
  8.0 336.6 %reduce-scatter.3.cloned.1.call-start = ((), (), s32[]{:S(2)}) async-start(), calls=%async_computation.6 | async-start | bytes 3145728 | tf_op jit(solution)/shard_map/reduce_scatter | solution.py:154
  24.0 8.7 %copy-start.4 = (s32[128,16]{1,0:T(8,128)S(1)}, s32[128,16]{1,0:T(8,128)}, u32[]{:S(2)}) copy-start(s32[128,16]{1,0:T(8,128)} %gather_fusion) | copy-start | bytes 24580
  24.0 8.8 %copy-start.8 = (s32[16,256]{1,0:T(8,128)S(1)}, s32[16,256]{1,0:T(8,128)}, u32[]{:S(2)}) copy-start(s32[16,256]{1,0:T(8,128)} %param.17) | copy-start | bytes 49156
  240.0 11.5 %copy-start.1 = (f32[128,8,16]{2,1,0:T(8,128)S(1)}, f32[128,8,16]{2,1,0:T(8,128)}, u32[]{:S(2)}) copy-start(f32[128,8,16]{2,1,0:T(8,128)} %get-tuple-element.13) | copy-start | bytes 196612
  307.2 3.4 copy-start.5
  307.2 3.8 copy-start.3
  307.2 3.8 copy-start.11
  311.0 3.0 copy-start.9
  311.0 3.5 copy-start.10
  314.0 59.9 %all-gather.8.cloned.1.call-start = ((), (), s32[]{:S(2)}) async-start(), calls=%async_computation.7 | async-start | bytes 1572864 | tf_op jit(solution)/shard_map/all_gather | solution.py:176
  352.5 204.2 %reduce-scatter.5.cloned.1.call-start = ((), (), s32[]{:S(2)}) async-start(), calls=%async_computation.8 | async-start | bytes 6291456 | tf_op jit(solution)/shard_map/reduce_scatter | solution.py:196
  353.7 0.6 copy-start.6
  386.0 100.4 %copy-start.12 = (bf16[1,2048,704]{1,2,0:T(8,128)(2,1)S(1)}, bf16[1,2048,704]{1,2,0:T(8,128)(2,1)}, u32[]{:S(2)}) copy-start(bf16[1,2048,704]{1,2,0:T(8,128)(2,1)} %param.24) | copy-start | bytes 8650756
  484.4 2.0 copy-start.2
  502.5 59.8 %copy-start.7 = (bf16[1024,16]{0,1:T(8,128)(2,1)S(1)}, bf16[1024,16]{0,1:T(8,128)(2,1)}, u32[]{:S(2)}) copy-start(bf16[1024,16]{0,1:T(8,128)(2,1)} %param.21) | copy-start | bytes 98308
  556.6 46.8 %all-to-all-start.1 = ((bf16[16,64,1024]{2,1,0:T(8,128)(2,1)}), bf16[16,64,1024]{2,1,0:T(8,128)(2,1)}, u32[]{:S(2)}, u32[]{:S(2)}) async-start(bf16[16,64,1024]{2,1,0:T(8,128)(2,1)} %bitcast.137), calls=%async_computation.3 | async-start | bytes 4194304 | tf_op jit(solution)/shard_map/all_to_all | solution.py:199
Sparse Core Ops, SparseCore 0:
  9.5 77.5 all-gather.3
  89.3 73.1 all-gather.5
  314.1 30.4 reduce-scatter.2
  352.6 21.2 all-gather.7
  502.6 53.9 reduce-scatter.4
where the time goes:
time: 636 us; the launch traced here: 624 us
  waiting for transfers between devices  190 us (30%)
  local copies, waits for them, and re-layouts  169 us (27%)
  blocking collectives  109 us (17%)
  matrix products  102 us (16%)
  other arithmetic  35.1 us (6%)
  between operations  14 us (2%)
    all_to_all x1, blocking collectives, local(): lax.all_to_all(outgoing.reshape(tracks, capacity, full_rows.shape[1]), 't...  98.4 us
    reduce_scatter x1, waiting for transfers between devices, local(): lax.psum_scatter(down_terms.astype(jnp.bfloat16), 'head', scatter_dimensi...  54.1 us
    all_gather x1, waiting for transfers between devices, local(): lax.all_gather(key_vectors, 'track', axis=0, tiled=True)  51.6 us
    dot_general x1, matrix products, local(): jnp.einsum('iqhd,ikhd->ihqk', slot_query, slot_keys, preferred_element_ty...  44.4 us
    all_to_all x1, waiting for transfers between devices, local(): lax.all_to_all(expert_out.reshape(tracks, capacity, feature_width), 'trac...  34.6 us
    dot_general x1, matrix products, local(): jnp.einsum('ihqk,ikhd->iqhd', new_weights, slot_values, preferred_element...  31.7 us
    reduce_scatter x1, waiting for transfers between devices, local(): lax.psum_scatter(projected, 'head', scatter_dimension=1, tiled=True)  30.1 us
    broadcast_in_dim x1, local copies, waits for them, and re-layouts, local(): jnp.repeat(block_piece[0].reshape(amount, events, local_heads, HEAD_DIM),...  24.6 us
  transfers between devices with their start and end apart: 6, of which 5 were waited for; matrix products, arithmetic and copies ran while one was open for 19% of the time, Pallas kernels for 0%

commit v1 on v0

v1 whole, which is shorter than its diff:
```python
import functools
import math

import jax
import jax.numpy as jnp
from jax import lax
from jax.experimental import pallas as pl
from jax.experimental.pallas import tpu as pltpu
from jax.sharding import PartitionSpec as P

D = 2048
QB = 16
PAIRS = 4
BAND = 2
TOP = 2
HEAD_DIM = 128
HEAD_CHUNKS = 2
SLOT_CHUNKS = 4
LANES = 128

MASKED_SCORE = -1e30
NO_CAP = 3e38
NORM_EPSILON = 1e-06
F32 = jnp.float32
BF16 = jnp.bfloat16


def dot(a, b):
    return jnp.dot(a, b, preferred_element_type=F32)


def dot_nt(a, b):
    return lax.dot_general(a, b, (((1,), (1,)), ((), ())), preferred_element_type=F32)


def chip_ring(rows, columns):
    order = []
    for row in range(rows):
        inner = list(range(1, columns))
        order += [(row, x) for x in (inner if row % 2 == 0 else inner[::-1])]
    order += [(row, 0) for row in range(rows - 1, -1, -1)]
    return [z * columns + x for z, x in order]


def shifted(x, axis, size, shift):
    return lax.ppermute(x, axis, [(i, (i + shift) % size) for i in range(size)])


def swap_cores(x, tracks):
    return lax.ppermute(x, "track", [(i, i ^ 1) for i in range(tracks)])


def attention_kernel(blocks, heads, *refs):
    q_ref, qbar_ref, kbar_ref = refs[:3]
    kv_refs = refs[3 : 3 + blocks]
    own_ref, other_ref, cap_ref = refs[3 + blocks :]
    head = pl.program_id(0)
    events = q_ref.shape[1]
    exponent_scale = math.log2(math.e) / math.sqrt(HEAD_DIM)
    tile = 128

    @pl.when(head == 0)
    def _():
        row = lax.broadcasted_iota(jnp.int32, (events, events), 0)
        column = lax.broadcasted_iota(jnp.int32, (events, events), 1)
        for side in range(2):
            for b in range(blocks):
                back = qbar_ref[side, :, b : b + 1] - kbar_ref[b : b + 1, :]
                allowed = (back >= 0) & (back <= BAND)
                if side == 0 and b == 0:
                    allowed = allowed & (column <= row)
                cap_ref[side, :, b * events : (b + 1) * events] = jnp.where(
                    allowed, NO_CAP, MASKED_SCORE
                )

    lane = lax.broadcasted_iota(jnp.int32, (tile, LANES), 1)
    for side, out_ref in enumerate((own_ref, other_ref)):
        for start in range(0, events, tile):
            rows = pl.ds(start, tile)
            query = q_ref[side, rows, :]
            scores = [
                jnp.minimum(
                    dot_nt(query, kv_refs[b][0]), cap_ref[side, rows, b * events : (b + 1) * events]
                )
                for b in range(blocks)
            ]
            peak = functools.reduce(jnp.maximum, scores).max(axis=1, keepdims=True)
            mass = jnp.zeros((tile, events), F32)
            value = jnp.zeros((tile, HEAD_DIM), F32)
            for b in range(blocks):
                weights = jnp.exp2((scores[b] - peak) * exponent_scale)
                mass = mass + weights
                value = value + dot(weights.astype(BF16), kv_refs[b][1])
            mass = mass.sum(axis=1, keepdims=True)
            out_ref[rows, pl.ds(pl.multiple_of(head * HEAD_DIM, HEAD_DIM), HEAD_DIM)] = value
            stat = jnp.where(lane == head, peak, jnp.where(lane == heads + head, mass, 0.0))

            @pl.when(head == 0)
            def _():
                out_ref[rows, heads * HEAD_DIM :] = stat

            @pl.when(head != 0)
            def _():
                out_ref[rows, heads * HEAD_DIM :] += stat


def attention(q, qbar, kbar, kvs):
    blocks, events, width = len(kvs), q.shape[1], q.shape[2]
    heads = width // HEAD_DIM
    shape = jax.ShapeDtypeStruct((events, width + LANES), F32)
    flops = 4 * 2 * events * blocks * events * width
    return pl.pallas_call(
        functools.partial(attention_kernel, blocks, heads),
        grid=(heads,),
        in_specs=[
            pl.BlockSpec((2, events, HEAD_DIM), lambda h: (0, 0, h)),
            pl.BlockSpec(qbar.shape, lambda h: (0, 0, 0)),
            pl.BlockSpec(kbar.shape, lambda h: (0, 0)),
        ]
        + [pl.BlockSpec((2, events, HEAD_DIM), lambda h: (0, 0, h))] * blocks,
        out_specs=[pl.BlockSpec(shape.shape, lambda h: (0, 0))] * 2,
        out_shape=[shape, shape],
        scratch_shapes=[pltpu.VMEM((2, events, blocks * events), F32)],
        cost_estimate=pl.CostEstimate(
            flops=flops, bytes_accessed=blocks * events * width * 4, transcendentals=flops // 512
        ),
        name="attention",
    )(q, qbar, kbar, *kvs)


def merge_kernel(heads, a_ref, b_ref, out_ref):
    scale = 1.0 / math.sqrt(HEAD_DIM)
    for head in range(heads):
        at = heads * HEAD_DIM + head
        peak_a, mass_a = a_ref[:, at : at + 1], a_ref[:, at + heads : at + heads + 1]
        peak_b, mass_b = b_ref[:, at : at + 1], b_ref[:, at + heads : at + heads + 1]
        peak = jnp.maximum(peak_a, peak_b)
        scale_a = jnp.exp((peak_a - peak) * scale)
        scale_b = jnp.exp((peak_b - peak) * scale)
        part = slice(head * HEAD_DIM, (head + 1) * HEAD_DIM)
        total = scale_a * a_ref[:, part] + scale_b * b_ref[:, part]
        out_ref[:, part] = (total / (scale_a * mass_a + scale_b * mass_b)).astype(BF16)


def merge(a, b):
    events, width = a.shape[0], a.shape[1] - LANES
    return pl.pallas_call(
        functools.partial(merge_kernel, width // HEAD_DIM),
        out_shape=jax.ShapeDtypeStruct((events, width), BF16),
        cost_estimate=pl.CostEstimate(
            flops=8 * events * width, bytes_accessed=10 * events * width, transcendentals=0
        ),
        name="merge",
    )(a, b)


def project_kernel(sources, chunks, experts, *refs):
    attended = refs[: sources * chunks]
    weights = refs[sources * chunks : sources * chunks + sources]
    residual_ref, gain_ref, router_ref, hidden_ref, stat_ref = refs[sources * chunks + sources :]
    step = pl.program_id(0)
    total = residual_ref[...].astype(F32)
    for source in range(sources):
        for chunk in range(chunks):
            part = attended[source * chunks + chunk][...]
            width = part.shape[1]
            total = total + dot(part, weights[source][chunk * width : (chunk + 1) * width, :])
    hidden = total.astype(BF16)
    hidden_ref[...] = hidden
    wide = hidden.astype(F32)
    scaled = (wide * gain_ref[...].astype(F32)).astype(BF16)
    lane = lax.broadcasted_iota(jnp.int32, stat_ref.shape, 1)
    square = jnp.sum(wide * wide, axis=1, keepdims=True)
    stat = dot(scaled, router_ref[...]) + jnp.where(lane == experts, square, 0.0)

    @pl.when(step == 0)
    def _():
        stat_ref[...] = stat

    @pl.when(step != 0)
    def _():
        stat_ref[...] += stat


def project(attended, weights, residual, gain, router, experts):
    events, width = residual.shape
    sources, chunks = len(attended), len(attended[0])
    tile = 256
    flat = [part for source in attended for part in source]
    return pl.pallas_call(
        functools.partial(project_kernel, sources, chunks, experts),
        grid=(width // tile,),
        in_specs=[pl.BlockSpec(part.shape, lambda j: (0, 0)) for part in flat]
        + [pl.BlockSpec((w.shape[0], tile), lambda j: (0, j)) for w in weights]
        + [
            pl.BlockSpec((events, tile), lambda j: (0, j)),
            pl.BlockSpec((1, tile), lambda j: (0, j)),
            pl.BlockSpec((tile, LANES), lambda j: (j, 0)),
        ],
        out_specs=[
            pl.BlockSpec((events, tile), lambda j: (0, j)),
            pl.BlockSpec((events, LANES), lambda j: (0, 0)),
        ],
        out_shape=[
            jax.ShapeDtypeStruct((events, width), BF16),
            jax.ShapeDtypeStruct((events, LANES), F32),
        ],
        cost_estimate=pl.CostEstimate(
            flops=2 * events * D * width, bytes_accessed=2 * D * width, transcendentals=0
        ),
        name="project",
    )(*flat, *weights, residual, gain, router)


def pack_kernel(sources, chunks, experts, *refs):
    hidden_ref = refs[0]
    stats = refs[1 : 1 + sources]
    gain_ref, route_ref, code_ref = refs[1 + sources : 4 + sources]
    outs = refs[4 + sources : 4 + sources + chunks]
    gate_ref = refs[4 + sources + chunks]
    total = functools.reduce(jnp.add, [s[...] for s in stats])
    lane = lax.broadcasted_iota(jnp.int32, total.shape, 1)
    square = jnp.sum(jnp.where(lane == experts, total, 0.0), axis=1, keepdims=True)
    inverse = lax.rsqrt(square / D + NORM_EPSILON)
    normed = (hidden_ref[...].astype(F32) * inverse * gain_ref[...].astype(F32)).astype(BF16)
    rows, events = outs[0].shape[0], normed.shape[0]
    tile = min(rows, 256)
    row = lax.broadcasted_iota(jnp.int32, (tile, events), 0)
    for chunk in range(chunks):
        for start in range(0, rows, tile):
            at = row + (chunk * rows + start)
            hit = (code_ref[0:1, :] == at) | (code_ref[1:2, :] == at)
            pick = jnp.where(hit, 1.0, 0.0).astype(BF16)
            outs[chunk][start : start + tile, :] = dot(pick, normed).astype(BF16)
    logits = total * inverse
    parts = []
    for k in range(TOP):
        chosen = jnp.sum(
            jnp.where(lane == route_ref[:, k : k + 1], logits, 0.0), axis=1, keepdims=True
        )
        parts.append(1.0 / (1.0 + jnp.exp(-chosen)))
    whole = parts[0] + parts[1]
    gate_ref[...] = jnp.where(
        lane == 0, parts[0] / whole, jnp.where(lane == 1, parts[1] / whole, 0.0)
    )


def pack(hidden, stats, gain, route, code_rows, chunks, rows, experts):
    events, width = hidden.shape
    out = jax.ShapeDtypeStruct((rows, width), BF16)
    return pl.pallas_call(
        functools.partial(pack_kernel, len(stats), chunks, experts),
        out_shape=[out] * chunks + [jax.ShapeDtypeStruct((events, LANES), F32)],
        cost_estimate=pl.CostEstimate(
            flops=2 * events * chunks * rows * width,
            bytes_accessed=2 * chunks * rows * width,
            transcendentals=0,
        ),
        name="pack",
    )(hidden, *stats, gain, route, code_rows)


def expert_in_kernel(sources, per_source, kmap_ref, *refs):
    rows = refs[:sources]
    gate_ref, up_ref, out_ref, gate_sum, up_sum = refs[sources:]
    step = pl.program_id(0)

    @pl.when(step == 0)
    def _():
        gate_sum[...] = jnp.zeros_like(gate_sum)
        up_sum[...] = jnp.zeros_like(up_sum)

    for source in range(sources):

        @pl.when(step // per_source == source)
        def _():
            x = rows[source][...]
            gate_sum[...] += dot(x, gate_ref[0])
            up_sum[...] += dot(x, up_ref[0])

    @pl.when(step == pl.num_programs(0) - 1)
    def _():
        gate = gate_sum[...]
        out_ref[...] = (gate / (1.0 + jnp.exp(-gate)) * up_sum[...]).astype(BF16)


def expert_in(rows, w_gate, w_up, my_head):
    sources = len(rows)
    count, width = rows[0].shape
    units = w_gate.shape[2]
    tile = 512
    per_source = width // tile
    steps = sources * per_source
    number = jnp.arange(steps, dtype=jnp.int32)
    kmap = (my_head - number // per_source + sources) % sources * per_source + number % per_source

    def row_map(source):
        return lambda k, m: (0, jnp.clip(k - source * per_source, 0, per_source - 1))

    weight = pl.BlockSpec((1, tile, units), lambda k, m: (0, m[k], 0))
    return pl.pallas_call(
        functools.partial(expert_in_kernel, sources, per_source),
        grid_spec=pltpu.PrefetchScalarGridSpec(
            num_scalar_prefetch=1,
            grid=(steps,),
            in_specs=[pl.BlockSpec((count, tile), row_map(s)) for s in range(sources)]
            + [weight, weight],
            out_specs=pl.BlockSpec((count, units), lambda k, m: (0, 0)),
            scratch_shapes=[pltpu.VMEM((count, units), F32)] * 2,
        ),
        out_shape=jax.ShapeDtypeStruct((count, units), BF16),
        cost_estimate=pl.CostEstimate(
            flops=4 * count * D * units, bytes_accessed=4 * D * units, transcendentals=count * units
        ),
        name="expert_in",
    )(kmap, *rows, w_gate, w_up)


def expert_out_kernel(sources, *refs):
    out_ref = refs[2 * sources]
    total = dot(refs[0][...], refs[sources][...])
    for s in range(1, sources):
        total = total + dot(refs[s][...], refs[sources + s][...])
    out_ref[...] = total.astype(BF16)


def expert_out(acts, weights):
    sources = len(acts)
    count, units = acts[0].shape
    width = weights[0].shape[1]
    tile = 256
    return pl.pallas_call(
        functools.partial(expert_out_kernel, sources),
        grid=(width // tile,),
        in_specs=[pl.BlockSpec((count, units), lambda j: (0, 0))] * sources
        + [pl.BlockSpec((units, tile), lambda j: (0, j))] * sources,
        out_specs=pl.BlockSpec((count, tile), lambda j: (0, j)),
        out_shape=jax.ShapeDtypeStruct((count, width), BF16),
        cost_estimate=pl.CostEstimate(
            flops=2 * sources * count * units * width,
            bytes_accessed=2 * sources * units * width,
            transcendentals=0,
        ),
        name="expert_out",
    )(*acts, *weights)


def combine_kernel(chunks, *refs):
    hidden_ref, gate_ref, code_ref = refs[:3]
    returned = refs[3 : 3 + chunks]
    out_ref = refs[3 + chunks]
    total = hidden_ref[...].astype(F32)
    events, rows = total.shape[0], returned[0].shape[0]
    column = lax.broadcasted_iota(jnp.int32, (events, rows), 1)
    picked = [None] * TOP
    for chunk in range(chunks):
        back = returned[chunk][...]
        for k in range(TOP):
            hit = column + chunk * rows == code_ref[:, k : k + 1]
            part = dot(jnp.where(hit, 1.0, 0.0).astype(BF16), back)
            picked[k] = part if chunk == 0 else picked[k] + part
    share = picked[0] * gate_ref[:, 0:1]
    for k in range(1, TOP):
        share = share + picked[k] * gate_ref[:, k : k + 1]
    out_ref[...] = (total + share).astype(BF16)


def combine(hidden, gates, code_columns, returned):
    events, width = hidden.shape
    chunks, rows = len(returned), returned[0].shape[0]
    return pl.pallas_call(
        functools.partial(combine_kernel, chunks),
        out_shape=jax.ShapeDtypeStruct((events, width), BF16),
        cost_estimate=pl.CostEstimate(
            flops=4 * events * chunks * rows * width,
            bytes_accessed=2 * chunks * rows * width,
            transcendentals=0,
        ),
        name="combine",
    )(hidden, gates, code_columns, *returned)


def local(
    order,
    residual_in,
    queries,
    key_vectors,
    values,
    bar_index,
    pair_offset,
    out_proj,
    norm_gain,
    router,
    expert_route,
    w_gate,
    w_up,
    w_down,
):
    tracks = lax.axis_size("track")
    head_parts = lax.axis_size("head")
    my_track = lax.axis_index("track")
    my_head = lax.axis_index("head")
    events, width = queries.shape[1], queries.shape[2]
    chips = len(order)
    shifts = range(1, head_parts)

    def columns_of(weight, owner):
        return lax.dynamic_slice_in_dim(weight, owner * width, width, 1)

    out_weights = [columns_of(out_proj, my_head)]
    down_weights = [columns_of(w_down[0], my_head)]
    for s in shifts:
        owner = (my_head + s) % head_parts
        out_weights.append(shifted(columns_of(out_proj, owner), "head", head_parts, s))
        down_weights.append(shifted(columns_of(w_down[0], owner), "head", head_parts, s))

    forward = [
        (2 * order[i] + c, 2 * order[(i + 1) % chips] + c) for i in range(chips) for c in range(2)
    ]
    backward = [(b, a) for a, b in forward]
    chunk_width = width // HEAD_CHUNKS
    both_queries = jnp.concatenate([queries, swap_cores(queries, tracks)], axis=0)
    rings = []
    for chunk in range(HEAD_CHUNKS):
        part = slice(chunk * chunk_width, (chunk + 1) * chunk_width)
        block = jnp.concatenate([key_vectors[:, :, part], values[:, :, part]], axis=0)
        got, ahead, back = [block], block, block
        for _ in range(chips // 2 - 1):
            ahead = lax.ppermute(ahead, "track", forward)
            back = lax.ppermute(back, "track", backward)
            got += [ahead, back]
        if chunk % 2 == 0:
            got.append(lax.ppermute(ahead, "track", forward))
        else:
            got.append(lax.ppermute(back, "track", backward))
        rings.append(got)
    hops = [0]
    for s in range(1, chips // 2):
        hops += [-s, s]
    hops.append(chips // 2)

    place = [0] * chips
    for i, chip in enumerate(order):
        place[chip] = i
    my_place = jnp.array(place, jnp.int32)[my_track // 2]
    block_chip = jnp.array(order, jnp.int32)[(my_place + jnp.array(hops, jnp.int32)) % chips]
    block_track = block_chip * 2 + my_track % 2
    key_bars = bar_index[block_track]
    query_track = jnp.stack([my_track, my_track ^ 1])
    query_bars = bar_index[query_track]
    partner = (query_track[:, None, None] + 1 + pair_offset[query_track]) % tracks
    listed = jnp.any(partner[:, :, :, None] == block_track, axis=2)
    listed = listed | (query_track[:, None, None] == block_track)
    listed = jnp.repeat(listed, QB, axis=1)
    query_bars = jnp.where(listed, query_bars[:, :, None], -1000)

    attended = [[] for _ in range(head_parts)]
    for chunk in range(HEAD_CHUNKS):
        part = slice(chunk * chunk_width, (chunk + 1) * chunk_width)
        mine, theirs = attention(both_queries[:, :, part], query_bars, key_bars, rings[chunk])
        merged = merge(mine, swap_cores(theirs, tracks))
        attended[0].append(merged)
        for s in shifts:
            attended[s].append(shifted(merged, "head", head_parts, s))

    experts = tracks
    wide_router = jnp.pad(router, ((0, 0), (0, LANES - experts)))
    gain = norm_gain.reshape(1, width)
    hidden, stat = project(attended, out_weights, residual_in[0], gain, wide_router, experts)
    stats = [stat] + [shifted(stat, "head", head_parts, s) for s in shifts]

    capacity = 2 * events * TOP // experts
    chunks = max(1, min(SLOT_CHUNKS, capacity // 16))
    slots = capacity // chunks
    rows = experts * slots
    route = expert_route[0]
    flat = route.reshape(-1)
    hits = (flat[:, None] == jnp.arange(experts, dtype=jnp.int32)).astype(jnp.int32)
    rank = jnp.sum((jnp.cumsum(hits, axis=0) - hits) * hits, axis=1)
    code = (rank // slots * rows + flat * slots + rank % slots).reshape(events, TOP)
    *outgoing, gates = pack(hidden, stats, gain, route, code.T, chunks, rows, experts)

    returned = []
    for chunk in range(chunks):
        arrived = lax.all_to_all(
            outgoing[chunk].reshape(experts, slots, width), "track", 0, 0, tiled=True
        ).reshape(rows, width)
        arrived = [arrived] + [shifted(arrived, "head", head_parts, s) for s in shifts]
        act = expert_in(arrived, w_gate, w_up, my_head)
        acts = [act] + [shifted(act, "head", head_parts, s) for s in shifts]
        result = expert_out(acts, down_weights)
        back = lax.all_to_all(result.reshape(experts, slots, width), "track", 0, 0, tiled=True)
        returned.append(back.reshape(rows, width))
    return combine(hidden, gates, code, returned)[None]


def solution(mesh):
    chips, columns = mesh.shape["track"] // 2, mesh.shape["head"]
    order = chip_ring(chips // columns, columns)
    in_specs = (
        P("track", None, "head"),
        P("track", None, "head"),
        P("track", None, "head"),
        P("track", None, "head"),
        P(),
        P(),
        P("head", None),
        P("head"),
        P("head", None),
        P("track", None, None),
        P("track", None, "head"),
        P("track", None, "head"),
        P("track", "head", None),
    )
    out_specs = P("track", None, "head")
    return jax.shard_map(
        functools.partial(local, order),
        mesh=mesh,
        in_specs=in_specs,
        out_specs=out_specs,
        check_vma=False,
    )
```

time: 636 us -> 376 us (0.59); the launches traced: 624 us -> 374 us
  local copies, waits for them, and re-layouts: 169 us -> 32.3 us
  matrix products: 102 us -> 0 us
  Pallas kernels: 0 us -> 95.4 us
  waiting for transfers between devices: 190 us -> 125 us
  starting transfers between devices: 5.83 us -> 58.5 us
  blocking collectives: 109 us -> 58.6 us
  other arithmetic: 35.1 us -> 4.04 us
  between operations: 14 us -> 0.38 us
    ppermute x0 -> x30, waiting for transfers between devices: none -> 114 us  [the longest x13 68.2 us: shifted(): return lax.ppermute(x, axis, [(i, (i + shift) % size) for i in range(size)])]
    dot_general x8 -> x0, matrix products: 102 us -> none  [the longest x1 44.4 us: local(): jnp.einsum('iqhd,ikhd->ihqk', slot_query, slot_keys, preferred_element_ty...]
    pallas_call x0 -> x15, Pallas kernels: none -> 95.4 us  [the longest x2 31.7 us: attention(): pl.pallas_call(functools.partial(attention_kernel, blocks, heads), grid=(...]
    reduce_scatter x2 -> x0, waiting for transfers between devices: 84.3 us -> none  [the longest x1 54.1 us: local(): lax.psum_scatter(down_terms.astype(jnp.bfloat16), 'head', scatter_dimensi...]
    all_gather x3 -> x0, waiting for transfers between devices: 70 us -> none  [the longest x1 51.6 us: local(): lax.all_gather(key_vectors, 'track', axis=0, tiled=True)]
    scatter x4 -> x0, local copies, waits for them, and re-layouts: 56.6 us -> none  [the longest x1 22.7 us: local(): pair_value = starting[2].at[slots].set(new_value, mode='drop')]
    broadcast_in_dim x5 -> x0, local copies, waits for them, and re-layouts: 52.1 us -> none  [the longest x1 24.6 us: local(): jnp.repeat(block_piece[0].reshape(amount, events, local_heads, HEAD_DIM),...]
    all_to_all x1 -> x3, blocking collectives: 98.4 us -> 58.6 us  [the longest x2 38.3 us: local(): lax.all_to_all(outgoing[chunk].reshape(experts, slots, width), 'track', 0...]
  transfers between devices with their start and end apart: 6 -> 35, of which waited for: 5 -> 15; matrix products, arithmetic and copies ran while one was open for 19% -> 7% of each run, Pallas kernels for 0% -> 22%
where the time goes in v1:
time: 376 us; the launch traced here: 374 us
  waiting for transfers between devices  125 us (33%)
  Pallas kernels  95.4 us (25%)
  blocking collectives  58.6 us (16%)
  starting transfers between devices  58.5 us (16%)
  local copies, waits for them, and re-layouts  32.3 us (9%)
  other arithmetic  4.04 us (1%)
    ppermute x13, waiting for transfers between devices, shifted(): return lax.ppermute(x, axis, [(i, (i + shift) % size) for i in range(size)])  68.2 us
    all_to_all x2, blocking collectives, local(): lax.all_to_all(outgoing[chunk].reshape(experts, slots, width), 'track', 0...  38.3 us
    pallas_call x2, Pallas kernels, attention(): pl.pallas_call(functools.partial(attention_kernel, blocks, heads), grid=(...  31.7 us
    pallas_call x4, Pallas kernels, expert_in(): pl.pallas_call(functools.partial(expert_in_kernel, sources, per_source),...  26.8 us
    ppermute x6, waiting for transfers between devices, local(): back = lax.ppermute(back, 'track', backward)  25.5 us
    ppermute x6, waiting for transfers between devices, local(): ahead = lax.ppermute(ahead, 'track', forward)  20.4 us
    all_to_all x1, blocking collectives, local(): lax.all_to_all(result.reshape(experts, slots, width), 'track', 0, 0, tile...  20.3 us
    pallas_call x4, Pallas kernels, expert_out(): pl.pallas_call(functools.partial(expert_out_kernel, sources), grid=(width...  18.3 us
  transfers between devices with their start and end apart: 35, of which 15 were waited for; matrix products, arithmetic and copies ran while one was open for 7% of the time, Pallas kernels for 22%

profile of v1, /device:TPU:0, one launch (start us, length us, event | category | flops | bytes accessed | tf_op | source)
XLA Modules:
  0.0 373.9 jit_solution(4233312441086433638)
XLA Ops:
  1.4 3.0 collective-permute-start.1
  4.6 1.9 collective-permute-start.9
  8.8 8.4 %collective-permute-done.1.refs_4_ = bf16[2,256,512]{2,1,0:T(8,128)(2,1)S(1)} collective-permute-done((bf16[2,256,512]{2,1,0:T(8,128)(2,1)S(1)}, bf16[2,256,512]{2,1,0:T(8,128)(2,1)S(1)}, u32[]{:S(2)}, u32[]{:S(2)}) %collective-permute-start.1) | collective-permute-done | bytes 524320 | tf_op jit(solution)/shard_map/ppermute | solution.py:429
  17.3 2.0 collective-permute-start.3
  19.3 9.8 %collective-permute-done.10.refs_5_ = bf16[2,256,512]{2,1,0:T(8,128)(2,1)} collective-permute-done((bf16[2,256,512]{2,1,0:T(8,128)(2,1)S(1)}, bf16[2,256,512]{2,1,0:T(8,128)(2,1)}, u32[]{:S(2)}, u32[]{:S(2)}) %collective-permute-start.10) | collective-permute-done | bytes 524320 | tf_op jit(solution)/shard_map/ppermute | solution.py:430
  30.3 1.7 collective-permute-start.4
  32.0 7.0 %collective-permute-done.3.refs_6_ = bf16[2,256,512]{2,1,0:T(8,128)(2,1)} collective-permute-done((bf16[2,256,512]{2,1,0:T(8,128)(2,1)S(1)}, bf16[2,256,512]{2,1,0:T(8,128)(2,1)}, u32[]{:S(2)}, u32[]{:S(2)}) %collective-permute-start.3) | collective-permute-done | bytes 524320 | tf_op jit(solution)/shard_map/ppermute | solution.py:429
  39.0 1.7 collective-permute-start.5
  40.7 4.0 %constant_dynamic-slice_fusion = (bf16[1024,1024]{1,0:T(8,128)(2,1)S(1)}, bf16[1024,1024]{1,0:T(8,128)(2,1)}) fusion(bf16[1024,2048]{1,0:T(8,128)(2,1)} %param.22, s32[]{:T(128)S(6)} %select_n.124, s32[]{:T(128)S(6)} %select_n.122), kind=kLoop, calls=%fused_computation.56 | loop fusion | bytes 8388616 | tf_op jit(solution)/shard_map/dynamic_slice | solution.py:408
  48.4 7.2 %collective-permute-done.4.refs_7_ = bf16[2,256,512]{2,1,0:T(8,128)(2,1)} collective-permute-done((bf16[2,256,512]{2,1,0:T(8,128)(2,1)}, bf16[2,256,512]{2,1,0:T(8,128)(2,1)}, u32[]{:S(2)}, u32[]{:S(2)}) %collective-permute-start.4) | collective-permute-done | bytes 524320 | tf_op jit(solution)/shard_map/ppermute | solution.py:430
  56.0 1.6 collective-permute-start.7
  60.3 5.0 %collective-permute-done.11.refs_6_ = bf16[2,256,512]{2,1,0:T(8,128)(2,1)S(1)} collective-permute-done((bf16[2,256,512]{2,1,0:T(8,128)(2,1)}, bf16[2,256,512]{2,1,0:T(8,128)(2,1)S(1)}, u32[]{:S(2)}, u32[]{:S(2)}) %collective-permute-start.11) | collective-permute-done | bytes 524320 | tf_op jit(solution)/shard_map/ppermute | solution.py:429
  65.3 1.7 collective-permute-start.13
  69.5 8.5 %collective-permute-done.6.refs_9_ = bf16[2,256,512]{2,1,0:T(8,128)(2,1)} collective-permute-done((bf16[2,256,512]{2,1,0:T(8,128)(2,1)}, bf16[2,256,512]{2,1,0:T(8,128)(2,1)}, u32[]{:S(2)}, u32[]{:S(2)}) %collective-permute-start.6) | collective-permute-done | bytes 524320 | tf_op jit(solution)/shard_map/ppermute | solution.py:430
  78.0 15.8 %attention.2 = (f32[256,640]{1,0:T(8,128)}, f32[256,640]{1,0:T(8,128)}) custom-call(bf16[2,256,512]{2,1,0:T(8,128)(2,1)} %get-tuple-element.36.refs_0_, s32[2,256,8]{2,1,0:T(8,128)} %bitcast_select_fusion.refs_1_, s32[8,256]{1,0:T(8,128)} %gather_fusion.3, bf16[2,256,512]{2,1,0:T(8,128)(2,1)} %copy-done.12, bf16[2,256,512]{2,1,0:T(8,128)(2,1)} %copy-done.28, ...), custom_call_target="tpu_custom_call" | custom-call | flops 2147483648 | bytes 4194304 | tf_op jit(solution)/shard_map/attention/pallas_call | solution.py:112
  94.0 15.9 %attention.3 = (f32[256,640]{1,0:T(8,128)}, f32[256,640]{1,0:T(8,128)}) custom-call(bf16[2,256,512]{2,1,0:T(8,128)(2,1)} %get-tuple-element.35.refs_0_, s32[2,256,8]{2,1,0:T(8,128)} %bitcast_select_fusion.refs_1_, s32[8,256]{1,0:T(8,128)} %gather_fusion.3, bf16[2,256,512]{2,1,0:T(8,128)(2,1)} %copy-done.11, ...), custom_call_target="tpu_custom_call" | custom-call | flops 2147483648 | bytes 4194304 | tf_op jit(solution)/shard_map/attention/pallas_call | solution.py:112
  111.5 2.9 merge.2.refs_0_
  116.0 2.9 merge.3.refs_1_
  123.8 4.7 %collective-permute-done.18.refs_3_ = bf16[256,512]{1,0:T(8,128)(2,1)S(1)} collective-permute-done((bf16[256,512]{1,0:T(8,128)(2,1)}, bf16[256,512]{1,0:T(8,128)(2,1)S(1)}, u32[]{:S(2)}, u32[]{:S(2)}) %collective-permute-start.18) | collective-permute-done | bytes 262176 | tf_op jit(solution)/shard_map/ppermute | solution.py:46
  129.2 5.8 %project.1 = (bf16[256,1024]{1,0:T(8,128)(2,1)}, f32[256,128]{1,0:T(8,128)}) custom-call(bf16[256,512]{1,0:T(8,128)(2,1)} %merge.2.refs_0_, bf16[256,512]{1,0:T(8,128)(2,1)} %merge.3.refs_1_, bf16[256,512]{1,0:T(8,128)(2,1)} %copy-done.23, bf16[256,512]{1,0:T(8,128)(2,1)} %copy-done.24, bf16[1024,1024]{1,0:T(8,128)(2,1)} %get-tuple-element.32.refs_4_, ...), custom_call_target="tpu_custom_call" | custom-call | flops 1073741824 | bytes 4194304 | tf_op jit(solution)/shard_map/project/pallas_call | solution.py:190
  137.4 2.9 collective-permute-done.20.refs_2_
  140.9 3.1 pack.1
  144.0 19.6 %all_to_all.40 = bf16[16,16,1024]{2,1,0:T(8,128)(2,1)} all-to-all(bf16[16,16,1024]{2,1,0:T(8,128)(2,1)} %bitcast.76), channel_id=1, replica_groups=mesh['track'=16,'head'=2] {'track'}, dimensions={0} | all-to-all | bytes 1048576 | tf_op jit(solution)/shard_map/all_to_all | solution.py:485
  163.6 18.7 %all_to_all.41 = bf16[16,16,1024]{2,1,0:T(8,128)(2,1)} all-to-all(bf16[16,16,1024]{2,1,0:T(8,128)(2,1)} %bitcast.75), channel_id=1, replica_groups=mesh['track'=16,'head'=2] {'track'}, dimensions={0} | all-to-all | bytes 1048576 | tf_op jit(solution)/shard_map/all_to_all | solution.py:485
  182.3 4.1 %all-to-all-start.4 = ((bf16[16,16,1024]{2,1,0:T(8,128)(2,1)}), bf16[16,16,1024]{2,1,0:T(8,128)(2,1)S(1)}, u32[]{:S(2)}, u32[]{:S(2)}) async-start(bf16[16,16,1024]{2,1,0:T(8,128)(2,1)} %bitcast.74), calls=%async_computation.4 | async-start | bytes 1048576 | tf_op jit(solution)/shard_map/all_to_all | solution.py:485
  186.4 1.9 dynamic-slice_bitcast_fusion
  190.3 10.5 %all-to-all-done.4 = bf16[16,16,1024]{2,1,0:T(8,128)(2,1)S(1)} async-done(((bf16[16,16,1024]{2,1,0:T(8,128)(2,1)}), bf16[16,16,1024]{2,1,0:T(8,128)(2,1)S(1)}, u32[]{:S(2)}, u32[]{:S(2)}) %all-to-all-start.4) | async-done | bytes 524320 | tf_op jit(solution)/shard_map/all_to_all | solution.py:485
  200.8 4.1 %all-to-all-start.6 = ((bf16[16,16,1024]{2,1,0:T(8,128)(2,1)}), bf16[16,16,1024]{2,1,0:T(8,128)(2,1)S(1)}, u32[]{:S(2)}, u32[]{:S(2)}) async-start(bf16[16,16,1024]{2,1,0:T(8,128)(2,1)} %bitcast.71), calls=%async_computation.6 | async-start | bytes 1048576 | tf_op jit(solution)/shard_map/all_to_all | solution.py:485
  204.9 4.6 %copy.51.refs_2_ = bf16[1,2048,704]{2,1,0:T(8,128)(2,1)} copy(bf16[1,2048,704]{1,2,0:T(8,128)(2,1)} %param.26) | data formatting | bytes 5767168 | tf_op args[10]
  209.5 4.7 %copy.52.refs_3_ = bf16[1,2048,704]{2,1,0:T(8,128)(2,1)} copy(bf16[1,2048,704]{1,2,0:T(8,128)(2,1)} %param.27) | data formatting | bytes 5767168 | tf_op args[11]
  214.8 19.0 %collective-permute-done.21.refs_1_ = bf16[256,1024]{1,0:T(8,128)(2,1)} collective-permute-done((bf16[256,1024]{1,0:T(8,128)(2,1)}, bf16[256,1024]{1,0:T(8,128)(2,1)}, u32[]{:S(2)}, u32[]{:S(2)}) %collective-permute-start.21) | collective-permute-done | bytes 524320 | tf_op jit(solution)/shard_map/ppermute | solution.py:46
  233.8 6.7 %expert_in.4.refs_0_ = bf16[256,704]{1,0:T(8,128)(2,1)} custom-call(s32[4]{0:T(128)} %fusion.12.kmap_ref, bf16[256,1024]{1,0:T(8,128)(2,1)} %bitcast.14.refs_0_, bf16[256,1024]{1,0:T(8,128)(2,1)} %collective-permute-done.21.refs_1_, bf16[1,2048,704]{2,1,0:T(8,128)(2,1)} %copy.51.refs_2_, bf16[1,2048,704]{2,1,0:T(8,128)(2,1)} %copy.52.refs_3_), custom_call_target="tpu_custom_call" | custom-call | flops 1476395008 | bytes 5767168 | tf_op jit(solution)/shard_map/expert_in/pallas_call | solution.py:301
  242.5 10.2 %collective-permute-done.22.refs_1_ = bf16[256,704]{1,0:T(8,128)(2,1)S(1)} collective-permute-done((bf16[256,704]{1,0:T(8,128)(2,1)}, bf16[256,704]{1,0:T(8,128)(2,1)S(1)}, u32[]{:S(2)}, u32[]{:S(2)}) %collective-permute-start.22) | collective-permute-done | bytes 360480 | tf_op jit(solution)/shard_map/ppermute | solution.py:46
  253.4 4.5 %expert_out.4 = bf16[256,1024]{1,0:T(8,128)(2,1)} custom-call(bf16[256,704]{1,0:T(8,128)(2,1)} %expert_in.4.refs_0_, bf16[256,704]{1,0:T(8,128)(2,1)} %copy-done.19, bf16[704,1024]{1,0:T(8,128)(2,1)} %get-tuple-element.34.refs_2_, bf16[704,1024]{1,0:T(8,128)(2,1)} %copy-done.2), custom_call_target="tpu_custom_call" | custom-call | flops 738197504 | bytes 2883584 | tf_op jit(solution)/shard_map/expert_out/pallas_call | solution.py:332
  258.0 5.8 %all-to-all-start.1 = ((bf16[16,16,1024]{2,1,0:T(8,128)(2,1)}), bf16[16,16,1024]{2,1,0:T(8,128)(2,1)S(1)}, u32[]{:S(2)}, u32[]{:S(2)}) async-start(bf16[16,16,1024]{2,1,0:T(8,128)(2,1)} %bitcast.59), calls=%async_computation.1 | async-start | bytes 1048576 | tf_op jit(solution)/shard_map/all_to_all | solution.py:492
  263.8 6.7 %expert_in.5.refs_0_ = bf16[256,704]{1,0:T(8,128)(2,1)} custom-call(s32[4]{0:T(128)} %fusion.12.kmap_ref, bf16[256,1024]{1,0:T(8,128)(2,1)} %bitcast.66, bf16[256,1024]{1,0:T(8,128)(2,1)} %collective-permute-done.24.refs_1_, bf16[1,2048,704]{2,1,0:T(8,128)(2,1)} %copy.51.refs_2_, bf16[1,2048,704]{2,1,0:T(8,128)(2,1)} %copy.52.refs_3_), custom_call_target="tpu_custom_call" | custom-call | flops 1476395008 | bytes 5767168 | tf_op jit(solution)/shard_map/expert_in/pallas_call | solution.py:301
  272.5 10.1 %collective-permute-done.25.refs_1_ = bf16[256,704]{1,0:T(8,128)(2,1)S(1)} collective-permute-done((bf16[256,704]{1,0:T(8,128)(2,1)}, bf16[256,704]{1,0:T(8,128)(2,1)S(1)}, u32[]{:S(2)}, u32[]{:S(2)}) %collective-permute-start.25) | collective-permute-done | bytes 360480 | tf_op jit(solution)/shard_map/ppermute | solution.py:46
  283.4 4.6 %expert_out.5 = bf16[256,1024]{1,0:T(8,128)(2,1)} custom-call(bf16[256,704]{1,0:T(8,128)(2,1)} %expert_in.5.refs_0_, bf16[256,704]{1,0:T(8,128)(2,1)} %copy-done.20, bf16[704,1024]{1,0:T(8,128)(2,1)} %get-tuple-element.34.refs_2_, bf16[704,1024]{1,0:T(8,128)(2,1)} %copy-done.2), custom_call_target="tpu_custom_call" | custom-call | flops 738197504 | bytes 2883584 | tf_op jit(solution)/shard_map/expert_out/pallas_call | solution.py:332
  288.0 6.1 %all-to-all-start.3 = ((bf16[16,16,1024]{2,1,0:T(8,128)(2,1)}), bf16[16,16,1024]{2,1,0:T(8,128)(2,1)S(1)}, u32[]{:S(2)}, u32[]{:S(2)}) async-start(bf16[16,16,1024]{2,1,0:T(8,128)(2,1)} %bitcast.60), calls=%async_computation.3 | async-start | bytes 1048576 | tf_op jit(solution)/shard_map/all_to_all | solution.py:492
  294.9 6.7 %expert_in.6.refs_0_ = bf16[256,704]{1,0:T(8,128)(2,1)} custom-call(s32[4]{0:T(128)} %fusion.12.kmap_ref, bf16[256,1024]{1,0:T(8,128)(2,1)} %bitcast.65, bf16[256,1024]{1,0:T(8,128)(2,1)} %copy-done.17, bf16[1,2048,704]{2,1,0:T(8,128)(2,1)} %copy.51.refs_2_, bf16[1,2048,704]{2,1,0:T(8,128)(2,1)} %copy.52.refs_3_), custom_call_target="tpu_custom_call" | custom-call | flops 1476395008 | bytes 5767168 | tf_op jit(solution)/shard_map/expert_in/pallas_call | solution.py:301
  303.6 10.1 %collective-permute-done.27.refs_1_ = bf16[256,704]{1,0:T(8,128)(2,1)S(1)} collective-permute-done((bf16[256,704]{1,0:T(8,128)(2,1)}, bf16[256,704]{1,0:T(8,128)(2,1)S(1)}, u32[]{:S(2)}, u32[]{:S(2)}) %collective-permute-start.27) | collective-permute-done | bytes 360480 | tf_op jit(solution)/shard_map/ppermute | solution.py:46
  314.5 4.5 %expert_out.6 = bf16[256,1024]{1,0:T(8,128)(2,1)} custom-call(bf16[256,704]{1,0:T(8,128)(2,1)} %expert_in.6.refs_0_, bf16[256,704]{1,0:T(8,128)(2,1)} %copy-done.21, bf16[704,1024]{1,0:T(8,128)(2,1)} %get-tuple-element.34.refs_2_, bf16[704,1024]{1,0:T(8,128)(2,1)} %copy-done.2), custom_call_target="tpu_custom_call" | custom-call | flops 738197504 | bytes 2883584 | tf_op jit(solution)/shard_map/expert_out/pallas_call | solution.py:332
  319.0 6.1 %all-to-all-start.5 = ((bf16[16,16,1024]{2,1,0:T(8,128)(2,1)}), bf16[16,16,1024]{2,1,0:T(8,128)(2,1)S(1)}, u32[]{:S(2)}, u32[]{:S(2)}) async-start(bf16[16,16,1024]{2,1,0:T(8,128)(2,1)} %bitcast.58), calls=%async_computation.5 | async-start | bytes 1048576 | tf_op jit(solution)/shard_map/all_to_all | solution.py:492
  325.9 6.7 %expert_in.7.refs_0_ = bf16[256,704]{1,0:T(8,128)(2,1)} custom-call(s32[4]{0:T(128)} %fusion.12.kmap_ref, bf16[256,1024]{1,0:T(8,128)(2,1)} %bitcast.63, bf16[256,1024]{1,0:T(8,128)(2,1)} %copy-done.16, bf16[1,2048,704]{2,1,0:T(8,128)(2,1)} %copy.51.refs_2_, bf16[1,2048,704]{2,1,0:T(8,128)(2,1)} %copy.52.refs_3_), custom_call_target="tpu_custom_call" | custom-call | flops 1476395008 | bytes 5767168 | tf_op jit(solution)/shard_map/expert_in/pallas_call | solution.py:301
  334.2 10.1 %collective-permute-done.29.refs_1_ = bf16[256,704]{1,0:T(8,128)(2,1)S(1)} collective-permute-done((bf16[256,704]{1,0:T(8,128)(2,1)}, bf16[256,704]{1,0:T(8,128)(2,1)S(1)}, u32[]{:S(2)}, u32[]{:S(2)}) %collective-permute-start.29) | collective-permute-done | bytes 360480 | tf_op jit(solution)/shard_map/ppermute | solution.py:46
  345.0 4.6 %expert_out.7 = bf16[256,1024]{1,0:T(8,128)(2,1)} custom-call(bf16[256,704]{1,0:T(8,128)(2,1)} %expert_in.7.refs_0_, bf16[256,704]{1,0:T(8,128)(2,1)} %copy-done.22, bf16[704,1024]{1,0:T(8,128)(2,1)} %get-tuple-element.34.refs_2_, bf16[704,1024]{1,0:T(8,128)(2,1)} %copy-done.2), custom_call_target="tpu_custom_call" | custom-call | flops 738197504 | bytes 2883584 | tf_op jit(solution)/shard_map/expert_out/pallas_call | solution.py:332
  349.6 20.3 %all_to_all.42 = bf16[16,16,1024]{2,1,0:T(8,128)(2,1)} all-to-all(bf16[16,16,1024]{2,1,0:T(8,128)(2,1)} %bitcast.61), channel_id=1, replica_groups=mesh['track'=16,'head'=2] {'track'}, dimensions={0} | all-to-all | bytes 1048576 | tf_op jit(solution)/shard_map/all_to_all | solution.py:492
  369.9 3.9 %combine.1 = bf16[256,1024]{1,0:T(8,128)(2,1)} custom-call(bf16[256,1024]{1,0:T(8,128)(2,1)} %get-tuple-element.20.refs_0_, f32[256,128]{1,0:T(8,128)} %get-tuple-element.22.refs_1_, s32[256,2]{1,0:T(8,128)} %copy-done.9, bf16[256,1024]{1,0:T(8,128)(2,1)} %bitcast.70, bf16[256,1024]{1,0:T(8,128)(2,1)} %bitcast.72, bf16[256,1024]{1,0:T(8,128)(2,1)} %bitcast.73, ...), custom_call_target="tpu_custom_call" | custom-call | flops 1073741824 | bytes 2097152 | tf_op jit(solution)/shard_map/combine/pallas_call | solution.py:371
  (149 shorter events, 41.2 us)
Async XLA Ops:
  0.0 29.6 %copy-start = (s32[16,16,4]{1,2,0:T(4,128)S(1)}, s32[16,16,4]{1,2,0:T(4,128)}, u32[]{:S(2)}) copy-start(s32[16,16,4]{1,2,0:T(4,128)} %param.21) | copy-start | bytes 12292
  1.4 37.6 %copy-start.12 = (bf16[2,256,512]{2,1,0:T(8,128)(2,1)}, bf16[2,256,512]{2,1,0:T(8,128)(2,1)S(1)}, u32[]{:S(2)}) copy-start(bf16[2,256,512]{2,1,0:T(8,128)(2,1)S(1)} %pad_maximum_fusion.refs_3_) | copy-start | bytes 1572868
  1.4 15.8 %collective-permute-start.1 = (bf16[2,256,512]{2,1,0:T(8,128)(2,1)S(1)}, bf16[2,256,512]{2,1,0:T(8,128)(2,1)S(1)}, u32[]{:S(2)}, u32[]{:S(2)}) collective-permute-start(bf16[2,256,512]{2,1,0:T(8,128)(2,1)S(1)} %pad_maximum_fusion.refs_3_), channel_id=1, source_target_pairs={{4,12},{6,14},{12,20},{14,22},{20,28},{22,30},{28,24},{30,26},{24,... | collective-permute-start | bytes 1572872 | tf_op jit(solution)/shard_map/ppermute | solution.py:429
  4.4 25.9 %collective-permute-start.2 = (bf16[2,256,512]{2,1,0:T(8,128)(2,1)S(1)}, bf16[2,256,512]{2,1,0:T(8,128)(2,1)}, u32[]{:S(2)}, u32[]{:S(2)}) collective-permute-start(bf16[2,256,512]{2,1,0:T(8,128)(2,1)S(1)} %pad_maximum_fusion.refs_3_), channel_id=1, source_target_pairs={{12,4},{14,6},{20,12},{22,14},{28,20},{30,22},{24,28},{26,30},{16,... | collective-permute-start | bytes 1572872 | tf_op jit(solution)/shard_map/ppermute | solution.py:430
  4.6 40.0 %copy-start.11 = (bf16[2,256,512]{2,1,0:T(8,128)(2,1)}, bf16[2,256,512]{2,1,0:T(8,128)(2,1)S(1)}, u32[]{:S(2)}) copy-start(bf16[2,256,512]{2,1,0:T(8,128)(2,1)S(1)} %pad_maximum_fusion.1.refs_3_) | copy-start | bytes 1572868
  4.6 40.0 %collective-permute-start.9 = (bf16[2,256,512]{2,1,0:T(8,128)(2,1)S(1)}, bf16[2,256,512]{2,1,0:T(8,128)(2,1)}, u32[]{:S(2)}, u32[]{:S(2)}) collective-permute-start(bf16[2,256,512]{2,1,0:T(8,128)(2,1)S(1)} %pad_maximum_fusion.1.refs_3_), channel_id=1, source_target_pairs={{4,12},{6,14},{12,20},{14,22},{20,28},{22,30},{28,24},{30,26},{24,... | collective-permute-start | bytes 1572872 | tf_op jit(solution)/shard_map/ppermute | solution.py:429
  6.6 22.6 %collective-permute-start.10 = (bf16[2,256,512]{2,1,0:T(8,128)(2,1)S(1)}, bf16[2,256,512]{2,1,0:T(8,128)(2,1)}, u32[]{:S(2)}, u32[]{:S(2)}) collective-permute-start(bf16[2,256,512]{2,1,0:T(8,128)(2,1)S(1)} %pad_maximum_fusion.1.refs_3_), channel_id=1, source_target_pairs={{12,4},{14,6},{20,12},{22,14},{28,20},{30,22},{24,28},{26,30},{16,... | collective-permute-start | bytes 1572872 | tf_op jit(solution)/shard_map/ppermute | solution.py:430
  6.7 40.1 %collective-permute-start = (bf16[1,256,1024]{2,1,0:T(8,128)(2,1)S(1)}, bf16[1,256,1024]{2,1,0:T(8,128)(2,1)}, u32[]{:S(2)}, u32[]{:S(2)}) collective-permute-start(bf16[1,256,1024]{2,1,0:T(8,128)(2,1)S(1)} %copy-done.10), channel_id=1, source_target_pairs={{0,2},{2,0},{4,6},{6,4},{8,10},{10,8},{12,14},{14,12},{16,18},{18,... | collective-permute-start | bytes 1572872 | tf_op jit(solution)/shard_map/ppermute | solution.py:50
  17.3 21.8 %copy-start.28 = (bf16[2,256,512]{2,1,0:T(8,128)(2,1)}, bf16[2,256,512]{2,1,0:T(8,128)(2,1)S(1)}, u32[]{:S(2)}) copy-start(bf16[2,256,512]{2,1,0:T(8,128)(2,1)S(1)} %collective-permute-done.1.refs_4_) | copy-start | bytes 1572868
  17.3 21.7 %collective-permute-start.3 = (bf16[2,256,512]{2,1,0:T(8,128)(2,1)S(1)}, bf16[2,256,512]{2,1,0:T(8,128)(2,1)}, u32[]{:S(2)}, u32[]{:S(2)}) collective-permute-start(bf16[2,256,512]{2,1,0:T(8,128)(2,1)S(1)} %collective-permute-done.1.refs_4_), channel_id=1, source_target_pairs={{4,12},{6,14},{12,20},{14,22},{20,28},{22,30},{28,24},{30,26},{24,... | collective-permute-start | bytes 1572872 | tf_op jit(solution)/shard_map/ppermute | solution.py:429
  29.1 17.1 %collective-permute-start.12 = (bf16[2,256,512]{2,1,0:T(8,128)(2,1)}, bf16[2,256,512]{2,1,0:T(8,128)(2,1)}, u32[]{:S(2)}, u32[]{:S(2)}) collective-permute-start(bf16[2,256,512]{2,1,0:T(8,128)(2,1)} %collective-permute-done.10.refs_5_), channel_id=1, source_target_pairs={{12,4},{14,6},{20,12},{22,14},{28,20},{30,22},{24,28},{26,30},{16,... | collective-permute-start | bytes 1572872 | tf_op jit(solution)/shard_map/ppermute | solution.py:430
  30.3 27.3 %copy-start.18 = (s32[16,256]{1,0:T(8,128)S(1)}, s32[16,256]{1,0:T(8,128)}, u32[]{:S(2)}) copy-start(s32[16,256]{1,0:T(8,128)} %param.20) | copy-start | bytes 49156
  30.3 25.2 %collective-permute-start.4 = (bf16[2,256,512]{2,1,0:T(8,128)(2,1)}, bf16[2,256,512]{2,1,0:T(8,128)(2,1)}, u32[]{:S(2)}, u32[]{:S(2)}) collective-permute-start(bf16[2,256,512]{2,1,0:T(8,128)(2,1)} %collective-permute-done.2.refs_5_), channel_id=1, source_target_pairs={{12,4},{14,6},{20,12},{22,14},{28,20},{30,22},{24,28},{26,30},{16,... | collective-permute-start | bytes 1572872 | tf_op jit(solution)/shard_map/ppermute | solution.py:430
  39.0 17.0 %collective-permute-start.5 = (bf16[2,256,512]{2,1,0:T(8,128)(2,1)}, bf16[2,256,512]{2,1,0:T(8,128)(2,1)}, u32[]{:S(2)}, u32[]{:S(2)}) collective-permute-start(bf16[2,256,512]{2,1,0:T(8,128)(2,1)} %collective-permute-done.3.refs_6_), channel_id=1, source_target_pairs={{4,12},{6,14},{12,20},{14,22},{20,28},{22,30},{28,24},{30,26},{24,... | collective-permute-start | bytes 1572872 | tf_op jit(solution)/shard_map/ppermute | solution.py:429
  44.6 20.7 %collective-permute-start.11 = (bf16[2,256,512]{2,1,0:T(8,128)(2,1)}, bf16[2,256,512]{2,1,0:T(8,128)(2,1)S(1)}, u32[]{:S(2)}, u32[]{:S(2)}) collective-permute-start(bf16[2,256,512]{2,1,0:T(8,128)(2,1)} %collective-permute-done.9.refs_4_), channel_id=1, source_target_pairs={{4,12},{6,14},{12,20},{14,22},{20,28},{22,30},{28,24},{30,26},{24,... | collective-permute-start | bytes 1572872 | tf_op jit(solution)/shard_map/ppermute | solution.py:429
  46.2 20.7 %collective-permute-start.14 = (bf16[2,256,512]{2,1,0:T(8,128)(2,1)}, bf16[2,256,512]{2,1,0:T(8,128)(2,1)}, u32[]{:S(2)}, u32[]{:S(2)}) collective-permute-start(bf16[2,256,512]{2,1,0:T(8,128)(2,1)} %collective-permute-done.12.refs_7_), channel_id=1, source_target_pairs={{12,4},{14,6},{20,12},{22,14},{28,20},{30,22},{24,28},{26,30},{16,... | collective-permute-start | bytes 1572872 | tf_op jit(solution)/shard_map/ppermute | solution.py:430
  46.8 75.9 %collective-permute-start.19 = (bf16[1024,1024]{1,0:T(8,128)(2,1)S(1)}, bf16[1024,1024]{1,0:T(8,128)(2,1)}, u32[]{:S(2)}, u32[]{:S(2)}) collective-permute-start(bf16[1024,1024]{1,0:T(8,128)(2,1)S(1)} %get-tuple-element.31), channel_id=1, source_target_pairs={{0,1},{1,0},{2,3},{3,2},{4,5},{5,4},{6,7},{7,6},{8,9},{9,8},{10,11... | collective-permute-start | bytes 6291464 | tf_op jit(solution)/shard_map/ppermute | solution.py:46
  55.6 22.5 %collective-permute-start.6 = (bf16[2,256,512]{2,1,0:T(8,128)(2,1)}, bf16[2,256,512]{2,1,0:T(8,128)(2,1)}, u32[]{:S(2)}, u32[]{:S(2)}) collective-permute-start(bf16[2,256,512]{2,1,0:T(8,128)(2,1)} %collective-permute-done.4.refs_7_), channel_id=1, source_target_pairs={{12,4},{14,6},{20,12},{22,14},{28,20},{30,22},{24,28},{26,30},{16,... | collective-permute-start | bytes 1572872 | tf_op jit(solution)/shard_map/ppermute | solution.py:430
  56.0 22.0 %collective-permute-start.7 = (bf16[2,256,512]{2,1,0:T(8,128)(2,1)}, bf16[2,256,512]{2,1,0:T(8,128)(2,1)}, u32[]{:S(2)}, u32[]{:S(2)}) collective-permute-start(bf16[2,256,512]{2,1,0:T(8,128)(2,1)} %collective-permute-done.5.refs_8_), channel_id=1, source_target_pairs={{4,12},{6,14},{12,20},{14,22},{20,28},{22,30},{28,24},{30,26},{24,... | collective-permute-start | bytes 1572872 | tf_op jit(solution)/shard_map/ppermute | solution.py:433
  65.3 28.5 %copy-start.29 = (bf16[2,256,512]{2,1,0:T(8,128)(2,1)}, bf16[2,256,512]{2,1,0:T(8,128)(2,1)S(1)}, u32[]{:S(2)}) copy-start(bf16[2,256,512]{2,1,0:T(8,128)(2,1)S(1)} %collective-permute-done.11.refs_6_) | copy-start | bytes 1572868
  65.3 28.6 %collective-permute-start.13 = (bf16[2,256,512]{2,1,0:T(8,128)(2,1)S(1)}, bf16[2,256,512]{2,1,0:T(8,128)(2,1)}, u32[]{:S(2)}, u32[]{:S(2)}) collective-permute-start(bf16[2,256,512]{2,1,0:T(8,128)(2,1)S(1)} %collective-permute-done.11.refs_6_), channel_id=1, source_target_pairs={{4,12},{6,14},{12,20},{14,22},{20,28},{22,30},{28,24},{30,26},{24,... | collective-permute-start | bytes 1572872 | tf_op jit(solution)/shard_map/ppermute | solution.py:429
  67.0 27.0 %collective-permute-start.15 = (bf16[2,256,512]{2,1,0:T(8,128)(2,1)}, bf16[2,256,512]{2,1,0:T(8,128)(2,1)}, u32[]{:S(2)}, u32[]{:S(2)}) collective-permute-start(bf16[2,256,512]{2,1,0:T(8,128)(2,1)} %collective-permute-done.14.refs_9_), channel_id=1, source_target_pairs={{12,4},{14,6},{20,12},{22,14},{28,20},{30,22},{24,28},{26,30},{16,... | collective-permute-start | bytes 1572872 | tf_op jit(solution)/shard_map/ppermute | solution.py:435
  93.9 16.8 %collective-permute-start.8 = (f32[256,640]{1,0:T(8,128)}, f32[256,640]{1,0:T(8,128)S(1)}, u32[]{:S(2)}, u32[]{:S(2)}) collective-permute-start(f32[256,640]{1,0:T(8,128)} %get-tuple-element.17), channel_id=1, source_target_pairs={{0,2},{2,0},{4,6},{6,4},{8,10},{10,8},{12,14},{14,12},{16,18},{18,... | collective-permute-start | bytes 1966088 | tf_op jit(solution)/shard_map/ppermute | solution.py:50
  94.0 16.4 %copy-start.26 = (s32[1,256,2]{1,2,0:T(2,128)S(1)}, s32[1,256,2]{1,2,0:T(2,128)}, u32[]{:S(2)}) copy-start(s32[1,256,2]{1,2,0:T(2,128)} %param.25) | copy-start | bytes 6148
  109.8 6.1 %collective-permute-start.16 = (f32[256,640]{1,0:T(8,128)}, f32[256,640]{1,0:T(8,128)}, u32[]{:S(2)}, u32[]{:S(2)}) collective-permute-start(f32[256,640]{1,0:T(8,128)} %get-tuple-element.19), channel_id=1, source_target_pairs={{0,2},{2,0},{4,6},{6,4},{8,10},{10,8},{12,14},{14,12},{16,18},{18,... | collective-permute-start | bytes 1966088 | tf_op jit(solution)/shard_map/ppermute | solution.py:50
  110.5 26.0 %copy-start.4 = (s32[1,256,2]{2,1,0:T(8,128)}, s32[1,256,2]{2,1,0:T(8,128)S(1)}, u32[]{:S(2)}) copy-start(s32[1,256,2]{2,1,0:T(8,128)S(1)} %copy.46) | copy-start | bytes 6148
  114.4 9.4 %collective-permute-start.17 = (bf16[256,512]{1,0:T(8,128)(2,1)}, bf16[256,512]{1,0:T(8,128)(2,1)S(1)}, u32[]{:S(2)}, u32[]{:S(2)}) collective-permute-start(bf16[256,512]{1,0:T(8,128)(2,1)} %merge.2.refs_0_), channel_id=1, source_target_pairs={{0,1},{1,0},{2,3},{3,2},{4,5},{5,4},{6,7},{7,6},{8,9},{9,8},{10,11... | collective-permute-start | bytes 786440 | tf_op jit(solution)/shard_map/ppermute | solution.py:46
  118.8 9.7 %collective-permute-start.18 = (bf16[256,512]{1,0:T(8,128)(2,1)}, bf16[256,512]{1,0:T(8,128)(2,1)S(1)}, u32[]{:S(2)}, u32[]{:S(2)}) collective-permute-start(bf16[256,512]{1,0:T(8,128)(2,1)} %merge.3.refs_1_), channel_id=1, source_target_pairs={{0,1},{1,0},{2,3},{3,2},{4,5},{5,4},{6,7},{7,6},{8,9},{9,8},{10,11... | collective-permute-start | bytes 786440 | tf_op jit(solution)/shard_map/ppermute | solution.py:46
  135.0 5.2 %collective-permute-start.20 = (f32[256,128]{1,0:T(8,128)}, f32[256,128]{1,0:T(8,128)S(1)}, u32[]{:S(2)}, u32[]{:S(2)}) collective-permute-start(f32[256,128]{1,0:T(8,128)} %get-tuple-element.21.refs_1_), channel_id=1, source_target_pairs={{0,1},{1,0},{2,3},{3,2},{4,5},{5,4},{6,7},{7,6},{8,9},{9,8},{10,11... | collective-permute-start | bytes 393224 | tf_op jit(solution)/shard_map/ppermute | solution.py:46
  140.9 45.5 %copy-start.3 = (bf16[1,704,2048]{2,1,0:T(8,128)(2,1)S(1)}, bf16[1,704,2048]{2,1,0:T(8,128)(2,1)}, u32[]{:S(2)}) copy-start(bf16[1,704,2048]{2,1,0:T(8,128)(2,1)} %param.28) | copy-start | bytes 8650756
  182.3 18.5 %all-to-all-start.4 = ((bf16[16,16,1024]{2,1,0:T(8,128)(2,1)}), bf16[16,16,1024]{2,1,0:T(8,128)(2,1)S(1)}, u32[]{:S(2)}, u32[]{:S(2)}) async-start(bf16[16,16,1024]{2,1,0:T(8,128)(2,1)} %bitcast.74), calls=%async_computation.4 | async-start | bytes 1048576 | tf_op jit(solution)/shard_map/all_to_all | solution.py:485
  188.3 54.2 %collective-permute-start.23 = (bf16[704,1024]{1,0:T(8,128)(2,1)}, bf16[704,1024]{1,0:T(8,128)(2,1)S(1)}, u32[]{:S(2)}, u32[]{:S(2)}) collective-permute-start(bf16[704,1024]{1,0:T(8,128)(2,1)} %get-tuple-element.33), channel_id=1, source_target_pairs={{0,1},{1,0},{2,3},{3,2},{4,5},{5,4},{6,7},{7,6},{8,9},{9,8},{10,11... | collective-permute-start | bytes 4325384 | tf_op jit(solution)/shard_map/ppermute | solution.py:46
  189.8 44.0 %collective-permute-start.21 = (bf16[256,1024]{1,0:T(8,128)(2,1)}, bf16[256,1024]{1,0:T(8,128)(2,1)}, u32[]{:S(2)}, u32[]{:S(2)}) collective-permute-start(bf16[256,1024]{1,0:T(8,128)(2,1)} %bitcast.14.refs_0_), channel_id=1, source_target_pairs={{0,1},{1,0},{2,3},{3,2},{4,5},{5,4},{6,7},{7,6},{8,9},{9,8},{10,11... | collective-permute-start | bytes 1572872 | tf_op jit(solution)/shard_map/ppermute | solution.py:46
  200.8 71.2 %copy-start.6 = (bf16[16,16,1024]{2,1,0:T(8,128)(2,1)}, bf16[16,16,1024]{2,1,0:T(8,128)(2,1)S(1)}, u32[]{:S(2)}) copy-start(bf16[16,16,1024]{2,1,0:T(8,128)(2,1)S(1)} %all-to-all-done.4) | copy-start | bytes 1572868
  200.8 57.2 %all-to-all-start.6 = ((bf16[16,16,1024]{2,1,0:T(8,128)(2,1)}), bf16[16,16,1024]{2,1,0:T(8,128)(2,1)S(1)}, u32[]{:S(2)}, u32[]{:S(2)}) async-start(bf16[16,16,1024]{2,1,0:T(8,128)(2,1)} %bitcast.71), calls=%async_computation.6 | async-start | bytes 1048576 | tf_op jit(solution)/shard_map/all_to_all | solution.py:485
  214.8 27.2 %copy-start.7 = (bf16[16,16,1024]{2,1,0:T(8,128)(2,1)S(1)}, bf16[16,16,1024]{2,1,0:T(8,128)(2,1)}, u32[]{:S(2)}) copy-start(bf16[16,16,1024]{2,1,0:T(8,128)(2,1)} %all_to_all.41) | copy-start | bytes 1572868
  240.4 12.2 %collective-permute-start.22 = (bf16[256,704]{1,0:T(8,128)(2,1)}, bf16[256,704]{1,0:T(8,128)(2,1)S(1)}, u32[]{:S(2)}, u32[]{:S(2)}) collective-permute-start(bf16[256,704]{1,0:T(8,128)(2,1)} %expert_in.4.refs_0_), channel_id=1, source_target_pairs={{0,1},{1,0},{2,3},{3,2},{4,5},{5,4},{6,7},{7,6},{8,9},{9,8},{10,11... | collective-permute-start | bytes 1081352 | tf_op jit(solution)/shard_map/ppermute | solution.py:46
  242.0 21.8 %collective-permute-start.24 = (bf16[256,1024]{1,0:T(8,128)(2,1)S(1)}, bf16[256,1024]{1,0:T(8,128)(2,1)}, u32[]{:S(2)}, u32[]{:S(2)}) collective-permute-start(bf16[256,1024]{1,0:T(8,128)(2,1)S(1)} %bitcast.67), channel_id=1, source_target_pairs={{0,1},{1,0},{2,3},{3,2},{4,5},{5,4},{6,7},{7,6},{8,9},{9,8},{10,11... | collective-permute-start | bytes 1572872 | tf_op jit(solution)/shard_map/ppermute | solution.py:46
  258.0 45.1 %copy-start.5 = (bf16[16,16,1024]{2,1,0:T(8,128)(2,1)}, bf16[16,16,1024]{2,1,0:T(8,128)(2,1)S(1)}, u32[]{:S(2)}) copy-start(bf16[16,16,1024]{2,1,0:T(8,128)(2,1)S(1)} %all-to-all-done.6) | copy-start | bytes 1572868
  258.0 30.0 %all-to-all-start.1 = ((bf16[16,16,1024]{2,1,0:T(8,128)(2,1)}), bf16[16,16,1024]{2,1,0:T(8,128)(2,1)S(1)}, u32[]{:S(2)}, u32[]{:S(2)}) async-start(bf16[16,16,1024]{2,1,0:T(8,128)(2,1)} %bitcast.59), calls=%async_computation.1 | async-start | bytes 1048576 | tf_op jit(solution)/shard_map/all_to_all | solution.py:492
  270.5 12.1 %collective-permute-start.25 = (bf16[256,704]{1,0:T(8,128)(2,1)}, bf16[256,704]{1,0:T(8,128)(2,1)S(1)}, u32[]{:S(2)}, u32[]{:S(2)}) collective-permute-start(bf16[256,704]{1,0:T(8,128)(2,1)} %expert_in.5.refs_0_), channel_id=1, source_target_pairs={{0,1},{1,0},{2,3},{3,2},{4,5},{5,4},{6,7},{7,6},{8,9},{9,8},{10,11... | collective-permute-start | bytes 1081352 | tf_op jit(solution)/shard_map/ppermute | solution.py:46
  272.0 22.1 %collective-permute-start.26 = (bf16[256,1024]{1,0:T(8,128)(2,1)S(1)}, bf16[256,1024]{1,0:T(8,128)(2,1)S(1)}, u32[]{:S(2)}, u32[]{:S(2)}) collective-permute-start(bf16[256,1024]{1,0:T(8,128)(2,1)S(1)} %bitcast.64), channel_id=1, source_target_pairs={{0,1},{1,0},{2,3},{3,2},{4,5},{5,4},{6,7},{7,6},{8,9},{9,8},{10,11... | collective-permute-start | bytes 1572872 | tf_op jit(solution)/shard_map/ppermute | solution.py:46
  288.0 31.0 %all-to-all-start.3 = ((bf16[16,16,1024]{2,1,0:T(8,128)(2,1)}), bf16[16,16,1024]{2,1,0:T(8,128)(2,1)S(1)}, u32[]{:S(2)}, u32[]{:S(2)}) async-start(bf16[16,16,1024]{2,1,0:T(8,128)(2,1)} %bitcast.60), calls=%async_computation.3 | async-start | bytes 1048576 | tf_op jit(solution)/shard_map/all_to_all | solution.py:492
  301.6 12.1 %collective-permute-start.27 = (bf16[256,704]{1,0:T(8,128)(2,1)}, bf16[256,704]{1,0:T(8,128)(2,1)S(1)}, u32[]{:S(2)}, u32[]{:S(2)}) collective-permute-start(bf16[256,704]{1,0:T(8,128)(2,1)} %expert_in.6.refs_0_), channel_id=1, source_target_pairs={{0,1},{1,0},{2,3},{3,2},{4,5},{5,4},{6,7},{7,6},{8,9},{9,8},{10,11... | collective-permute-start | bytes 1081352 | tf_op jit(solution)/shard_map/ppermute | solution.py:46
  303.1 22.0 %collective-permute-start.28 = (bf16[256,1024]{1,0:T(8,128)(2,1)S(1)}, bf16[256,1024]{1,0:T(8,128)(2,1)S(1)}, u32[]{:S(2)}, u32[]{:S(2)}) collective-permute-start(bf16[256,1024]{1,0:T(8,128)(2,1)S(1)} %bitcast.62), channel_id=1, source_target_pairs={{0,1},{1,0},{2,3},{3,2},{4,5},{5,4},{6,7},{7,6},{8,9},{9,8},{10,11... | collective-permute-start | bytes 1572872 | tf_op jit(solution)/shard_map/ppermute | solution.py:46
  319.0 30.6 %all-to-all-start.5 = ((bf16[16,16,1024]{2,1,0:T(8,128)(2,1)}), bf16[16,16,1024]{2,1,0:T(8,128)(2,1)S(1)}, u32[]{:S(2)}, u32[]{:S(2)}) async-start(bf16[16,16,1024]{2,1,0:T(8,128)(2,1)} %bitcast.58), calls=%async_computation.5 | async-start | bytes 1048576 | tf_op jit(solution)/shard_map/all_to_all | solution.py:492
  332.6 11.7 %collective-permute-start.29 = (bf16[256,704]{1,0:T(8,128)(2,1)}, bf16[256,704]{1,0:T(8,128)(2,1)S(1)}, u32[]{:S(2)}, u32[]{:S(2)}) collective-permute-start(bf16[256,704]{1,0:T(8,128)(2,1)} %expert_in.7.refs_0_), channel_id=1, source_target_pairs={{0,1},{1,0},{2,3},{3,2},{4,5},{5,4},{6,7},{7,6},{8,9},{9,8},{10,11... | collective-permute-start | bytes 1081352 | tf_op jit(solution)/shard_map/ppermute | solution.py:46
  349.6 20.3 %copy-start.15 = (bf16[16,16,1024]{2,1,0:T(8,128)(2,1)}, bf16[16,16,1024]{2,1,0:T(8,128)(2,1)S(1)}, u32[]{:S(2)}) copy-start(bf16[16,16,1024]{2,1,0:T(8,128)(2,1)S(1)} %all-to-all-done.5) | copy-start | bytes 1572868
  (20 other events, 101.4 us)

commit v2 on v1

v2 whole, which is shorter than its diff:
```python
import functools
import math

import jax
import jax.numpy as jnp
from jax import lax
from jax.experimental import pallas as pl
from jax.experimental.pallas import tpu as pltpu
from jax.sharding import PartitionSpec as P

D = 2048
QB = 16
PAIRS = 4
BAND = 2
TOP = 2
HEAD_DIM = 128
FIRST_HEADS = 4
EXPERT_GROUPS = (3, 5, 7, 8)
TAG_ROWS = 16
LANES = 128

MASKED_SCORE = -1e30
NO_CAP = 3e38
NORM_EPSILON = 1e-06
F32 = jnp.float32
BF16 = jnp.bfloat16


def dot(a, b):
    return jnp.dot(a, b, preferred_element_type=F32)


def dot_nt(a, b):
    return lax.dot_general(a, b, (((1,), (1,)), ((), ())), preferred_element_type=F32)


def chip_ring(rows, columns):
    order = []
    for row in range(rows):
        inner = list(range(1, columns))
        order += [(row, x) for x in (inner if row % 2 == 0 else inner[::-1])]
    order += [(row, 0) for row in range(rows - 1, -1, -1)]
    return [z * columns + x for z, x in order]


def shifted(x, axis, size, shift):
    return lax.ppermute(x, axis, [(i, (i + shift) % size) for i in range(size)])


def swap_cores(x, tracks):
    return lax.ppermute(x, "track", [(i, i ^ 1) for i in range(tracks)])


def attention_kernel(blocks, heads, causal, carried, *refs):
    q_ref, qbar_ref, kbar_ref = refs[:3]
    kv_refs = refs[3 : 3 + blocks]
    earlier = refs[3 + blocks : 3 + blocks + 2 * carried]
    *out_refs, cap_ref, score_ref = refs[3 + blocks + 2 * carried :]
    head = pl.program_id(0)
    events = q_ref.shape[1]
    exponent_scale = math.log2(math.e) / math.sqrt(HEAD_DIM)

    @pl.when(head == 0)
    def _():
        row = lax.broadcasted_iota(jnp.int32, (events, events), 0)
        column = lax.broadcasted_iota(jnp.int32, (events, events), 1)
        for side in range(2):
            for b in range(blocks):
                back = qbar_ref[side, :, b : b + 1] - kbar_ref[b : b + 1, :]
                allowed = (back >= 0) & (back <= BAND)
                if causal and side == 0 and b == 0:
                    allowed = allowed & (column <= row)
                cap_ref[b, side] = jnp.where(allowed, NO_CAP, MASKED_SCORE)

    lane = lax.broadcasted_iota(jnp.int32, (events, LANES), 1)
    columns = pl.ds(pl.multiple_of(head * HEAD_DIM, HEAD_DIM), HEAD_DIM)
    for side, out_ref in enumerate(out_refs):
        query = q_ref[side]
        peaks = None
        for b in range(blocks):
            scores = jnp.minimum(dot_nt(query, kv_refs[b][0]), cap_ref[b, side])
            score_ref[b] = scores
            for start in range(0, events, LANES):
                part = scores[:, start : start + LANES]
                peaks = part if peaks is None else jnp.maximum(peaks, part)
        peak = peaks.max(axis=1, keepdims=True)
        value = jnp.zeros((events, HEAD_DIM), F32)
        mass = jnp.zeros((events, 1), F32)
        if carried:
            stat = earlier[side][:, heads * HEAD_DIM :]
            old_peak = jnp.sum(jnp.where(lane == head, stat, 0.0), axis=1, keepdims=True)
            mass = jnp.sum(jnp.where(lane == heads + head, stat, 0.0), axis=1, keepdims=True)
            peak = jnp.maximum(peak, old_peak)
            shrink = jnp.exp2((old_peak - peak) * exponent_scale)
            mass = mass * shrink
            value = earlier[side][:, columns] * shrink
        masses = jnp.zeros((events, LANES), F32)
        for b in range(blocks):
            weights = jnp.exp2((score_ref[b] - peak) * exponent_scale)
            for start in range(0, events, LANES):
                masses = masses + weights[:, start : start + LANES]
            value = value + dot(weights.astype(BF16), kv_refs[b][1])
        mass = mass + masses.sum(axis=1, keepdims=True)
        out_ref[:, columns] = value
        stat = jnp.where(lane == head, peak, jnp.where(lane == heads + head, mass, 0.0))

        @pl.when(head == 0)
        def _():
            out_ref[:, heads * HEAD_DIM :] = stat

        @pl.when(head != 0)
        def _():
            out_ref[:, heads * HEAD_DIM :] += stat


def attention(q, qbar, kbar, kvs, causal, earlier=()):
    blocks, events, width = len(kvs), q.shape[1], q.shape[2]
    heads = width // HEAD_DIM
    shape = jax.ShapeDtypeStruct((events, width + LANES), F32)
    flops = 4 * 2 * events * blocks * events * width
    return pl.pallas_call(
        functools.partial(attention_kernel, blocks, heads, causal, bool(earlier)),
        grid=(heads,),
        in_specs=[
            pl.BlockSpec((2, events, HEAD_DIM), lambda h: (0, 0, h)),
            pl.BlockSpec(qbar.shape, lambda h: (0, 0, 0)),
            pl.BlockSpec(kbar.shape, lambda h: (0, 0)),
        ]
        + [pl.BlockSpec((2, events, HEAD_DIM), lambda h: (0, 0, h))] * blocks
        + [pl.BlockSpec(shape.shape, lambda h: (0, 0))] * len(earlier),
        out_specs=[pl.BlockSpec(shape.shape, lambda h: (0, 0))] * 2,
        out_shape=[shape, shape],
        scratch_shapes=[
            pltpu.VMEM((blocks, 2, events, events), F32),
            pltpu.VMEM((blocks, events, events), F32),
        ],
        cost_estimate=pl.CostEstimate(
            flops=flops, bytes_accessed=blocks * events * width * 4, transcendentals=flops // 512
        ),
        name="attention",
    )(q, qbar, kbar, *kvs, *earlier)


def merge_kernel(heads, a_ref, b_ref, out_ref):
    scale = 1.0 / math.sqrt(HEAD_DIM)
    for head in range(heads):
        at = heads * HEAD_DIM + head
        peak_a, mass_a = a_ref[:, at : at + 1], a_ref[:, at + heads : at + heads + 1]
        peak_b, mass_b = b_ref[:, at : at + 1], b_ref[:, at + heads : at + heads + 1]
        peak = jnp.maximum(peak_a, peak_b)
        scale_a = jnp.exp((peak_a - peak) * scale)
        scale_b = jnp.exp((peak_b - peak) * scale)
        part = slice(head * HEAD_DIM, (head + 1) * HEAD_DIM)
        total = scale_a * a_ref[:, part] + scale_b * b_ref[:, part]
        out_ref[:, part] = (total / (scale_a * mass_a + scale_b * mass_b)).astype(BF16)


def merge(a, b):
    events, width = a.shape[0], a.shape[1] - LANES
    return pl.pallas_call(
        functools.partial(merge_kernel, width // HEAD_DIM),
        out_shape=jax.ShapeDtypeStruct((events, width), BF16),
        cost_estimate=pl.CostEstimate(
            flops=8 * events * width, bytes_accessed=10 * events * width, transcendentals=0
        ),
        name="merge",
    )(a, b)


def project_kernel(count, experts, *refs):
    attended, weights = refs[:count], refs[count : 2 * count]
    residual_ref, gain_ref, router_ref, hidden_ref, stat_ref = refs[2 * count :]
    step = pl.program_id(0)
    total = residual_ref[...].astype(F32)
    for part, weight in zip(attended, weights, strict=True):
        total = total + dot(part[...], weight[...])
    hidden = total.astype(BF16)
    hidden_ref[...] = hidden
    wide = hidden.astype(F32)
    scaled = (wide * gain_ref[...].astype(F32)).astype(BF16)
    lane = lax.broadcasted_iota(jnp.int32, stat_ref.shape, 1)
    square = jnp.sum(wide * wide, axis=1, keepdims=True)
    stat = dot(scaled, router_ref[...]) + jnp.where(lane == experts, square, 0.0)

    @pl.when(step == 0)
    def _():
        stat_ref[...] = stat

    @pl.when(step != 0)
    def _():
        stat_ref[...] += stat


def project(attended, weights, residual, gain, router, experts):
    events, width = residual.shape
    tile = 256
    return pl.pallas_call(
        functools.partial(project_kernel, len(attended), experts),
        grid=(width // tile,),
        in_specs=[pl.BlockSpec(part.shape, lambda j: (0, 0)) for part in attended]
        + [pl.BlockSpec((w.shape[0], tile), lambda j: (0, j)) for w in weights]
        + [
            pl.BlockSpec((events, tile), lambda j: (0, j)),
            pl.BlockSpec((1, tile), lambda j: (0, j)),
            pl.BlockSpec((tile, LANES), lambda j: (j, 0)),
        ],
        out_specs=[
            pl.BlockSpec((events, tile), lambda j: (0, j)),
            pl.BlockSpec((events, LANES), lambda j: (0, 0)),
        ],
        out_shape=[
            jax.ShapeDtypeStruct((events, width), BF16),
            jax.ShapeDtypeStruct((events, LANES), F32),
        ],
        cost_estimate=pl.CostEstimate(
            flops=2 * events * D * width, bytes_accessed=2 * D * width, transcendentals=0
        ),
        name="project",
    )(*attended, *weights, residual, gain, router)


def pack_kernel(sources, experts, *refs):
    hidden_ref = refs[0]
    stats = refs[1 : 1 + sources]
    gain_ref, route_ref, tag_ref, block_ref, gate_ref = refs[1 + sources :]
    total = functools.reduce(jnp.add, [s[...] for s in stats])
    events = total.shape[0]
    lane = lax.broadcasted_iota(jnp.int32, total.shape, 1)
    square = jnp.sum(jnp.where(lane == experts, total, 0.0), axis=1, keepdims=True)
    inverse = lax.rsqrt(square / D + NORM_EPSILON)
    block_ref[:events, :] = (
        hidden_ref[...].astype(F32) * inverse * gain_ref[...].astype(F32)
    ).astype(BF16)
    block_ref[events:, :events] = tag_ref[...]
    logits = total * inverse
    parts = []
    for k in range(TOP):
        chosen = jnp.sum(
            jnp.where(lane == route_ref[:, k : k + 1], logits, 0.0), axis=1, keepdims=True
        )
        parts.append(1.0 / (1.0 + jnp.exp(-chosen)))
    whole = parts[0] + parts[1]
    gate_ref[...] = jnp.where(
        lane == 0, parts[0] / whole, jnp.where(lane == 1, parts[1] / whole, 0.0)
    )


def pack(hidden, stats, gain, route, tags, experts):
    events, width = hidden.shape
    return pl.pallas_call(
        functools.partial(pack_kernel, len(stats), experts),
        out_shape=[
            jax.ShapeDtypeStruct((events + TAG_ROWS, width), BF16),
            jax.ShapeDtypeStruct((events, LANES), F32),
        ],
        cost_estimate=pl.CostEstimate(
            flops=8 * events * width, bytes_accessed=4 * events * width, transcendentals=0
        ),
        name="pack",
    )(hidden, *stats, gain, route, tags)


def select_kernel(count, slots, experts_ref, *refs):
    blocks, out_ref = refs[:count], refs[count]
    events = blocks[0].shape[0] - TAG_ROWS
    row = lax.broadcasted_iota(jnp.int32, (2 * slots, events), 0)
    expert = jnp.where(row < slots, experts_ref[0], experts_ref[1])
    wanted = (expert * slots + row % slots).astype(F32)
    for i, block in enumerate(blocks):
        tags = block[events:, :events].astype(F32)
        hit = wanted == tags[0:1, :] * slots + tags[1:2, :]
        for k in range(1, TOP):
            hit = hit | (wanted == tags[2 * k : 2 * k + 1, :] * slots + tags[2 * k + 1 : 2 * k + 2, :])
        rows = dot(jnp.where(hit, 1.0, 0.0).astype(BF16), block[:events, :]).astype(BF16)
        for e in range(2):
            out_ref[e, i * slots : (i + 1) * slots, :] = rows[e * slots : (e + 1) * slots]


def select(experts, blocks, slots):
    count, width = len(blocks), blocks[0].shape[1]
    out = jax.ShapeDtypeStruct((2, count * slots, width), BF16)
    return pl.pallas_call(
        functools.partial(select_kernel, count, slots),
        in_specs=[pl.BlockSpec(memory_space=pltpu.SMEM)]
        + [pl.BlockSpec(memory_space=pltpu.VMEM)] * count,
        out_shape=out,
        cost_estimate=pl.CostEstimate(
            flops=4 * count * slots * blocks[0].shape[0] * width,
            bytes_accessed=2 * count * width * (blocks[0].shape[0] + 2 * slots),
            transcendentals=0,
        ),
        name="select",
    )(experts, *blocks)


def expert_in_kernel(sources, per_source, kmap_ref, *refs):
    rows = refs[:sources]
    weights = refs[sources : sources + 4]
    out_ref, gate_sum, up_sum = refs[sources + 4 :]
    step = pl.program_id(0)

    @pl.when(step == 0)
    def _():
        gate_sum[...] = jnp.zeros_like(gate_sum)
        up_sum[...] = jnp.zeros_like(up_sum)

    for source in range(sources):

        @pl.when(step // per_source == source)
        def _():
            for e in range(2):
                x = rows[source][e]
                gate_sum[e] += dot_nt(x, weights[2 * e][0])
                up_sum[e] += dot_nt(x, weights[2 * e + 1][0])

    @pl.when(step == pl.num_programs(0) - 1)
    def _():
        gate = gate_sum[...]
        out_ref[...] = (gate / (1.0 + jnp.exp(-gate)) * up_sum[...]).astype(BF16)


def expert_in(rows, weights, my_head):
    sources = len(rows)
    _, count, width = rows[0].shape
    units = weights[0].shape[1]
    tile = min(width, 1024)
    per_source = width // tile
    steps = sources * per_source
    number = jnp.arange(steps, dtype=jnp.int32)
    kmap = (my_head - number // per_source + sources) % sources * per_source + number % per_source

    def row_map(source):
        return lambda k, m: (0, 0, jnp.clip(k - source * per_source, 0, per_source - 1))

    weight = pl.BlockSpec((1, units, tile), lambda k, m: (0, 0, m[k]))
    return pl.pallas_call(
        functools.partial(expert_in_kernel, sources, per_source),
        grid_spec=pltpu.PrefetchScalarGridSpec(
            num_scalar_prefetch=1,
            grid=(steps,),
            in_specs=[pl.BlockSpec((2, count, tile), row_map(s)) for s in range(sources)]
            + [weight] * 4,
            out_specs=pl.BlockSpec((2, count, units), lambda k, m: (0, 0, 0)),
            scratch_shapes=[pltpu.VMEM((2, count, units), F32)] * 2,
        ),
        out_shape=jax.ShapeDtypeStruct((2, count, units), BF16),
        cost_estimate=pl.CostEstimate(
            flops=8 * count * D * units,
            bytes_accessed=8 * D * units,
            transcendentals=2 * count * units,
        ),
        name="expert_in",
    )(kmap, *rows, *weights)


def expert_out_kernel(sources, slots, *refs):
    acts = refs[:sources]
    weights = refs[sources : 3 * sources]
    outs = refs[3 * sources :]
    for e in range(2):
        total = dot(acts[0][e], weights[e * sources][...])
        for s in range(1, sources):
            total = total + dot(acts[s][e], weights[e * sources + s][...])
        total = total.astype(BF16)
        for i, out_ref in enumerate(outs):
            out_ref[e] = total[i * slots : (i + 1) * slots]


def expert_out(acts, weights, slots):
    sources = len(acts)
    _, count, units = acts[0].shape
    width = weights[0][0].shape[1]
    blocks = count // slots
    tile = min(width, 512)
    return pl.pallas_call(
        functools.partial(expert_out_kernel, sources, slots),
        grid=(width // tile,),
        in_specs=[pl.BlockSpec((2, count, units), lambda j: (0, 0, 0))] * sources
        + [pl.BlockSpec((units, tile), lambda j: (0, j))] * (2 * sources),
        out_specs=[pl.BlockSpec((2, slots, tile), lambda j: (0, 0, j))] * blocks,
        out_shape=[jax.ShapeDtypeStruct((2, slots, width), BF16)] * blocks,
        cost_estimate=pl.CostEstimate(
            flops=4 * sources * count * units * width,
            bytes_accessed=4 * sources * units * width,
            transcendentals=0,
        ),
        name="expert_out",
    )(*acts, *weights[0], *weights[1])


def combine_kernel(first, count, slots, base_ref, gate_ref, code_ref, *refs):
    returned, out_ref = refs[:count], refs[count]
    total = base_ref[...].astype(F32)
    events = total.shape[0]
    column = lax.broadcasted_iota(jnp.int32, (events, 2 * slots), 1)
    picked = [None] * TOP
    for i, block in enumerate(returned):
        back = block[...].reshape(2 * slots, block.shape[2])
        for k in range(TOP):
            hit = column + (first + i) * 2 * slots == code_ref[:, k : k + 1]
            part = dot(jnp.where(hit, 1.0, 0.0).astype(BF16), back)
            picked[k] = part if i == 0 else picked[k] + part
    for k in range(TOP):
        total = total + picked[k] * gate_ref[:, k : k + 1]
    out_ref[...] = total.astype(out_ref.dtype)


def combine(base, gates, codes, returned, first, dtype):
    events, width = base.shape
    count, slots = len(returned), returned[0].shape[1]
    return pl.pallas_call(
        functools.partial(combine_kernel, first, count, slots),
        out_shape=jax.ShapeDtypeStruct((events, width), dtype),
        cost_estimate=pl.CostEstimate(
            flops=8 * events * count * slots * width,
            bytes_accessed=4 * count * slots * width,
            transcendentals=0,
        ),
        name="combine",
    )(base, gates, codes, *returned)


def local(
    order,
    residual_in,
    queries,
    key_vectors,
    values,
    bar_index,
    pair_offset,
    out_proj,
    norm_gain,
    router,
    expert_route,
    w_gate,
    w_up,
    w_down,
):
    tracks = lax.axis_size("track")
    head_parts = lax.axis_size("head")
    my_track = lax.axis_index("track")
    my_head = lax.axis_index("head")
    events, width = queries.shape[1], queries.shape[2]
    chips = len(order)
    shifts = range(1, head_parts)

    barrier = lax.optimization_barrier

    forward = [
        (2 * order[i] + c, 2 * order[(i + 1) % chips] + c) for i in range(chips) for c in range(2)
    ]
    backward = [(b, a) for a, b in forward]
    hops = [0]
    for s in range(1, chips // 2):
        hops += [-s, s]
    hops.append(chips // 2)

    place = [0] * chips
    for i, chip in enumerate(order):
        place[chip] = i
    my_place = jnp.array(place, jnp.int32)[my_track // 2]
    block_chip = jnp.array(order, jnp.int32)[(my_place + jnp.array(hops, jnp.int32)) % chips]
    block_track = block_chip * 2 + my_track % 2
    key_bars = bar_index[block_track]
    query_track = jnp.stack([my_track, my_track ^ 1])
    query_bars = bar_index[query_track]
    partner = (query_track[:, None, None] + 1 + pair_offset[query_track]) % tracks
    listed = jnp.any(partner[:, :, :, None] == block_track, axis=2)
    listed = listed | (query_track[:, None, None] == block_track)
    listed = jnp.repeat(listed, QB, axis=1)
    query_bars = jnp.where(listed, query_bars[:, :, None], -1000)

    def columns_of(weight, owner):
        return lax.dynamic_slice_in_dim(weight, owner * width, width, 1)

    all_heads = width // HEAD_DIM
    cut = all_heads * FIRST_HEADS // 8 * HEAD_DIM
    parts = [slice(0, cut), slice(cut, width)]
    got = [
        [jnp.concatenate([key_vectors[:, :, part], values[:, :, part]], axis=0)] for part in parts
    ]
    both_queries = jnp.concatenate([queries, swap_cores(queries, tracks)], axis=0)
    chunk_queries = [both_queries[:, :, part] for part in parts]
    fetched = []
    for s in shifts:
        owner = (my_head + s) % head_parts
        out_part = columns_of(out_proj, owner)
        down_part = columns_of(w_down[0], owner)
        for part in (out_part[:cut], out_part[cut:], down_part):
            if fetched:
                part, fetched[-1] = barrier((part, fetched[-1]))
            fetched.append(shifted(part, "head", head_parts, s))
    in_weights = [jnp.swapaxes(w_gate, 1, 2), jnp.swapaxes(w_up, 1, 2)]
    in_weights += [swap_cores(w, tracks) for w in in_weights]

    steps = chips // 2
    ahead, back = [g[0] for g in got], [g[0] for g in got]
    for _ in range(1, steps):
        for i in range(2):
            ahead[i] = lax.ppermute(ahead[i], "track", forward)
            back[i] = lax.ppermute(back[i], "track", backward)
            got[i] += [ahead[i], back[i]]
    got[0].append(lax.ppermute(ahead[0], "track", forward))
    got[1].append(lax.ppermute(back[1], "track", backward))

    attended = [[] for _ in range(head_parts)]
    for i in range(2):
        mine, theirs = attention(chunk_queries[i], query_bars, key_bars, got[i], True)
        merged = merge(mine, swap_cores(theirs, tracks))
        attended[0].append(merged)
        for s in shifts:
            attended[s].append(shifted(merged, "head", head_parts, s))
    attended[0][0], fetched = barrier((attended[0][0], fetched))

    own_out = columns_of(out_proj, my_head)
    out_weights = [own_out[:cut], own_out[cut:]]
    down_weights = [columns_of(w_down[0], my_head)]
    for s in shifts:
        top, bottom, down = fetched[3 * s - 3 : 3 * s]
        out_weights += [top, bottom]
        down_weights.append(down)
    down_weights = [down_weights, [swap_cores(w, tracks) for w in down_weights]]

    experts = tracks
    wide_router = jnp.pad(router, ((0, 0), (0, LANES - experts)))
    gain = norm_gain.reshape(1, width)
    attended = [part for source in attended for part in source]
    hidden, stat = project(attended, out_weights, residual_in[0], gain, wide_router, experts)
    stats = [stat] + [shifted(stat, "head", head_parts, s) for s in shifts]

    slots = 2 * events * TOP // experts
    route = expert_route[0]
    flat = route.reshape(-1)
    hits = (flat[:, None] == jnp.arange(experts, dtype=jnp.int32)).astype(jnp.int32)
    rank = jnp.sum((jnp.cumsum(hits, axis=0) - hits) * hits, axis=1).reshape(events, TOP)
    tags = jnp.stack([route, rank], axis=2).reshape(events, 2 * TOP).T.astype(BF16)
    tags = jnp.pad(tags, ((0, TAG_ROWS - 2 * TOP), (0, 0)))
    hop_number = [0] * chips
    for i, hop in enumerate(hops):
        hop_number[hop % chips] = i
    hop_of_chip = jnp.array(hop_number, jnp.int32)[(my_place - jnp.array(place, jnp.int32)) % chips]
    chip_match = (route // 2)[:, :, None] == jnp.arange(chips, dtype=jnp.int32)
    hop_of_route = jnp.sum(jnp.where(chip_match, hop_of_chip, 0), axis=2)
    other_core = (route % 2 != my_track % 2).astype(jnp.int32)
    codes = (hop_of_route * 2 + other_core) * slots + rank
    my_experts = jnp.stack([my_track, my_track ^ 1])

    block, gates = pack(hidden, stats, gain, route, tags, experts)
    ends = [chips * share // 8 for share in EXPERT_GROUPS]
    blocks, forth, back = [block], block, block
    picked, ready = [], []
    for step in range(1, chips // 2 + 1):
        for group, when in enumerate(ready):
            if when == step - 2:
                forth, back, picked[group] = barrier((forth, back, picked[group]))
        forth = lax.ppermute(forth, "track", forward)
        blocks.append(forth)
        if step < chips // 2:
            back = lax.ppermute(back, "track", backward)
            blocks.append(back)
        while len(picked) < len(ends) and len(blocks) >= ends[len(picked)]:
            first = ends[len(picked) - 1] if picked else 0
            picked.append(select(my_experts, blocks[first : ends[len(picked)]], slots))
            ready.append(step)

    def across(x):
        return [x] + [shifted(x, "head", head_parts, s) for s in shifts]

    acts, returned, waiting, first = [], [], None, 0
    starts = [0] + ends[:-1]
    for group in range(len(ends) + 1):
        if group < len(ends):
            rows = across(picked[group])
            if waiting is not None:
                rows, waiting = barrier((rows, waiting))
            acts.append(across(expert_in(rows, in_weights, my_head)))
        if group > 0:
            outs = expert_out(acts[group - 1], down_weights, slots)
            for i, out in enumerate(outs):
                hop_length = hops[starts[group - 1] + i]
                pairs = [
                    (2 * order[p] + c, 2 * order[(p + hop_length) % chips] + c)
                    for p in range(chips)
                    for c in range(2)
                ]
                returned.append(lax.ppermute(out, "track", pairs) if hop_length else out)
            waiting = outs[0]
    result = combine(hidden, gates, codes, returned[: starts[-1]], 0, F32)
    result = combine(result, gates, codes, returned[starts[-1] :], starts[-1], BF16)
    return result[None]


def solution(mesh):
    chips, columns = mesh.shape["track"] // 2, mesh.shape["head"]
    order = chip_ring(chips // columns, columns)
    in_specs = (
        P("track", None, "head"),
        P("track", None, "head"),
        P("track", None, "head"),
        P("track", None, "head"),
        P(),
        P(),
        P("head", None),
        P("head"),
        P("head", None),
        P("track", None, None),
        P("track", None, "head"),
        P("track", None, "head"),
        P("track", "head", None),
    )
    out_specs = P("track", None, "head")
    return jax.shard_map(
        functools.partial(local, order),
        mesh=mesh,
        in_specs=in_specs,
        out_specs=out_specs,
        check_vma=False,
    )
```

time: 376 us -> 294 us (0.78)
  blocking collectives: 58.6 us -> 0 us
  waiting for transfers between devices: 125 us -> 97.3 us
  Pallas kernels: 95.4 us -> 106 us
  local copies, waits for them, and re-layouts: 32.3 us -> 26.6 us
    all_to_all x3 -> x0, blocking collectives: 58.6 us -> none  [the longest x2 38.3 us: local(): lax.all_to_all(outgoing[chunk].reshape(experts, slots, width), 'track', 0...]
    ppermute x8 -> x25, waiting for transfers between devices: 20.4 us -> 74.7 us  [the longest x6 26.7 us: local(): back[i] = lax.ppermute(back[i], 'track', backward)]
    ppermute x13 -> x14, waiting for transfers between devices: 68.2 us -> 20.6 us  [shifted(): return lax.ppermute(x, axis, [(i, (i + shift) % size) for i in range(size)])]
    all_to_all x5 -> x0, starting transfers between devices: 26 us -> none  [the longest x3 17.9 us: local(): lax.all_to_all(result.reshape(experts, slots, width), 'track', 0, 0, tile...]
    ppermute x6 -> x3, waiting for transfers between devices: 25.5 us -> 2 us  [local(): back = lax.ppermute(back, 'track', backward)]
    ppermute x8 -> x25, starting transfers between devices: 13.8 us -> 35.7 us  [the longest x7 11.9 us: local(): returned.append(lax.ppermute(out, 'track', pairs) if hop_length else out)]
    all_to_all x5 -> x0, waiting for transfers between devices: 10.5 us -> none  [the longest x2 10.5 us: local(): lax.all_to_all(outgoing[chunk].reshape(experts, slots, width), 'track', 0...]
    unnamed x71 -> x93, local copies, waits for them, and re-layouts: 16.6 us -> 9.41 us
  transfers between devices with their start and end apart: 35 -> 49, of which waited for: 15 -> 19; matrix products, arithmetic and copies ran while one was open for 7% -> 8% of each run, Pallas kernels for 22% -> 35%
where the time goes in v2:
time: 294 us; the launch traced here: 293 us
  Pallas kernels  106 us (36%)
  waiting for transfers between devices  97.3 us (33%)
  starting transfers between devices  56.3 us (19%)
  local copies, waits for them, and re-layouts  26.6 us (9%)
  other arithmetic  6.41 us (2%)
    pallas_call x4, Pallas kernels, expert_in(): pl.pallas_call(functools.partial(expert_in_kernel, sources, per_source),...  33.3 us
    ppermute x6, waiting for transfers between devices, local(): back[i] = lax.ppermute(back[i], 'track', backward)  26.7 us
    ppermute x4, waiting for transfers between devices, local(): forth = lax.ppermute(forth, 'track', forward)  25.3 us
    pallas_call x2, Pallas kernels, attention(): pl.pallas_call(functools.partial(attention_kernel, blocks, heads, causal,...  24.6 us
    ppermute x14, waiting for transfers between devices, shifted(): return lax.ppermute(x, axis, [(i, (i + shift) % size) for i in range(size)])  20.6 us
    ppermute x14, starting transfers between devices, shifted(): return lax.ppermute(x, axis, [(i, (i + shift) % size) for i in range(size)])  18.2 us
    pallas_call x4, Pallas kernels, expert_out(): pl.pallas_call(functools.partial(expert_out_kernel, sources, slots), grid...  17.1 us
    ppermute x7, waiting for transfers between devices, local(): returned.append(lax.ppermute(out, 'track', pairs) if hop_length else out)  17 us
  transfers between devices with their start and end apart: 49, of which 19 were waited for; matrix products, arithmetic and copies ran while one was open for 8% of the time, Pallas kernels for 35%

profile of v2, /device:TPU:0, one launch (start us, length us, event | category | flops | bytes accessed | tf_op | source)
XLA Modules:
  0.0 293.0 jit_solution(13142290963959831757)
XLA Ops:
  2.1 2.9 %collective-permute-start.1 = (bf16[2,256,512]{2,1,0:T(8,128)(2,1)}, bf16[2,256,512]{2,1,0:T(8,128)(2,1)}, u32[]{:S(2)}, u32[]{:S(2)}) collective-permute-start(bf16[2,256,512]{2,1,0:T(8,128)(2,1)} %pad_maximum_fusion.refs_3_), channel_id=1, source_target_pairs={{4,12},{6,14},{12,20},{14,22},{20,28},{22,30},{28,24},{30,26},{24,... | collective-permute-start | bytes 1572872 | tf_op jit(solution)/shard_map/ppermute | solution.py:500
  5.2 4.4 %fusion.14 = (bf16[512,1024]{1,0:T(8,128)(2,1)}, bf16[512,1024]{1,0:T(8,128)(2,1)}, bf16[512,1024]{1,0:T(8,128)(2,1)}, bf16[512,1024]{1,0:T(8,128)(2,1)}) fusion(bf16[1024,2048]{1,0:T(8,128)(2,1)} %param.24, s32[]{:T(128)S(6)} %add.202, s32[]{:T(128)S(6)} %select_n.136, s32[]{:T(128)S(6)} %select_n.135), kind=kLoop, calls=%fused_computation.70 | loop fusion | bytes 8388620 | tf_op jit(solution)/shard_map/slice | solution.py:516
  9.6 2.0 collective-permute-start.9
  17.4 1.7 collective-permute-start.3
  21.8 8.2 %collective-permute-done.13.refs_5_ = bf16[2,256,512]{2,1,0:T(8,128)(2,1)} collective-permute-done((bf16[2,256,512]{2,1,0:T(8,128)(2,1)}, bf16[2,256,512]{2,1,0:T(8,128)(2,1)}, u32[]{:S(2)}, u32[]{:S(2)}) %collective-permute-start.13) | collective-permute-done | bytes 524320 | tf_op jit(solution)/shard_map/ppermute | solution.py:501
  30.4 5.3 %collective-permute-done.9.refs_6_ = bf16[512,1024]{1,0:T(8,128)(2,1)} collective-permute-done((bf16[512,1024]{1,0:T(8,128)(2,1)}, bf16[512,1024]{1,0:T(8,128)(2,1)}, u32[]{:S(2)}, u32[]{:S(2)}) %collective-permute-start.9) | collective-permute-done | bytes 1048608 | tf_op jit(solution)/shard_map/ppermute | solution.py:47
  35.7 1.8 collective-permute-start.4
  39.6 1.9 dynamic-slice_bitcast_fusion
  43.0 2.2 collective-permute-start.14
  45.7 10.7 %collective-permute-done.4.refs_7_ = bf16[2,256,512]{2,1,0:T(8,128)(2,1)} collective-permute-done((bf16[2,256,512]{2,1,0:T(8,128)(2,1)}, bf16[2,256,512]{2,1,0:T(8,128)(2,1)}, u32[]{:S(2)}, u32[]{:S(2)}) %collective-permute-start.4) | collective-permute-done | bytes 524320 | tf_op jit(solution)/shard_map/ppermute | solution.py:501
  56.8 1.7 collective-permute-start.7
  62.2 3.3 %collective-permute-done.14.refs_6_ = bf16[2,256,512]{2,1,0:T(8,128)(2,1)S(1)} collective-permute-done((bf16[2,256,512]{2,1,0:T(8,128)(2,1)S(1)}, bf16[2,256,512]{2,1,0:T(8,128)(2,1)S(1)}, u32[]{:S(2)}, u32[]{:S(2)}) %collective-permute-start.14) | collective-permute-done | bytes 524320 | tf_op jit(solution)/shard_map/ppermute | solution.py:500
  65.5 2.2 collective-permute-start.16
  69.0 1.9 collective-permute-start.11
  72.0 6.8 %collective-permute-done.6.refs_9_ = bf16[2,256,512]{2,1,0:T(8,128)(2,1)S(1)} collective-permute-done((bf16[2,256,512]{2,1,0:T(8,128)(2,1)}, bf16[2,256,512]{2,1,0:T(8,128)(2,1)S(1)}, u32[]{:S(2)}, u32[]{:S(2)}) %collective-permute-start.6) | collective-permute-done | bytes 524320 | tf_op jit(solution)/shard_map/ppermute | solution.py:501
  79.8 12.2 %attention.2 = (f32[256,640]{1,0:T(8,128)}, f32[256,640]{1,0:T(8,128)}) custom-call(bf16[2,256,512]{2,1,0:T(8,128)(2,1)} %get-tuple-element.80.refs_0_, s32[2,256,8]{2,1,0:T(8,128)} %bitcast_select_fusion.refs_1_, s32[8,256]{1,0:T(8,128)} %gather_fusion.3, bf16[2,256,512]{2,1,0:T(8,128)(2,1)} %pad_maximum_fusion.refs_3_, ...), custom_call_target="tpu_custom_call" | custom-call | flops 2147483648 | bytes 4194304 | tf_op jit(solution)/shard_map/attention/pallas_call | solution.py:121
  92.9 12.3 %attention.3 = (f32[256,640]{1,0:T(8,128)}, f32[256,640]{1,0:T(8,128)}) custom-call(bf16[2,256,512]{2,1,0:T(8,128)(2,1)} %get-tuple-element.79.refs_0_, s32[2,256,8]{2,1,0:T(8,128)} %bitcast_select_fusion.refs_1_, s32[8,256]{1,0:T(8,128)} %gather_fusion.3, bf16[2,256,512]{2,1,0:T(8,128)(2,1)} %pad_maximum_fusion.1.refs_3_, bf16[2,256,512]{2,1,0:T(8,128)(2,1)} %copy-done.33, ...), custom_call_target="tpu_custom_call" | custom-call | flops 2147483648 | bytes 4194304 | tf_op jit(solution)/shard_map/attention/pallas_call | solution.py:121
  107.8 2.9 merge.2.refs_0_
  112.2 2.9 merge.3.refs_1_
  117.6 2.6 collective-permute-done.20.refs_2_
  120.2 4.8 %collective-permute-done.21.refs_3_ = bf16[256,512]{1,0:T(8,128)(2,1)} collective-permute-done((bf16[256,512]{1,0:T(8,128)(2,1)}, bf16[256,512]{1,0:T(8,128)(2,1)}, u32[]{:S(2)}, u32[]{:S(2)}) %collective-permute-start.21) | collective-permute-done | bytes 262176 | tf_op jit(solution)/shard_map/ppermute | solution.py:47
  124.9 5.8 %project.1 = (bf16[256,1024]{1,0:T(8,128)(2,1)}, f32[256,128]{1,0:T(8,128)}) custom-call(bf16[256,512]{1,0:T(8,128)(2,1)} %merge.2.refs_0_, bf16[256,512]{1,0:T(8,128)(2,1)} %merge.3.refs_1_, bf16[256,512]{1,0:T(8,128)(2,1)} %collective-permute-done.20.refs_2_, bf16[256,512]{1,0:T(8,128)(2,1)} %collective-permute-done.21.refs_3_, ...), custom_call_target="tpu_custom_call" | custom-call | flops 1073741824 | bytes 4194304 | tf_op jit(solution)/shard_map/project/pallas_call | solution.py:197
  133.4 2.6 collective-permute-done.22.refs_2_
  136.6 2.5 pack.1
  141.2 10.9 %collective-permute-done.23.refs_1_ = bf16[272,1024]{1,0:T(8,128)(2,1)} collective-permute-done((bf16[272,1024]{1,0:T(8,128)(2,1)}, bf16[272,1024]{1,0:T(8,128)(2,1)}, u32[]{:S(2)}, u32[]{:S(2)}) %collective-permute-start.23) | collective-permute-done | bytes 557088 | tf_op jit(solution)/shard_map/ppermute | solution.py:556
  154.1 2.7 select.52.refs_0_
  156.8 7.2 %collective-permute-done.24.refs_0_ = bf16[272,1024]{1,0:T(8,128)(2,1)S(1)} collective-permute-done((bf16[272,1024]{1,0:T(8,128)(2,1)}, bf16[272,1024]{1,0:T(8,128)(2,1)S(1)}, u32[]{:S(2)}, u32[]{:S(2)}) %collective-permute-start.24) | collective-permute-done | bytes 557088 | tf_op jit(solution)/shard_map/ppermute | solution.py:556
  169.0 7.2 %collective-permute-done.35.refs_0_ = bf16[272,1024]{1,0:T(8,128)(2,1)S(1)} collective-permute-done((bf16[272,1024]{1,0:T(8,128)(2,1)}, bf16[272,1024]{1,0:T(8,128)(2,1)S(1)}, u32[]{:S(2)}, u32[]{:S(2)}) %collective-permute-start.35) | collective-permute-done | bytes 557088 | tf_op jit(solution)/shard_map/ppermute | solution.py:556
  177.5 2.3 select.53.refs_0_
  183.5 8.5 %expert_in.4.refs_0_ = bf16[2,192,704]{2,1,0:T(8,128)(2,1)} custom-call(s32[2]{0:T(128)} %and_select_fusion.kmap_ref, bf16[2,192,1024]{2,1,0:T(8,128)(2,1)} %select.52.refs_0_, bf16[2,192,1024]{2,1,0:T(8,128)(2,1)} %collective-permute-done.27.refs_1_, bf16[1,704,2048]{2,1,0:T(8,128)(2,1)} %bitcast.48, bf16[1,704,2048]{2,1,0:T(8,128)(2,1)} %bitcast.54, ...), custom_call_target="tpu_custom_call" | custom-call | flops 2214592512 | bytes 11534336 | tf_op jit(solution)/shard_map/expert_in/pallas_call | solution.py:336
  192.7 2.3 select.54.refs_0_
  196.4 8.3 %expert_in.5.refs_0_ = bf16[2,128,704]{2,1,0:T(8,128)(2,1)} custom-call(s32[2]{0:T(128)} %and_select_fusion.kmap_ref, bf16[2,128,1024]{2,1,0:T(8,128)(2,1)} %select.53.refs_0_, bf16[2,128,1024]{2,1,0:T(8,128)(2,1)} %copy-done.13, bf16[1,704,2048]{2,1,0:T(8,128)(2,1)} %bitcast.49, bf16[1,704,2048]{2,1,0:T(8,128)(2,1)} %bitcast.55, ...), custom_call_target="tpu_custom_call" | custom-call | flops 1476395008 | bytes 11534336 | tf_op jit(solution)/shard_map/expert_in/pallas_call | solution.py:336
  205.7 2.0 select.55.refs_0_
  209.7 4.7 %expert_out.4 = (bf16[2,64,1024]{2,1,0:T(8,128)(2,1)}, bf16[2,64,1024]{2,1,0:T(8,128)(2,1)}, bf16[2,64,1024]{2,1,0:T(8,128)(2,1)}) custom-call(bf16[2,192,704]{2,1,0:T(8,128)(2,1)} %expert_in.4.refs_0_, bf16[2,192,704]{2,1,0:T(8,128)(2,1)} %copy-done.8, bf16[704,1024]{1,0:T(8,128)(2,1)} %get-tuple-element.77.refs_2_, ...), custom_call_target="tpu_custom_call" | custom-call | flops 1107296256 | bytes 5767168 | tf_op jit(solution)/shard_map/expert_out/pallas_call | solution.py:375
  214.4 5.3 %collective-permute-done.41.refs_1_ = bf16[2,128,1024]{2,1,0:T(8,128)(2,1)S(1)} collective-permute-done((bf16[2,128,1024]{2,1,0:T(8,128)(2,1)}, bf16[2,128,1024]{2,1,0:T(8,128)(2,1)S(1)}, u32[]{:S(2)}, u32[]{:S(2)}) %collective-permute-start.41) | collective-permute-done | bytes 524320 | tf_op jit(solution)/shard_map/ppermute | solution.py:47
  220.6 8.5 %expert_in.6.refs_0_ = bf16[2,128,704]{2,1,0:T(8,128)(2,1)} custom-call(s32[2]{0:T(128)} %and_select_fusion.kmap_ref, bf16[2,128,1024]{2,1,0:T(8,128)(2,1)} %select.54.refs_0_, bf16[2,128,1024]{2,1,0:T(8,128)(2,1)} %copy-done.12, bf16[1,704,2048]{2,1,0:T(8,128)(2,1)} %bitcast.50, bf16[1,704,2048]{2,1,0:T(8,128)(2,1)} %bitcast.56, ...), custom_call_target="tpu_custom_call" | custom-call | flops 1476395008 | bytes 11534336 | tf_op jit(solution)/shard_map/expert_in/pallas_call | solution.py:336
  232.7 4.2 %expert_out.5 = (bf16[2,64,1024]{2,1,0:T(8,128)(2,1)}, bf16[2,64,1024]{2,1,0:T(8,128)(2,1)}) custom-call(bf16[2,128,704]{2,1,0:T(8,128)(2,1)} %expert_in.5.refs_0_, bf16[2,128,704]{2,1,0:T(8,128)(2,1)} %copy-done.16, bf16[704,1024]{1,0:T(8,128)(2,1)} %get-tuple-element.77.refs_2_, bf16[704,1024]{1,0:T(8,128)(2,1)} %collective-permute-done.11.refs_3_, ...), custom_call_target="tpu_custom_call" | custom-call | flops 738197504 | bytes 5767168 | tf_op jit(solution)/shard_map/expert_out/pallas_call | solution.py:375
  237.6 8.0 %expert_in.7.refs_0_ = bf16[2,64,704]{2,1,0:T(8,128)(2,1)} custom-call(s32[2]{0:T(128)} %and_select_fusion.kmap_ref, bf16[2,64,1024]{2,1,0:T(8,128)(2,1)} %select.55.refs_0_, bf16[2,64,1024]{2,1,0:T(8,128)(2,1)} %copy-done.23, bf16[1,704,2048]{2,1,0:T(8,128)(2,1)} %bitcast.51, bf16[1,704,2048]{2,1,0:T(8,128)(2,1)} %bitcast.57, ...), custom_call_target="tpu_custom_call" | custom-call | flops 738197504 | bytes 11534336 | tf_op jit(solution)/shard_map/expert_in/pallas_call | solution.py:336
  248.5 2.2 collective-permute-start.40
  250.8 4.2 %expert_out.6 = (bf16[2,64,1024]{2,1,0:T(8,128)(2,1)}, bf16[2,64,1024]{2,1,0:T(8,128)(2,1)}) custom-call(bf16[2,128,704]{2,1,0:T(8,128)(2,1)} %expert_in.6.refs_0_, bf16[2,128,704]{2,1,0:T(8,128)(2,1)} %copy-done.15, bf16[704,1024]{1,0:T(8,128)(2,1)} %get-tuple-element.77.refs_2_, bf16[704,1024]{1,0:T(8,128)(2,1)} %collective-permute-done.11.refs_3_, ...), custom_call_target="tpu_custom_call" | custom-call | flops 738197504 | bytes 5767168 | tf_op jit(solution)/shard_map/expert_out/pallas_call | solution.py:375
  255.0 2.1 collective-permute-start.43
  257.1 1.7 collective-permute-start.44
  259.2 4.1 %expert_out.7 = bf16[2,64,1024]{2,1,0:T(8,128)(2,1)} custom-call(bf16[2,64,704]{2,1,0:T(8,128)(2,1)} %expert_in.7.refs_0_, bf16[2,64,704]{2,1,0:T(8,128)(2,1)} %copy-done.25, bf16[704,1024]{1,0:T(8,128)(2,1)} %get-tuple-element.77.refs_2_, bf16[704,1024]{1,0:T(8,128)(2,1)} %collective-permute-done.11.refs_3_, ...), custom_call_target="tpu_custom_call" | custom-call | flops 369098752 | bytes 5767168 | tf_op jit(solution)/shard_map/expert_out/pallas_call | solution.py:375
  263.2 3.0 %collective-permute-start.48 = (bf16[2,64,1024]{2,1,0:T(8,128)(2,1)}, bf16[2,64,1024]{2,1,0:T(8,128)(2,1)S(1)}, u32[]{:S(2)}, u32[]{:S(2)}) collective-permute-start(bf16[2,64,1024]{2,1,0:T(8,128)(2,1)} %expert_out.7), channel_id=1, source_target_pairs={{4,24},{6,26},{12,16},{14,18},{20,8},{22,10},{28,0},{30,2},{24,4},... | collective-permute-start | bytes 786440 | tf_op jit(solution)/shard_map/ppermute | solution.py:586
  267.0 10.8 %collective-permute-done.40.refs_4_ = bf16[2,64,1024]{2,1,0:T(8,128)(2,1)S(1)} collective-permute-done((bf16[2,64,1024]{2,1,0:T(8,128)(2,1)S(1)}, bf16[2,64,1024]{2,1,0:T(8,128)(2,1)S(1)}, u32[]{:S(2)}, u32[]{:S(2)}) %collective-permute-start.40) | collective-permute-done | bytes 262176 | tf_op jit(solution)/shard_map/ppermute | solution.py:586
  277.9 6.2 %collective-permute-done.43.refs_5_ = bf16[2,64,1024]{2,1,0:T(8,128)(2,1)S(1)} collective-permute-done((bf16[2,64,1024]{2,1,0:T(8,128)(2,1)}, bf16[2,64,1024]{2,1,0:T(8,128)(2,1)S(1)}, u32[]{:S(2)}, u32[]{:S(2)}) %collective-permute-start.43) | collective-permute-done | bytes 262176 | tf_op jit(solution)/shard_map/ppermute | solution.py:586
  284.8 4.8 %combine.2.base_ref = f32[256,1024]{1,0:T(8,128)} custom-call(bf16[256,1024]{1,0:T(8,128)(2,1)} %get-tuple-element.48.refs_0_.base_ref, f32[256,128]{1,0:T(8,128)} %get-tuple-element.50.gate_ref, s32[256,2]{1,0:T(8,128)} %add.195.code_ref, bf16[2,64,1024]{2,1,0:T(8,128)(2,1)} %get-tuple-element.54.refs_0_, bf16[2,64,1024]{2,1,0:T(8,128)(2,1)} %copy-done.17, ...), custom_call_target="tpu_custom_call" | custom-call | flops 939524096 | bytes 1835008 | tf_op jit(solution)/shard_map/combine/pallas_call | solution.py:411
  290.3 2.7 combine.3
  (217 shorter events, 63.0 us)
Async XLA Ops:
  2.1 15.3 %collective-permute-start.1 = (bf16[2,256,512]{2,1,0:T(8,128)(2,1)}, bf16[2,256,512]{2,1,0:T(8,128)(2,1)}, u32[]{:S(2)}, u32[]{:S(2)}) collective-permute-start(bf16[2,256,512]{2,1,0:T(8,128)(2,1)} %pad_maximum_fusion.refs_3_), channel_id=1, source_target_pairs={{4,12},{6,14},{12,20},{14,22},{20,28},{22,30},{28,24},{30,26},{24,... | collective-permute-start | bytes 1572872 | tf_op jit(solution)/shard_map/ppermute | solution.py:500
  5.1 15.2 %collective-permute-start.2 = (bf16[2,256,512]{2,1,0:T(8,128)(2,1)}, bf16[2,256,512]{2,1,0:T(8,128)(2,1)}, u32[]{:S(2)}, u32[]{:S(2)}) collective-permute-start(bf16[2,256,512]{2,1,0:T(8,128)(2,1)} %pad_maximum_fusion.refs_3_), channel_id=1, source_target_pairs={{12,4},{14,6},{20,12},{22,14},{28,20},{30,22},{24,28},{26,30},{16,... | collective-permute-start | bytes 1572872 | tf_op jit(solution)/shard_map/ppermute | solution.py:501
  5.1 32.4 %collective-permute-start = (bf16[1,256,1024]{2,1,0:T(8,128)(2,1)}, bf16[1,256,1024]{2,1,0:T(8,128)(2,1)}, u32[]{:S(2)}, u32[]{:S(2)}) collective-permute-start(bf16[1,256,1024]{2,1,0:T(8,128)(2,1)} %param.19), channel_id=1, source_target_pairs={{0,2},{2,0},{4,6},{6,4},{8,10},{10,8},{12,14},{14,12},{16,18},{18,... | collective-permute-start | bytes 1572872 | tf_op jit(solution)/shard_map/ppermute | solution.py:51
  9.6 26.1 %collective-permute-start.9 = (bf16[512,1024]{1,0:T(8,128)(2,1)}, bf16[512,1024]{1,0:T(8,128)(2,1)}, u32[]{:S(2)}, u32[]{:S(2)}) collective-permute-start(bf16[512,1024]{1,0:T(8,128)(2,1)} %get-tuple-element.76), channel_id=1, source_target_pairs={{0,1},{1,0},{2,3},{3,2},{4,5},{5,4},{6,7},{7,6},{8,9},{9,8},{10,11... | collective-permute-start | bytes 3145736 | tf_op jit(solution)/shard_map/ppermute | solution.py:47
  12.4 17.6 %collective-permute-start.13 = (bf16[2,256,512]{2,1,0:T(8,128)(2,1)}, bf16[2,256,512]{2,1,0:T(8,128)(2,1)}, u32[]{:S(2)}, u32[]{:S(2)}) collective-permute-start(bf16[2,256,512]{2,1,0:T(8,128)(2,1)} %pad_maximum_fusion.1.refs_3_), channel_id=1, source_target_pairs={{12,4},{14,6},{20,12},{22,14},{28,20},{30,22},{24,28},{26,30},{16,... | collective-permute-start | bytes 1572872 | tf_op jit(solution)/shard_map/ppermute | solution.py:501
  17.4 21.7 %collective-permute-start.3 = (bf16[2,256,512]{2,1,0:T(8,128)(2,1)}, bf16[2,256,512]{2,1,0:T(8,128)(2,1)S(1)}, u32[]{:S(2)}, u32[]{:S(2)}) collective-permute-start(bf16[2,256,512]{2,1,0:T(8,128)(2,1)} %collective-permute-done.1.refs_4_), channel_id=1, source_target_pairs={{4,12},{6,14},{12,20},{14,22},{20,28},{22,30},{28,24},{30,26},{24,... | collective-permute-start | bytes 1572872 | tf_op jit(solution)/shard_map/ppermute | solution.py:500
  20.2 22.8 %collective-permute-start.12 = (bf16[2,256,512]{2,1,0:T(8,128)(2,1)}, bf16[2,256,512]{2,1,0:T(8,128)(2,1)S(1)}, u32[]{:S(2)}, u32[]{:S(2)}) collective-permute-start(bf16[2,256,512]{2,1,0:T(8,128)(2,1)} %pad_maximum_fusion.1.refs_3_), channel_id=1, source_target_pairs={{4,12},{6,14},{12,20},{14,22},{20,28},{22,30},{28,24},{30,26},{24,... | collective-permute-start | bytes 1572872 | tf_op jit(solution)/shard_map/ppermute | solution.py:500
  30.0 15.3 %collective-permute-start.15 = (bf16[2,256,512]{2,1,0:T(8,128)(2,1)}, bf16[2,256,512]{2,1,0:T(8,128)(2,1)}, u32[]{:S(2)}, u32[]{:S(2)}) collective-permute-start(bf16[2,256,512]{2,1,0:T(8,128)(2,1)} %collective-permute-done.13.refs_5_), channel_id=1, source_target_pairs={{12,4},{14,6},{20,12},{22,14},{28,20},{30,22},{24,28},{26,30},{16,... | collective-permute-start | bytes 1572872 | tf_op jit(solution)/shard_map/ppermute | solution.py:501
  35.7 20.7 %collective-permute-start.4 = (bf16[2,256,512]{2,1,0:T(8,128)(2,1)}, bf16[2,256,512]{2,1,0:T(8,128)(2,1)}, u32[]{:S(2)}, u32[]{:S(2)}) collective-permute-start(bf16[2,256,512]{2,1,0:T(8,128)(2,1)} %collective-permute-done.2.refs_5_), channel_id=1, source_target_pairs={{12,4},{14,6},{20,12},{22,14},{28,20},{30,22},{24,28},{26,30},{16,... | collective-permute-start | bytes 1572872 | tf_op jit(solution)/shard_map/ppermute | solution.py:501
  37.5 31.5 %collective-permute-start.10 = (bf16[512,1024]{1,0:T(8,128)(2,1)}, bf16[512,1024]{1,0:T(8,128)(2,1)}, u32[]{:S(2)}, u32[]{:S(2)}) collective-permute-start(bf16[512,1024]{1,0:T(8,128)(2,1)} %get-tuple-element.40), channel_id=1, source_target_pairs={{0,1},{1,0},{2,3},{3,2},{4,5},{5,4},{6,7},{7,6},{8,9},{9,8},{10,11... | collective-permute-start | bytes 3145736 | tf_op jit(solution)/shard_map/ppermute | solution.py:47
  39.0 17.7 %collective-permute-start.5 = (bf16[2,256,512]{2,1,0:T(8,128)(2,1)S(1)}, bf16[2,256,512]{2,1,0:T(8,128)(2,1)}, u32[]{:S(2)}, u32[]{:S(2)}) collective-permute-start(bf16[2,256,512]{2,1,0:T(8,128)(2,1)S(1)} %collective-permute-done.3.refs_6_), channel_id=1, source_target_pairs={{4,12},{6,14},{12,20},{14,22},{20,28},{22,30},{28,24},{30,26},{24,... | collective-permute-start | bytes 1572872 | tf_op jit(solution)/shard_map/ppermute | solution.py:500
  43.0 22.5 %collective-permute-start.14 = (bf16[2,256,512]{2,1,0:T(8,128)(2,1)S(1)}, bf16[2,256,512]{2,1,0:T(8,128)(2,1)S(1)}, u32[]{:S(2)}, u32[]{:S(2)}) collective-permute-start(bf16[2,256,512]{2,1,0:T(8,128)(2,1)S(1)} %collective-permute-done.12.refs_4_), channel_id=1, source_target_pairs={{4,12},{6,14},{12,20},{14,22},{20,28},{22,30},{28,24},{30,26},{24,... | collective-permute-start | bytes 1572872 | tf_op jit(solution)/shard_map/ppermute | solution.py:500
  45.2 22.5 %collective-permute-start.17 = (bf16[2,256,512]{2,1,0:T(8,128)(2,1)}, bf16[2,256,512]{2,1,0:T(8,128)(2,1)S(1)}, u32[]{:S(2)}, u32[]{:S(2)}) collective-permute-start(bf16[2,256,512]{2,1,0:T(8,128)(2,1)} %collective-permute-done.15.refs_7_), channel_id=1, source_target_pairs={{12,4},{14,6},{20,12},{22,14},{28,20},{30,22},{24,28},{26,30},{16,... | collective-permute-start | bytes 1572872 | tf_op jit(solution)/shard_map/ppermute | solution.py:501
  56.4 22.4 %collective-permute-start.6 = (bf16[2,256,512]{2,1,0:T(8,128)(2,1)}, bf16[2,256,512]{2,1,0:T(8,128)(2,1)S(1)}, u32[]{:S(2)}, u32[]{:S(2)}) collective-permute-start(bf16[2,256,512]{2,1,0:T(8,128)(2,1)} %collective-permute-done.4.refs_7_), channel_id=1, source_target_pairs={{12,4},{14,6},{20,12},{22,14},{28,20},{30,22},{24,28},{26,30},{16,... | collective-permute-start | bytes 1572872 | tf_op jit(solution)/shard_map/ppermute | solution.py:501
  56.8 22.0 %collective-permute-start.7 = (bf16[2,256,512]{2,1,0:T(8,128)(2,1)}, bf16[2,256,512]{2,1,0:T(8,128)(2,1)S(1)}, u32[]{:S(2)}, u32[]{:S(2)}) collective-permute-start(bf16[2,256,512]{2,1,0:T(8,128)(2,1)} %collective-permute-done.5.refs_8_), channel_id=1, source_target_pairs={{4,12},{6,14},{12,20},{14,22},{20,28},{22,30},{28,24},{30,26},{24,... | collective-permute-start | bytes 1572872 | tf_op jit(solution)/shard_map/ppermute | solution.py:503
  65.5 26.6 %collective-permute-start.16 = (bf16[2,256,512]{2,1,0:T(8,128)(2,1)S(1)}, bf16[2,256,512]{2,1,0:T(8,128)(2,1)S(1)}, u32[]{:S(2)}, u32[]{:S(2)}) collective-permute-start(bf16[2,256,512]{2,1,0:T(8,128)(2,1)S(1)} %collective-permute-done.14.refs_6_), channel_id=1, source_target_pairs={{4,12},{6,14},{12,20},{14,22},{20,28},{22,30},{28,24},{30,26},{24,... | collective-permute-start | bytes 1572872 | tf_op jit(solution)/shard_map/ppermute | solution.py:500
  67.7 24.4 %collective-permute-start.18 = (bf16[2,256,512]{2,1,0:T(8,128)(2,1)S(1)}, bf16[2,256,512]{2,1,0:T(8,128)(2,1)}, u32[]{:S(2)}, u32[]{:S(2)}) collective-permute-start(bf16[2,256,512]{2,1,0:T(8,128)(2,1)S(1)} %collective-permute-done.17.refs_9_), channel_id=1, source_target_pairs={{12,4},{14,6},{20,12},{22,14},{28,20},{30,22},{24,28},{26,30},{16,... | collective-permute-start | bytes 1572872 | tf_op jit(solution)/shard_map/ppermute | solution.py:504
  69.0 48.6 %collective-permute-start.11 = (bf16[704,1024]{1,0:T(8,128)(2,1)}, bf16[704,1024]{1,0:T(8,128)(2,1)}, u32[]{:S(2)}, u32[]{:S(2)}) collective-permute-start(bf16[704,1024]{1,0:T(8,128)(2,1)} %get-tuple-element.42), channel_id=1, source_target_pairs={{0,1},{1,0},{2,3},{3,2},{4,5},{5,4},{6,7},{7,6},{8,9},{9,8},{10,11... | collective-permute-start | bytes 4325384 | tf_op jit(solution)/shard_map/ppermute | solution.py:47
  92.0 15.8 %collective-permute-start.8 = (f32[256,640]{1,0:T(8,128)}, f32[256,640]{1,0:T(8,128)}, u32[]{:S(2)}, u32[]{:S(2)}) collective-permute-start(f32[256,640]{1,0:T(8,128)} %get-tuple-element.38), channel_id=1, source_target_pairs={{0,2},{2,0},{4,6},{6,4},{8,10},{10,8},{12,14},{14,12},{16,18},{18,... | collective-permute-start | bytes 1966088 | tf_op jit(solution)/shard_map/ppermute | solution.py:51
  105.3 6.9 %collective-permute-start.19 = (f32[256,640]{1,0:T(8,128)}, f32[256,640]{1,0:T(8,128)}, u32[]{:S(2)}, u32[]{:S(2)}) collective-permute-start(f32[256,640]{1,0:T(8,128)} %get-tuple-element.45), channel_id=1, source_target_pairs={{0,2},{2,0},{4,6},{6,4},{8,10},{10,8},{12,14},{14,12},{16,18},{18,... | collective-permute-start | bytes 1966088 | tf_op jit(solution)/shard_map/ppermute | solution.py:51
  105.8 74.1 %collective-permute-start.28 = (bf16[1,704,2048]{2,1,0:T(8,128)(2,1)S(1)}, bf16[1,704,2048]{2,1,0:T(8,128)(2,1)}, u32[]{:S(2)}, u32[]{:S(2)}) collective-permute-start(bf16[1,704,2048]{2,1,0:T(8,128)(2,1)S(1)} %bitcast.52), channel_id=1, source_target_pairs={{0,2},{2,0},{4,6},{6,4},{8,10},{10,8},{12,14},{14,12},{16,18},{18,... | collective-permute-start | bytes 8650760 | tf_op jit(solution)/shard_map/ppermute | solution.py:51
  105.9 76.0 %collective-permute-start.29 = (bf16[1,704,2048]{2,1,0:T(8,128)(2,1)}, bf16[1,704,2048]{2,1,0:T(8,128)(2,1)}, u32[]{:S(2)}, u32[]{:S(2)}) collective-permute-start(bf16[1,704,2048]{2,1,0:T(8,128)(2,1)} %bitcast.53), channel_id=1, source_target_pairs={{0,2},{2,0},{4,6},{6,4},{8,10},{10,8},{12,14},{14,12},{16,18},{18,... | collective-permute-start | bytes 8650760 | tf_op jit(solution)/shard_map/ppermute | solution.py:51
  110.7 9.5 %collective-permute-start.20 = (bf16[256,512]{1,0:T(8,128)(2,1)}, bf16[256,512]{1,0:T(8,128)(2,1)}, u32[]{:S(2)}, u32[]{:S(2)}) collective-permute-start(bf16[256,512]{1,0:T(8,128)(2,1)} %merge.2.refs_0_), channel_id=1, source_target_pairs={{0,1},{1,0},{2,3},{3,2},{4,5},{5,4},{6,7},{7,6},{8,9},{9,8},{10,11... | collective-permute-start | bytes 786440 | tf_op jit(solution)/shard_map/ppermute | solution.py:47
  115.1 9.8 %collective-permute-start.21 = (bf16[256,512]{1,0:T(8,128)(2,1)}, bf16[256,512]{1,0:T(8,128)(2,1)}, u32[]{:S(2)}, u32[]{:S(2)}) collective-permute-start(bf16[256,512]{1,0:T(8,128)(2,1)} %merge.3.refs_1_), channel_id=1, source_target_pairs={{0,1},{1,0},{2,3},{3,2},{4,5},{5,4},{6,7},{7,6},{8,9},{9,8},{10,11... | collective-permute-start | bytes 786440 | tf_op jit(solution)/shard_map/ppermute | solution.py:47
  139.1 12.9 %collective-permute-start.23 = (bf16[272,1024]{1,0:T(8,128)(2,1)}, bf16[272,1024]{1,0:T(8,128)(2,1)}, u32[]{:S(2)}, u32[]{:S(2)}) collective-permute-start(bf16[272,1024]{1,0:T(8,128)(2,1)} %get-tuple-element.51.refs_0_), channel_id=1, source_target_pairs={{4,12},{6,14},{12,20},{14,22},{20,28},{22,30},{28,24},{30,26},{24,... | collective-permute-start | bytes 1671176 | tf_op jit(solution)/shard_map/ppermute | solution.py:556
  140.7 13.0 %collective-permute-start.25 = (bf16[272,1024]{1,0:T(8,128)(2,1)}, bf16[272,1024]{1,0:T(8,128)(2,1)}, u32[]{:S(2)}, u32[]{:S(2)}) collective-permute-start(bf16[272,1024]{1,0:T(8,128)(2,1)} %get-tuple-element.51.refs_0_), channel_id=1, source_target_pairs={{12,4},{14,6},{20,12},{22,14},{28,20},{30,22},{24,28},{26,30},{16,... | collective-permute-start | bytes 1671176 | tf_op jit(solution)/shard_map/ppermute | solution.py:559
  152.1 11.9 %collective-permute-start.24 = (bf16[272,1024]{1,0:T(8,128)(2,1)}, bf16[272,1024]{1,0:T(8,128)(2,1)S(1)}, u32[]{:S(2)}, u32[]{:S(2)}) collective-permute-start(bf16[272,1024]{1,0:T(8,128)(2,1)} %collective-permute-done.23.refs_1_), channel_id=1, source_target_pairs={{4,12},{6,14},{12,20},{14,22},{20,28},{22,30},{28,24},{30,26},{24,... | collective-permute-start | bytes 1671176 | tf_op jit(solution)/shard_map/ppermute | solution.py:556
  153.7 11.7 %collective-permute-start.26 = (bf16[272,1024]{1,0:T(8,128)(2,1)}, bf16[272,1024]{1,0:T(8,128)(2,1)}, u32[]{:S(2)}, u32[]{:S(2)}) collective-permute-start(bf16[272,1024]{1,0:T(8,128)(2,1)} %collective-permute-done.25.refs_2_), channel_id=1, source_target_pairs={{12,4},{14,6},{20,12},{22,14},{28,20},{30,22},{24,28},{26,30},{16,... | collective-permute-start | bytes 1671176 | tf_op jit(solution)/shard_map/ppermute | solution.py:559
  165.4 10.7 %collective-permute-start.35 = (bf16[272,1024]{1,0:T(8,128)(2,1)}, bf16[272,1024]{1,0:T(8,128)(2,1)S(1)}, u32[]{:S(2)}, u32[]{:S(2)}) collective-permute-start(bf16[272,1024]{1,0:T(8,128)(2,1)} %copy-done.10), channel_id=1, source_target_pairs={{4,12},{6,14},{12,20},{14,22},{20,28},{22,30},{28,24},{30,26},{24,... | collective-permute-start | bytes 1671176 | tf_op jit(solution)/shard_map/ppermute | solution.py:556
  167.0 10.5 %collective-permute-start.36 = (bf16[272,1024]{1,0:T(8,128)(2,1)}, bf16[272,1024]{1,0:T(8,128)(2,1)}, u32[]{:S(2)}, u32[]{:S(2)}) collective-permute-start(bf16[272,1024]{1,0:T(8,128)(2,1)} %collective-permute-done.26.refs_1_), channel_id=1, source_target_pairs={{12,4},{14,6},{20,12},{22,14},{28,20},{30,22},{24,28},{26,30},{16,... | collective-permute-start | bytes 1671176 | tf_op jit(solution)/shard_map/ppermute | solution.py:559
  167.4 16.1 %collective-permute-start.27 = (bf16[2,192,1024]{2,1,0:T(8,128)(2,1)}, bf16[2,192,1024]{2,1,0:T(8,128)(2,1)}, u32[]{:S(2)}, u32[]{:S(2)}) collective-permute-start(bf16[2,192,1024]{2,1,0:T(8,128)(2,1)} %select.52.refs_0_), channel_id=1, source_target_pairs={{0,1},{1,0},{2,3},{3,2},{4,5},{5,4},{6,7},{7,6},{8,9},{9,8},{10,11... | collective-permute-start | bytes 2359304 | tf_op jit(solution)/shard_map/ppermute | solution.py:47
  176.1 31.5 %collective-permute-start.31 = (bf16[704,1024]{1,0:T(8,128)(2,1)}, bf16[704,1024]{1,0:T(8,128)(2,1)}, u32[]{:S(2)}, u32[]{:S(2)}) collective-permute-start(bf16[704,1024]{1,0:T(8,128)(2,1)} %get-tuple-element.77.refs_2_), channel_id=1, source_target_pairs={{0,2},{2,0},{4,6},{6,4},{8,10},{10,8},{12,14},{14,12},{16,18},{18,... | collective-permute-start | bytes 4325384 | tf_op jit(solution)/shard_map/ppermute | solution.py:51
  177.5 31.3 %collective-permute-start.32 = (bf16[704,1024]{1,0:T(8,128)(2,1)}, bf16[704,1024]{1,0:T(8,128)(2,1)}, u32[]{:S(2)}, u32[]{:S(2)}) collective-permute-start(bf16[704,1024]{1,0:T(8,128)(2,1)} %collective-permute-done.11.refs_3_), channel_id=1, source_target_pairs={{0,2},{2,0},{4,6},{6,4},{8,10},{10,8},{12,14},{14,12},{16,18},{18,... | collective-permute-start | bytes 4325384 | tf_op jit(solution)/shard_map/ppermute | solution.py:51
  179.9 15.1 %collective-permute-start.37 = (bf16[2,128,1024]{2,1,0:T(8,128)(2,1)}, bf16[2,128,1024]{2,1,0:T(8,128)(2,1)S(1)}, u32[]{:S(2)}, u32[]{:S(2)}) collective-permute-start(bf16[2,128,1024]{2,1,0:T(8,128)(2,1)} %select.53.refs_0_), channel_id=1, source_target_pairs={{0,1},{1,0},{2,3},{3,2},{4,5},{5,4},{6,7},{7,6},{8,9},{9,8},{10,11... | collective-permute-start | bytes 1572872 | tf_op jit(solution)/shard_map/ppermute | solution.py:47
  181.9 22.8 %collective-permute-start.45 = (bf16[272,1024]{1,0:T(8,128)(2,1)S(1)}, bf16[272,1024]{1,0:T(8,128)(2,1)S(1)}, u32[]{:S(2)}, u32[]{:S(2)}) collective-permute-start(bf16[272,1024]{1,0:T(8,128)(2,1)S(1)} %collective-permute-done.35.refs_0_), channel_id=1, source_target_pairs={{4,12},{6,14},{12,20},{14,22},{20,28},{22,30},{28,24},{30,26},{24,... | collective-permute-start | bytes 1671176 | tf_op jit(solution)/shard_map/ppermute | solution.py:556
  192.1 16.8 %collective-permute-start.30 = (bf16[2,192,704]{2,1,0:T(8,128)(2,1)}, bf16[2,192,704]{2,1,0:T(8,128)(2,1)S(1)}, u32[]{:S(2)}, u32[]{:S(2)}) collective-permute-start(bf16[2,192,704]{2,1,0:T(8,128)(2,1)} %expert_in.4.refs_0_), channel_id=1, source_target_pairs={{0,1},{1,0},{2,3},{3,2},{4,5},{5,4},{6,7},{7,6},{8,9},{9,8},{10,11... | collective-permute-start | bytes 1622024 | tf_op jit(solution)/shard_map/ppermute | solution.py:47
  195.0 24.7 %collective-permute-start.41 = (bf16[2,128,1024]{2,1,0:T(8,128)(2,1)}, bf16[2,128,1024]{2,1,0:T(8,128)(2,1)S(1)}, u32[]{:S(2)}, u32[]{:S(2)}) collective-permute-start(bf16[2,128,1024]{2,1,0:T(8,128)(2,1)} %select.54.refs_0_), channel_id=1, source_target_pairs={{0,1},{1,0},{2,3},{3,2},{4,5},{5,4},{6,7},{7,6},{8,9},{9,8},{10,11... | collective-permute-start | bytes 1572872 | tf_op jit(solution)/shard_map/ppermute | solution.py:47
  204.7 27.2 %collective-permute-start.38 = (bf16[2,128,704]{2,1,0:T(8,128)(2,1)}, bf16[2,128,704]{2,1,0:T(8,128)(2,1)S(1)}, u32[]{:S(2)}, u32[]{:S(2)}) collective-permute-start(bf16[2,128,704]{2,1,0:T(8,128)(2,1)} %expert_in.5.refs_0_), channel_id=1, source_target_pairs={{0,1},{1,0},{2,3},{3,2},{4,5},{5,4},{6,7},{7,6},{8,9},{9,8},{10,11... | collective-permute-start | bytes 1081352 | tf_op jit(solution)/shard_map/ppermute | solution.py:47
  207.7 29.2 %collective-permute-start.46 = (bf16[2,64,1024]{2,1,0:T(8,128)(2,1)}, bf16[2,64,1024]{2,1,0:T(8,128)(2,1)S(1)}, u32[]{:S(2)}, u32[]{:S(2)}) collective-permute-start(bf16[2,64,1024]{2,1,0:T(8,128)(2,1)} %select.55.refs_0_), channel_id=1, source_target_pairs={{0,1},{1,0},{2,3},{3,2},{4,5},{5,4},{6,7},{7,6},{8,9},{9,8},{10,11... | collective-permute-start | bytes 786440 | tf_op jit(solution)/shard_map/ppermute | solution.py:47
  229.0 19.5 %collective-permute-start.42 = (bf16[2,128,704]{2,1,0:T(8,128)(2,1)}, bf16[2,128,704]{2,1,0:T(8,128)(2,1)S(1)}, u32[]{:S(2)}, u32[]{:S(2)}) collective-permute-start(bf16[2,128,704]{2,1,0:T(8,128)(2,1)} %expert_in.6.refs_0_), channel_id=1, source_target_pairs={{0,1},{1,0},{2,3},{3,2},{4,5},{5,4},{6,7},{7,6},{8,9},{9,8},{10,11... | collective-permute-start | bytes 1081352 | tf_op jit(solution)/shard_map/ppermute | solution.py:47
  229.8 25.1 %collective-permute-start.33 = (bf16[2,64,1024]{2,1,0:T(8,128)(2,1)S(1)}, bf16[2,64,1024]{2,1,0:T(8,128)(2,1)S(1)}, u32[]{:S(2)}, u32[]{:S(2)}) collective-permute-start(bf16[2,64,1024]{2,1,0:T(8,128)(2,1)S(1)} %copy-done.43), channel_id=1, source_target_pairs={{4,0},{6,2},{12,4},{14,6},{20,12},{22,14},{28,20},{30,22},{24,28},... | collective-permute-start | bytes 786440 | tf_op jit(solution)/shard_map/ppermute | solution.py:586
  230.3 32.9 %collective-permute-start.34 = (bf16[2,64,1024]{2,1,0:T(8,128)(2,1)S(1)}, bf16[2,64,1024]{2,1,0:T(8,128)(2,1)S(1)}, u32[]{:S(2)}, u32[]{:S(2)}) collective-permute-start(bf16[2,64,1024]{2,1,0:T(8,128)(2,1)S(1)} %copy-done.40), channel_id=1, source_target_pairs={{4,12},{6,14},{12,20},{14,22},{20,28},{22,30},{28,24},{30,26},{24,... | collective-permute-start | bytes 786440 | tf_op jit(solution)/shard_map/ppermute | solution.py:586
  245.6 11.5 %collective-permute-start.47 = (bf16[2,64,704]{2,1,0:T(8,128)(2,1)}, bf16[2,64,704]{2,1,0:T(8,128)(2,1)S(1)}, u32[]{:S(2)}, u32[]{:S(2)}) collective-permute-start(bf16[2,64,704]{2,1,0:T(8,128)(2,1)} %expert_in.7.refs_0_), channel_id=1, source_target_pairs={{0,1},{1,0},{2,3},{3,2},{4,5},{5,4},{6,7},{7,6},{8,9},{9,8},{10,11... | collective-permute-start | bytes 540680 | tf_op jit(solution)/shard_map/ppermute | solution.py:47
  247.7 19.3 %collective-permute-start.39 = (bf16[2,64,1024]{2,1,0:T(8,128)(2,1)S(1)}, bf16[2,64,1024]{2,1,0:T(8,128)(2,1)S(1)}, u32[]{:S(2)}, u32[]{:S(2)}) collective-permute-start(bf16[2,64,1024]{2,1,0:T(8,128)(2,1)S(1)} %copy-done.42), channel_id=1, source_target_pairs={{4,8},{6,10},{12,0},{14,2},{20,4},{22,6},{28,12},{30,14},{24,20},{... | collective-permute-start | bytes 786440 | tf_op jit(solution)/shard_map/ppermute | solution.py:586
  248.5 29.3 %collective-permute-start.40 = (bf16[2,64,1024]{2,1,0:T(8,128)(2,1)S(1)}, bf16[2,64,1024]{2,1,0:T(8,128)(2,1)S(1)}, u32[]{:S(2)}, u32[]{:S(2)}) collective-permute-start(bf16[2,64,1024]{2,1,0:T(8,128)(2,1)S(1)} %copy-done.41), channel_id=1, source_target_pairs={{4,20},{6,22},{12,28},{14,30},{20,24},{22,26},{28,16},{30,18},{24,... | collective-permute-start | bytes 786440 | tf_op jit(solution)/shard_map/ppermute | solution.py:586
  255.0 29.1 %collective-permute-start.43 = (bf16[2,64,1024]{2,1,0:T(8,128)(2,1)}, bf16[2,64,1024]{2,1,0:T(8,128)(2,1)S(1)}, u32[]{:S(2)}, u32[]{:S(2)}) collective-permute-start(bf16[2,64,1024]{2,1,0:T(8,128)(2,1)} %get-tuple-element.64), channel_id=1, source_target_pairs={{4,16},{6,18},{12,8},{14,10},{20,0},{22,2},{28,4},{30,6},{24,12},{... | collective-permute-start | bytes 786440 | tf_op jit(solution)/shard_map/ppermute | solution.py:586
  257.1 26.9 %collective-permute-start.44 = (bf16[2,64,1024]{2,1,0:T(8,128)(2,1)}, bf16[2,64,1024]{2,1,0:T(8,128)(2,1)S(1)}, u32[]{:S(2)}, u32[]{:S(2)}) collective-permute-start(bf16[2,64,1024]{2,1,0:T(8,128)(2,1)} %get-tuple-element.65), channel_id=1, source_target_pairs={{4,28},{6,30},{12,24},{14,26},{20,16},{22,18},{28,8},{30,10},{24,0... | collective-permute-start | bytes 786440 | tf_op jit(solution)/shard_map/ppermute | solution.py:586
  263.2 26.4 %collective-permute-start.48 = (bf16[2,64,1024]{2,1,0:T(8,128)(2,1)}, bf16[2,64,1024]{2,1,0:T(8,128)(2,1)S(1)}, u32[]{:S(2)}, u32[]{:S(2)}) collective-permute-start(bf16[2,64,1024]{2,1,0:T(8,128)(2,1)} %expert_out.7), channel_id=1, source_target_pairs={{4,24},{6,26},{12,16},{14,18},{20,8},{22,10},{28,0},{30,2},{24,4},... | collective-permute-start | bytes 786440 | tf_op jit(solution)/shard_map/ppermute | solution.py:586
  (46 other events, 461.8 us)

commit v3 on v2

--- a/solution.py
+++ b/solution.py
@@ -14,7 +14,6 @@
 BAND = 2
 TOP = 2
 HEAD_DIM = 128
-FIRST_HEADS = 4
 EXPERT_GROUPS = (3, 5, 7, 8)
 TAG_ROWS = 16
 LANES = 128
@@ -51,16 +50,43 @@
     return lax.ppermute(x, "track", [(i, i ^ 1) for i in range(tracks)])
 
 
-def attention_kernel(blocks, heads, causal, carried, *refs):
+def halves_kernel(count, which_ref, *refs):
+    for i in range(2):
+        for j in range(count):
+            refs[2 * count + i][j] = refs[i * count + j][0]
+
+
+def halves(core, *arrays):
+    _, events, width = arrays[0].shape
+    count = len(arrays)
+    block = (1, events, width // 2)
+    shape = jax.ShapeDtypeStruct((count, events, width // 2), BF16)
+    return pl.pallas_call(
+        functools.partial(halves_kernel, count),
+        grid_spec=pltpu.PrefetchScalarGridSpec(
+            num_scalar_prefetch=1,
+            grid=(1,),
+            in_specs=[pl.BlockSpec(block, lambda g, m: (0, 0, m[0]))] * count
+            + [pl.BlockSpec(block, lambda g, m: (0, 0, m[1]))] * count,
+            out_specs=[pl.BlockSpec(shape.shape, lambda g, m: (0, 0, 0))] * 2,
+        ),
+        out_shape=[shape, shape],
+        compiler_params=pltpu.CompilerParams(vmem_limit_bytes=16 << 20),
+        cost_estimate=pl.CostEstimate(
+            flops=0, bytes_accessed=4 * count * events * width, transcendentals=0
+        ),
+        name="halves",
+    )(jnp.stack([core, 1 - core]), *arrays, *arrays)
+
+
+def attention_kernel(blocks, *refs):
     q_ref, qbar_ref, kbar_ref = refs[:3]
     kv_refs = refs[3 : 3 + blocks]
-    earlier = refs[3 + blocks : 3 + blocks + 2 * carried]
-    *out_refs, cap_ref, score_ref = refs[3 + blocks + 2 * carried :]
-    head = pl.program_id(0)
+    *out_refs, cap_ref, score_ref = refs[3 + blocks :]
     events = q_ref.shape[1]
     exponent_scale = math.log2(math.e) / math.sqrt(HEAD_DIM)
 
-    @pl.when(head == 0)
+    @pl.when(pl.program_id(0) == 0)
     def _():
         row = lax.broadcasted_iota(jnp.int32, (events, events), 0)
         column = lax.broadcasted_iota(jnp.int32, (events, events), 1)
@@ -68,106 +94,63 @@
             for b in range(blocks):
                 back = qbar_ref[side, :, b : b + 1] - kbar_ref[b : b + 1, :]
                 allowed = (back >= 0) & (back <= BAND)
-                if causal and side == 0 and b == 0:
+                if side == b:
                     allowed = allowed & (column <= row)
-                cap_ref[b, side] = jnp.where(allowed, NO_CAP, MASKED_SCORE)
-
-    lane = lax.broadcasted_iota(jnp.int32, (events, LANES), 1)
-    columns = pl.ds(pl.multiple_of(head * HEAD_DIM, HEAD_DIM), HEAD_DIM)
+                cap_ref[b, side] = jnp.where(allowed, NO_CAP, MASKED_SCORE).astype(cap_ref.dtype)
+
     for side, out_ref in enumerate(out_refs):
         query = q_ref[side]
         peaks = None
         for b in range(blocks):
-            scores = jnp.minimum(dot_nt(query, kv_refs[b][0]), cap_ref[b, side])
+            scores = jnp.minimum(dot_nt(query, kv_refs[b][0]), cap_ref[b, side].astype(F32))
             score_ref[b] = scores
             for start in range(0, events, LANES):
                 part = scores[:, start : start + LANES]
                 peaks = part if peaks is None else jnp.maximum(peaks, part)
         peak = peaks.max(axis=1, keepdims=True)
         value = jnp.zeros((events, HEAD_DIM), F32)
-        mass = jnp.zeros((events, 1), F32)
-        if carried:
-            stat = earlier[side][:, heads * HEAD_DIM :]
-            old_peak = jnp.sum(jnp.where(lane == head, stat, 0.0), axis=1, keepdims=True)
-            mass = jnp.sum(jnp.where(lane == heads + head, stat, 0.0), axis=1, keepdims=True)
-            peak = jnp.maximum(peak, old_peak)
-            shrink = jnp.exp2((old_peak - peak) * exponent_scale)
-            mass = mass * shrink
-            value = earlier[side][:, columns] * shrink
         masses = jnp.zeros((events, LANES), F32)
         for b in range(blocks):
             weights = jnp.exp2((score_ref[b] - peak) * exponent_scale)
             for start in range(0, events, LANES):
                 masses = masses + weights[:, start : start + LANES]
             value = value + dot(weights.astype(BF16), kv_refs[b][1])
-        mass = mass + masses.sum(axis=1, keepdims=True)
-        out_ref[:, columns] = value
-        stat = jnp.where(lane == head, peak, jnp.where(lane == heads + head, mass, 0.0))
-
-        @pl.when(head == 0)
-        def _():
-            out_ref[:, heads * HEAD_DIM :] = stat
-
-        @pl.when(head != 0)
-        def _():
-            out_ref[:, heads * HEAD_DIM :] += stat
-
-
-def attention(q, qbar, kbar, kvs, causal, earlier=()):
-    blocks, events, width = len(kvs), q.shape[1], q.shape[2]
-    heads = width // HEAD_DIM
-    shape = jax.ShapeDtypeStruct((events, width + LANES), F32)
-    flops = 4 * 2 * events * blocks * events * width
-    return pl.pallas_call(
-        functools.partial(attention_kernel, blocks, heads, causal, bool(earlier)),
+        out_ref[...] = (value / masses.sum(axis=1, keepdims=True)).astype(BF16)
+
+
+def attention(q, qbar, kbar, kvs, first, heads):
+    blocks, events = len(kvs), q.shape[1]
+    shape = jax.ShapeDtypeStruct((events, heads * HEAD_DIM), BF16)
+    flops = 4 * 2 * events * blocks * events * heads * HEAD_DIM
+    part = pl.BlockSpec((2, events, HEAD_DIM), lambda h: (0, 0, first + h))
+    return pl.pallas_call(
+        functools.partial(attention_kernel, blocks),
         grid=(heads,),
         in_specs=[
-            pl.BlockSpec((2, events, HEAD_DIM), lambda h: (0, 0, h)),
+            part,
             pl.BlockSpec(qbar.shape, lambda h: (0, 0, 0)),
             pl.BlockSpec(kbar.shape, lambda h: (0, 0)),
         ]
-        + [pl.BlockSpec((2, events, HEAD_DIM), lambda h: (0, 0, h))] * blocks
-        + [pl.BlockSpec(shape.shape, lambda h: (0, 0))] * len(earlier),
-        out_specs=[pl.BlockSpec(shape.shape, lambda h: (0, 0))] * 2,
+        + [part] * blocks,
+        out_specs=[pl.BlockSpec((events, HEAD_DIM), lambda h: (0, h))] * 2,
         out_shape=[shape, shape],
         scratch_shapes=[
-            pltpu.VMEM((blocks, 2, events, events), F32),
+            pltpu.VMEM((blocks, 2, events, events), F32 if blocks <= 16 else BF16),
             pltpu.VMEM((blocks, events, events), F32),
         ],
         cost_estimate=pl.CostEstimate(
-            flops=flops, bytes_accessed=blocks * events * width * 4, transcendentals=flops // 512
+            flops=flops,
+            bytes_accessed=4 * blocks * events * heads * HEAD_DIM,
+            transcendentals=flops // 512,
+        ),
+        compiler_params=pltpu.CompilerParams(
+            vmem_limit_bytes=(28 if blocks <= 16 else 60) << 20
         ),
         name="attention",
-    )(q, qbar, kbar, *kvs, *earlier)
-
-
-def merge_kernel(heads, a_ref, b_ref, out_ref):
-    scale = 1.0 / math.sqrt(HEAD_DIM)
-    for head in range(heads):
-        at = heads * HEAD_DIM + head
-        peak_a, mass_a = a_ref[:, at : at + 1], a_ref[:, at + heads : at + heads + 1]
-        peak_b, mass_b = b_ref[:, at : at + 1], b_ref[:, at + heads : at + heads + 1]
-        peak = jnp.maximum(peak_a, peak_b)
-        scale_a = jnp.exp((peak_a - peak) * scale)
-        scale_b = jnp.exp((peak_b - peak) * scale)
-        part = slice(head * HEAD_DIM, (head + 1) * HEAD_DIM)
-        total = scale_a * a_ref[:, part] + scale_b * b_ref[:, part]
-        out_ref[:, part] = (total / (scale_a * mass_a + scale_b * mass_b)).astype(BF16)
-
-
-def merge(a, b):
-    events, width = a.shape[0], a.shape[1] - LANES
-    return pl.pallas_call(
-        functools.partial(merge_kernel, width // HEAD_DIM),
-        out_shape=jax.ShapeDtypeStruct((events, width), BF16),
-        cost_estimate=pl.CostEstimate(
-            flops=8 * events * width, bytes_accessed=10 * events * width, transcendentals=0
-        ),
-        name="merge",
-    )(a, b)
-
-
-def project_kernel(count, experts, *refs):
+    )(q, qbar, kbar, *kvs)
+
+
+def project_kernel(count, experts, place_ref, *refs):
     attended, weights = refs[:count], refs[count : 2 * count]
     residual_ref, gain_ref, router_ref, hidden_ref, stat_ref = refs[2 * count :]
     step = pl.program_id(0)
@@ -191,23 +174,29 @@
         stat_ref[...] += stat
 
 
-def project(attended, weights, residual, gain, router, experts):
+def project(attended, weights, places, residual, gain, router, experts):
     events, width = residual.shape
     tile = 256
     return pl.pallas_call(
         functools.partial(project_kernel, len(attended), experts),
-        grid=(width // tile,),
-        in_specs=[pl.BlockSpec(part.shape, lambda j: (0, 0)) for part in attended]
-        + [pl.BlockSpec((w.shape[0], tile), lambda j: (0, j)) for w in weights]
-        + [
-            pl.BlockSpec((events, tile), lambda j: (0, j)),
-            pl.BlockSpec((1, tile), lambda j: (0, j)),
-            pl.BlockSpec((tile, LANES), lambda j: (j, 0)),
-        ],
-        out_specs=[
-            pl.BlockSpec((events, tile), lambda j: (0, j)),
-            pl.BlockSpec((events, LANES), lambda j: (0, 0)),
-        ],
+        grid_spec=pltpu.PrefetchScalarGridSpec(
+            num_scalar_prefetch=1,
+            grid=(width // tile,),
+            in_specs=[pl.BlockSpec(part.shape, lambda j, m: (0, 0)) for part in attended]
+            + [
+                pl.BlockSpec((part.shape[1], tile), lambda j, m, i=i: (m[i], j))
+                for i, part in enumerate(attended)
+            ]
+            + [
+                pl.BlockSpec((events, tile), lambda j, m: (0, j)),
+                pl.BlockSpec((1, tile), lambda j, m: (0, j)),
+                pl.BlockSpec((tile, LANES), lambda j, m: (j, 0)),
+            ],
+            out_specs=[
+                pl.BlockSpec((events, tile), lambda j, m: (0, j)),
+                pl.BlockSpec((events, LANES), lambda j, m: (0, 0)),
+            ],
+        ),
         out_shape=[
             jax.ShapeDtypeStruct((events, width), BF16),
             jax.ShapeDtypeStruct((events, LANES), F32),
@@ -215,8 +204,9 @@
         cost_estimate=pl.CostEstimate(
             flops=2 * events * D * width, bytes_accessed=2 * D * width, transcendentals=0
         ),
+        compiler_params=pltpu.CompilerParams(vmem_limit_bytes=24 << 20),
         name="project",
-    )(*attended, *weights, residual, gain, router)
+    )(places, *attended, *weights, residual, gain, router)
 
 
 def pack_kernel(sources, experts, *refs):
@@ -256,6 +246,7 @@
         cost_estimate=pl.CostEstimate(
             flops=8 * events * width, bytes_accessed=4 * events * width, transcendentals=0
         ),
+        compiler_params=pltpu.CompilerParams(vmem_limit_bytes=16 << 20),
         name="pack",
     )(hidden, *stats, gain, route, tags)
 
@@ -289,6 +280,7 @@
             bytes_accessed=2 * count * width * (blocks[0].shape[0] + 2 * slots),
             transcendentals=0,
         ),
+        compiler_params=pltpu.CompilerParams(vmem_limit_bytes=16 << 20),
         name="select",
     )(experts, *blocks)
 
@@ -349,6 +341,7 @@
             bytes_accessed=8 * D * units,
             transcendentals=2 * count * units,
         ),
+        compiler_params=pltpu.CompilerParams(vmem_limit_bytes=24 << 20),
         name="expert_in",
     )(kmap, *rows, *weights)
 
@@ -384,6 +377,7 @@
             bytes_accessed=4 * sources * units * width,
             transcendentals=0,
         ),
+        compiler_params=pltpu.CompilerParams(vmem_limit_bytes=16 << 20),
         name="expert_out",
     )(*acts, *weights[0], *weights[1])
 
@@ -416,6 +410,7 @@
             bytes_accessed=4 * count * slots * width,
             transcendentals=0,
         ),
+        compiler_params=pltpu.CompilerParams(vmem_limit_bytes=16 << 20),
         name="combine",
     )(base, gates, codes, *returned)
 
@@ -460,7 +455,8 @@
         place[chip] = i
     my_place = jnp.array(place, jnp.int32)[my_track // 2]
     block_chip = jnp.array(order, jnp.int32)[(my_place + jnp.array(hops, jnp.int32)) % chips]
-    block_track = block_chip * 2 + my_track % 2
+    core = my_track % 2
+    block_track = jnp.stack([block_chip * 2 + core, block_chip * 2 + 1 - core], 1).reshape(-1)
     key_bars = bar_index[block_track]
     query_track = jnp.stack([my_track, my_track ^ 1])
     query_bars = bar_index[query_track]
@@ -473,20 +469,14 @@
     def columns_of(weight, owner):
         return lax.dynamic_slice_in_dim(weight, owner * width, width, 1)
 
-    all_heads = width // HEAD_DIM
-    cut = all_heads * FIRST_HEADS // 8 * HEAD_DIM
-    parts = [slice(0, cut), slice(cut, width)]
-    got = [
-        [jnp.concatenate([key_vectors[:, :, part], values[:, :, part]], axis=0)] for part in parts
-    ]
-    both_queries = jnp.concatenate([queries, swap_cores(queries, tracks)], axis=0)
-    chunk_queries = [both_queries[:, :, part] for part in parts]
+    own_half, other_half = halves(core, key_vectors, values)
+    streams = [[own_half], [swap_cores(other_half, tracks)]]
+    own_queries, other_queries = halves(core, queries)
+    both_queries = jnp.concatenate([own_queries, swap_cores(other_queries, tracks)], axis=0)
     fetched = []
     for s in shifts:
         owner = (my_head + s) % head_parts
-        out_part = columns_of(out_proj, owner)
-        down_part = columns_of(w_down[0], owner)
-        for part in (out_part[:cut], out_part[cut:], down_part):
+        for part in (columns_of(out_proj, owner), columns_of(w_down[0], owner)):
             if fetched:
                 part, fetched[-1] = barrier((part, fetched[-1]))
             fetched.append(shifted(part, "head", head_parts, s))
@@ -494,38 +484,54 @@
     in_weights += [swap_cores(w, tracks) for w in in_weights]
 
     steps = chips // 2
-    ahead, back = [g[0] for g in got], [g[0] for g in got]
+    ahead, back = [g[0] for g in streams], [g[0] for g in streams]
     for _ in range(1, steps):
         for i in range(2):
             ahead[i] = lax.ppermute(ahead[i], "track", forward)
             back[i] = lax.ppermute(back[i], "track", backward)
-            got[i] += [ahead[i], back[i]]
-    got[0].append(lax.ppermute(ahead[0], "track", forward))
-    got[1].append(lax.ppermute(back[1], "track", backward))
-
-    attended = [[] for _ in range(head_parts)]
-    for i in range(2):
-        mine, theirs = attention(chunk_queries[i], query_bars, key_bars, got[i], True)
-        merged = merge(mine, swap_cores(theirs, tracks))
-        attended[0].append(merged)
+            streams[i] += [ahead[i], back[i]]
+    streams[0].append(lax.ppermute(ahead[0], "track", forward))
+    streams[1].append(lax.ppermute(back[1], "track", backward))
+    kvs = [block for pair in zip(*streams, strict=True) for block in pair]
+
+    local_heads = width // HEAD_DIM // 2
+    cuts = [0, local_heads - local_heads // 2, local_heads]
+    attended, weight_of, places = [], [], []
+    for first, end in zip(cuts[:-1], cuts[1:], strict=True):
+        mine, theirs = attention(both_queries, query_bars, key_bars, kvs, first, end - first)
+        pieces = [(0, 0, mine), (0, 1, swap_cores(theirs, tracks))]
         for s in shifts:
-            attended[s].append(shifted(merged, "head", head_parts, s))
-    attended[0][0], fetched = barrier((attended[0][0], fetched))
-
-    own_out = columns_of(out_proj, my_head)
-    out_weights = [own_out[:cut], own_out[cut:]]
+            pieces.append((s, 0, shifted(mine, "head", head_parts, s)))
+            pairs = [
+                (t * head_parts + h, (t ^ 1) * head_parts + (h + s) % head_parts)
+                for t in range(tracks)
+                for h in range(head_parts)
+            ]
+            pieces.append((s, 1, lax.ppermute(theirs, ("track", "head"), pairs)))
+        for s, other, piece in pieces:
+            attended.append(piece)
+            weight_of.append(s)
+            half = 1 - core if other else core
+            places.append(half * (local_heads // (end - first)) + first // (end - first))
+    attended[0], fetched = barrier((attended[0], fetched))
+    out_weights = [columns_of(out_proj, my_head)] + fetched[::2]
     down_weights = [columns_of(w_down[0], my_head)]
     for s in shifts:
-        top, bottom, down = fetched[3 * s - 3 : 3 * s]
-        out_weights += [top, bottom]
-        down_weights.append(down)
+        down_weights.append(fetched[2 * s - 1])
     down_weights = [down_weights, [swap_cores(w, tracks) for w in down_weights]]
 
     experts = tracks
     wide_router = jnp.pad(router, ((0, 0), (0, LANES - experts)))
     gain = norm_gain.reshape(1, width)
-    attended = [part for source in attended for part in source]
-    hidden, stat = project(attended, out_weights, residual_in[0], gain, wide_router, experts)
+    hidden, stat = project(
+        attended,
+        [out_weights[s] for s in weight_of],
+        jnp.stack(places),
+        residual_in[0],
+        gain,
+        wide_router,
+        experts,
+    )
     stats = [stat] + [shifted(stat, "head", head_parts, s) for s in shifts]
 
     slots = 2 * events * TOP // experts
@@ -545,6 +551,10 @@
     codes = (hop_of_route * 2 + other_core) * slots + rank
     my_experts = jnp.stack([my_track, my_track ^ 1])
 
+    in_weights = [pltpu.with_memory_space_constraint(w, pltpu.VMEM) for w in in_weights]
+    down_weights = [
+        [pltpu.with_memory_space_constraint(w, pltpu.VMEM) for w in ws] for ws in down_weights
+    ]
     block, gates = pack(hidden, stats, gain, route, tags, experts)
     ends = [chips * share // 8 for share in EXPERT_GROUPS]
     blocks, forth, back = [block], block, block

time: 294 us -> 284 us (0.966)
  Pallas kernels: 106 us -> 76.9 us
  waiting for transfers between devices: 97.3 us -> 124 us
  starting transfers between devices: 56.3 us -> 52 us
  other arithmetic: 6.41 us -> 2.82 us
    ppermute x6, waiting for transfers between devices: 5.66 us -> 16.7 us  [local(): ahead[i] = lax.ppermute(ahead[i], 'track', forward)]
    ppermute x2 -> x4, waiting for transfers between devices: 0.01 us -> 9.61 us  [the longest x1 8.71 us: local(): streams[0].append(lax.ppermute(ahead[0], 'track', forward))]
    pallas_call x4, Pallas kernels: 30.3 us -> 23.6 us  [the longest x2 21.3 us: attention(): pl.pallas_call(functools.partial(attention_kernel, blocks), grid=(heads,)...]
    slice x4 -> x1, local copies, waits for them, and re-layouts: 6.97 us -> 0.21 us  [the longest x1 4.42 us: local(): out_weights = [own_out[:cut], own_out[cut:]]]
    pallas_call x4, Pallas kernels: 33.3 us -> 27 us  [expert_in(): pl.pallas_call(functools.partial(expert_in_kernel, sources, per_source),...]
    pallas_call x4, Pallas kernels: 9.4 us -> 3.38 us  [select(): pl.pallas_call(functools.partial(select_kernel, count, slots), in_specs=[...]
    dynamic_slice x1 -> x2, local copies, waits for them, and re-layouts: 1.89 us -> 7.72 us  [columns_of(): return lax.dynamic_slice_in_dim(weight, owner * width, width, 1)]
    ppermute x14 -> x13, waiting for transfers between devices: 20.6 us -> 25.8 us  [shifted(): return lax.ppermute(x, axis, [(i, (i + shift) % size) for i in range(size)])]
  transfers between devices with their start and end apart: 49 -> 51, of which waited for: 19 -> 25; matrix products, arithmetic and copies ran while one was open for 8% -> 6% of each run, Pallas kernels for 35% -> 27%
where the time goes in v3:
time: 284 us
  waiting for transfers between devices  124 us (44%)
  Pallas kernels  76.9 us (27%)
  starting transfers between devices  52 us (18%)
  local copies, waits for them, and re-layouts  26.9 us (9%)
    ppermute x4, waiting for transfers between devices, local(): forth = lax.ppermute(forth, 'track', forward)  29.9 us
    pallas_call x4, Pallas kernels, expert_in(): pl.pallas_call(functools.partial(expert_in_kernel, sources, per_source),...  27 us
    ppermute x13, waiting for transfers between devices, shifted(): return lax.ppermute(x, axis, [(i, (i + shift) % size) for i in range(size)])  25.8 us
    ppermute x6, waiting for transfers between devices, local(): back[i] = lax.ppermute(back[i], 'track', backward)  24.4 us
    pallas_call x2, Pallas kernels, attention(): pl.pallas_call(functools.partial(attention_kernel, blocks), grid=(heads,)...  21.3 us
    ppermute x6, waiting for transfers between devices, local(): ahead[i] = lax.ppermute(ahead[i], 'track', forward)  16.7 us
    ppermute x13, starting transfers between devices, shifted(): return lax.ppermute(x, axis, [(i, (i + shift) % size) for i in range(size)])  13.8 us
    ppermute x7, waiting for transfers between devices, local(): returned.append(lax.ppermute(out, 'track', pairs) if hop_length else out)  12.5 us
  transfers between devices with their start and end apart: 51, of which 25 were waited for; matrix products, arithmetic and copies ran while one was open for 6% of the time, Pallas kernels for 27%

profile of v3, /device:TPU:0, one launch (start us, length us, event | category | flops | bytes accessed | tf_op | source)
XLA Modules:
  0.0 283.5 jit_solution(1563311095274619913)
XLA Ops:
  0.0 4.1 %constant_dynamic-slice_fusion = (bf16[1024,1024]{1,0:T(8,128)(2,1)S(1)}, bf16[1024,1024]{1,0:T(8,128)(2,1)}) fusion(bf16[1024,2048]{1,0:T(8,128)(2,1)} %param.24, s32[]{:T(128)S(6)} %select_n.136, s32[]{:T(128)S(6)} %select_n.135), kind=kLoop, calls=%fused_computation.58 | loop fusion | bytes 8388616 | tf_op jit(solution)/shard_map/dynamic_slice | solution.py:470
  4.1 3.0 %collective-permute-start.16 = (bf16[1024,1024]{1,0:T(8,128)(2,1)}, bf16[1024,1024]{1,0:T(8,128)(2,1)}, u32[]{:S(2)}, u32[]{:S(2)}) collective-permute-start(bf16[1024,1024]{1,0:T(8,128)(2,1)} %get-tuple-element.74), channel_id=1, source_target_pairs={{0,1},{1,0},{2,3},{3,2},{4,5},{5,4},{6,7},{7,6},{8,9},{9,8},{10,11... | collective-permute-start | bytes 6291464 | tf_op jit(solution)/shard_map/ppermute | solution.py:46
  7.2 1.6 halves.3
  13.7 1.6 collective-permute-start.5
  16.8 7.1 %collective-permute-done.2.refs_5_ = bf16[2,256,512]{2,1,0:T(8,128)(2,1)} collective-permute-done((bf16[2,256,512]{2,1,0:T(8,128)(2,1)}, bf16[2,256,512]{2,1,0:T(8,128)(2,1)}, u32[]{:S(2)}, u32[]{:S(2)}) %collective-permute-start.2) | collective-permute-done | bytes 524320 | tf_op jit(solution)/shard_map/ppermute | solution.py:490
  25.4 10.6 %collective-permute-done.5.refs_8_ = bf16[2,256,512]{2,1,0:T(8,128)(2,1)} collective-permute-done((bf16[2,256,512]{2,1,0:T(8,128)(2,1)S(1)}, bf16[2,256,512]{2,1,0:T(8,128)(2,1)}, u32[]{:S(2)}, u32[]{:S(2)}) %collective-permute-start.5) | collective-permute-done | bytes 524320 | tf_op jit(solution)/shard_map/ppermute | solution.py:491
  38.9 3.7 %dynamic-slice_bitcast_fusion = (bf16[704,1024]{1,0:T(8,128)(2,1)}, bf16[704,1024]{1,0:T(8,128)(2,1)}) fusion(bf16[1,704,2048]{2,1,0:T(8,128)(2,1)} %param.30, s32[]{:T(128)S(6)} %select_n.136, s32[]{:T(128)S(6)} %select_n.135), kind=kLoop, calls=%fused_computation.5 | loop fusion | bytes 5767176 | tf_op jit(solution)/shard_map/dynamic_slice | solution.py:470
  42.7 1.6 collective-permute-start.8
  44.3 1.7 collective-permute-done.6.refs_9_
  47.5 3.7 %collective-permute-done.9.refs_12_ = bf16[2,256,512]{2,1,0:T(8,128)(2,1)} collective-permute-done((bf16[2,256,512]{2,1,0:T(8,128)(2,1)}, bf16[2,256,512]{2,1,0:T(8,128)(2,1)}, u32[]{:S(2)}, u32[]{:S(2)}) %collective-permute-start.9) | collective-permute-done | bytes 524320 | tf_op jit(solution)/shard_map/ppermute | solution.py:491
  51.1 1.6 collective-permute-start.10
  53.1 1.8 collective-permute-start.13
  59.4 3.0 %collective-permute-done.8.refs_11_ = bf16[2,256,512]{2,1,0:T(8,128)(2,1)} collective-permute-done((bf16[2,256,512]{2,1,0:T(8,128)(2,1)}, bf16[2,256,512]{2,1,0:T(8,128)(2,1)}, u32[]{:S(2)}, u32[]{:S(2)}) %collective-permute-start.8) | collective-permute-done | bytes 524320 | tf_op jit(solution)/shard_map/ppermute | solution.py:491
  64.4 8.0 %collective-permute-done.10.refs_13_ = bf16[2,256,512]{2,1,0:T(8,128)(2,1)} collective-permute-done((bf16[2,256,512]{2,1,0:T(8,128)(2,1)}, bf16[2,256,512]{2,1,0:T(8,128)(2,1)}, u32[]{:S(2)}, u32[]{:S(2)}) %collective-permute-start.10) | collective-permute-done | bytes 524320 | tf_op jit(solution)/shard_map/ppermute | solution.py:490
  77.7 7.1 %collective-permute-done.12.refs_15_ = bf16[2,256,512]{2,1,0:T(8,128)(2,1)} collective-permute-done((bf16[2,256,512]{2,1,0:T(8,128)(2,1)}, bf16[2,256,512]{2,1,0:T(8,128)(2,1)}, u32[]{:S(2)}, u32[]{:S(2)}) %collective-permute-start.12) | collective-permute-done | bytes 524320 | tf_op jit(solution)/shard_map/ppermute | solution.py:491
  84.9 8.7 %collective-permute-done.14.refs_17_ = bf16[2,256,512]{2,1,0:T(8,128)(2,1)} collective-permute-done((bf16[2,256,512]{2,1,0:T(8,128)(2,1)}, bf16[2,256,512]{2,1,0:T(8,128)(2,1)}, u32[]{:S(2)}, u32[]{:S(2)}) %collective-permute-start.14) | collective-permute-done | bytes 524320 | tf_op jit(solution)/shard_map/ppermute | solution.py:493
  94.5 10.7 %attention.3 = (bf16[256,256]{1,0:T(8,128)(2,1)S(1)}, bf16[256,256]{1,0:T(8,128)(2,1)S(1)}) custom-call(bf16[2,256,512]{2,1,0:T(8,128)(2,1)S(1)} %constant_dynamic-update-slice_fusion.refs_0_, s32[2,256,16]{2,1,0:T(8,128)S(1)} %bitcast_select_fusion.refs_1_, s32[16,256]{1,0:T(8,128)S(1)} %gather_fusion.3, bf16[2,256,512]{2,1,0:T(8,128)(2,1)} %get-tuple-element.40.refs_3_, ...), custom_call_target="tpu_custom_call" | custom-call | flops 2147483648 | bytes 4194304 | tf_op jit(solution)/shard_map/attention/pallas_call | solution.py:126
  107.4 10.7 %attention.2 = (bf16[256,256]{1,0:T(8,128)(2,1)S(1)}, bf16[256,256]{1,0:T(8,128)(2,1)S(1)}) custom-call(bf16[2,256,512]{2,1,0:T(8,128)(2,1)S(1)} %constant_dynamic-update-slice_fusion.refs_0_, s32[2,256,16]{2,1,0:T(8,128)S(1)} %bitcast_select_fusion.refs_1_, s32[16,256]{1,0:T(8,128)S(1)} %gather_fusion.3, bf16[2,256,512]{2,1,0:T(8,128)(2,1)} %get-tuple-element.40.refs_3_, ...), custom_call_target="tpu_custom_call" | custom-call | flops 2147483648 | bytes 4194304 | tf_op jit(solution)/shard_map/attention/pallas_call | solution.py:126
  120.4 2.9 %collective-permute-done.18.refs_1_ = bf16[256,256]{1,0:T(8,128)(2,1)S(1)} collective-permute-done((bf16[256,256]{1,0:T(8,128)(2,1)S(1)}, bf16[256,256]{1,0:T(8,128)(2,1)S(1)}, u32[]{:S(2)}, u32[]{:S(2)}) %collective-permute-start.18) | collective-permute-done | bytes 131104 | tf_op jit(solution)/shard_map/ppermute | solution.py:50
  123.2 4.0 %collective-permute-done.19.refs_2_ = bf16[256,256]{1,0:T(8,128)(2,1)S(1)} collective-permute-done((bf16[256,256]{1,0:T(8,128)(2,1)S(1)}, bf16[256,256]{1,0:T(8,128)(2,1)S(1)}, u32[]{:S(2)}, u32[]{:S(2)}) %collective-permute-start.19) | collective-permute-done | bytes 131104 | tf_op jit(solution)/shard_map/ppermute | solution.py:46
  127.2 5.3 %project.1 = (bf16[256,1024]{1,0:T(8,128)(2,1)S(1)}, f32[256,128]{1,0:T(8,128)S(1)}) custom-call(s32[8]{0:T(128)S(1)} %stack.62.place_ref, bf16[256,256]{1,0:T(8,128)(2,1)S(1)} %get-tuple-element.45.refs_0_, bf16[256,256]{1,0:T(8,128)(2,1)S(1)} %collective-permute-done.18.refs_1_, bf16[256,256]{1,0:T(8,128)(2,1)S(1)} %collective-permute-done.19.refs_2_, ...), custom_call_target="tpu_custom_call" | custom-call | flops 1073741824 | bytes 4194304 | tf_op jit(solution)/shard_map/project/pallas_call | solution.py:180
  133.5 4.3 %collective-permute-done.24.refs_2_ = f32[256,128]{1,0:T(8,128)S(1)} collective-permute-done((f32[256,128]{1,0:T(8,128)S(1)}, f32[256,128]{1,0:T(8,128)S(1)}, u32[]{:S(2)}, u32[]{:S(2)}) %collective-permute-start.24) | collective-permute-done | bytes 131104 | tf_op jit(solution)/shard_map/ppermute | solution.py:46
  138.4 1.6 collective-permute-start.25
  140.4 11.5 %collective-permute-done.25.refs_1_ = bf16[272,1024]{1,0:T(8,128)(2,1)S(1)} collective-permute-done((bf16[272,1024]{1,0:T(8,128)(2,1)S(1)}, bf16[272,1024]{1,0:T(8,128)(2,1)S(1)}, u32[]{:S(2)}, u32[]{:S(2)}) %collective-permute-start.25) | collective-permute-done | bytes 557088 | tf_op jit(solution)/shard_map/ppermute | solution.py:566
  154.9 9.6 %collective-permute-done.26.refs_0_ = bf16[272,1024]{1,0:T(8,128)(2,1)S(1)} collective-permute-done((bf16[272,1024]{1,0:T(8,128)(2,1)S(1)}, bf16[272,1024]{1,0:T(8,128)(2,1)S(1)}, u32[]{:S(2)}, u32[]{:S(2)}) %collective-permute-start.26) | collective-permute-done | bytes 557088 | tf_op jit(solution)/shard_map/ppermute | solution.py:566
  165.8 1.6 collective-permute-start.37
  168.3 8.8 %collective-permute-done.37.refs_0_ = bf16[272,1024]{1,0:T(8,128)(2,1)S(1)} collective-permute-done((bf16[272,1024]{1,0:T(8,128)(2,1)S(1)}, bf16[272,1024]{1,0:T(8,128)(2,1)S(1)}, u32[]{:S(2)}, u32[]{:S(2)}) %collective-permute-start.37) | collective-permute-done | bytes 557088 | tf_op jit(solution)/shard_map/ppermute | solution.py:566
  179.9 1.6 collective-permute-start.47
  181.5 3.0 %collective-permute-done.29.refs_1_ = bf16[2,192,1024]{2,1,0:T(8,128)(2,1)S(1)} collective-permute-done((bf16[2,192,1024]{2,1,0:T(8,128)(2,1)S(1)}, bf16[2,192,1024]{2,1,0:T(8,128)(2,1)S(1)}, u32[]{:S(2)}, u32[]{:S(2)}) %collective-permute-start.29) | collective-permute-done | bytes 786464 | tf_op jit(solution)/shard_map/ppermute | solution.py:46
  184.5 6.8 %expert_in.4.refs_0_ = bf16[2,192,704]{2,1,0:T(8,128)(2,1)S(1)} custom-call(s32[2]{0:T(128)S(1)} %and_select_fusion.kmap_ref, bf16[2,192,1024]{2,1,0:T(8,128)(2,1)S(1)} %select.52.refs_0_, bf16[2,192,1024]{2,1,0:T(8,128)(2,1)S(1)} %collective-permute-done.29.refs_1_, bf16[1,704,2048]{2,1,0:T(8,128)(2,1)S(1)} %bitcast.57, ...), custom_call_target="tpu_custom_call" | custom-call | flops 2214592512 | bytes 11534336 | tf_op jit(solution)/shard_map/expert_in/pallas_call | solution.py:328
  192.8 3.0 %collective-permute-done.39.refs_1_ = bf16[2,128,1024]{2,1,0:T(8,128)(2,1)S(1)} collective-permute-done((bf16[2,128,1024]{2,1,0:T(8,128)(2,1)S(1)}, bf16[2,128,1024]{2,1,0:T(8,128)(2,1)S(1)}, u32[]{:S(2)}, u32[]{:S(2)}) %collective-permute-start.39) | collective-permute-done | bytes 524320 | tf_op jit(solution)/shard_map/ppermute | solution.py:46
  196.3 6.8 %expert_in.5.refs_0_ = bf16[2,128,704]{2,1,0:T(8,128)(2,1)S(1)} custom-call(s32[2]{0:T(128)S(1)} %and_select_fusion.kmap_ref, bf16[2,128,1024]{2,1,0:T(8,128)(2,1)S(1)} %select.53.refs_0_, bf16[2,128,1024]{2,1,0:T(8,128)(2,1)S(1)} %collective-permute-done.39.refs_1_, bf16[1,704,2048]{2,1,0:T(8,128)(2,1)S(1)} %bitcast.58, ...), custom_call_target="tpu_custom_call" | custom-call | flops 1476395008 | bytes 11534336 | tf_op jit(solution)/shard_map/expert_in/pallas_call | solution.py:328
  206.1 2.3 collective-permute-done.32.refs_1_
  208.4 3.4 %expert_out.4 = (bf16[2,64,1024]{2,1,0:T(8,128)(2,1)S(1)}, bf16[2,64,1024]{2,1,0:T(8,128)(2,1)}, bf16[2,64,1024]{2,1,0:T(8,128)(2,1)S(1)}) custom-call(bf16[2,192,704]{2,1,0:T(8,128)(2,1)S(1)} %expert_in.4.refs_0_, bf16[2,192,704]{2,1,0:T(8,128)(2,1)S(1)} %collective-permute-done.32.refs_1_, bf16[704,1024]{1,0:T(8,128)(2,1)S(1)} %copy-done.2, ...), custom_call_target="tpu_custom_call" | custom-call | flops 1107296256 | bytes 5767168 | tf_op jit(solution)/shard_map/expert_out/pallas_call | solution.py:368
  211.8 7.8 %collective-permute-done.43.refs_1_ = bf16[2,128,1024]{2,1,0:T(8,128)(2,1)S(1)} collective-permute-done((bf16[2,128,1024]{2,1,0:T(8,128)(2,1)S(1)}, bf16[2,128,1024]{2,1,0:T(8,128)(2,1)S(1)}, u32[]{:S(2)}, u32[]{:S(2)}) %collective-permute-start.43) | collective-permute-done | bytes 524320 | tf_op jit(solution)/shard_map/ppermute | solution.py:46
  219.6 6.8 %expert_in.6.refs_0_ = bf16[2,128,704]{2,1,0:T(8,128)(2,1)S(1)} custom-call(s32[2]{0:T(128)S(1)} %and_select_fusion.kmap_ref, bf16[2,128,1024]{2,1,0:T(8,128)(2,1)S(1)} %select.54.refs_0_, bf16[2,128,1024]{2,1,0:T(8,128)(2,1)S(1)} %collective-permute-done.43.refs_1_, bf16[1,704,2048]{2,1,0:T(8,128)(2,1)S(1)} %bitcast.59, ...), custom_call_target="tpu_custom_call" | custom-call | flops 1476395008 | bytes 11534336 | tf_op jit(solution)/shard_map/expert_in/pallas_call | solution.py:328
  227.7 1.6 collective-permute-start.36
  229.3 3.3 %expert_out.5 = (bf16[2,64,1024]{2,1,0:T(8,128)(2,1)}, bf16[2,64,1024]{2,1,0:T(8,128)(2,1)S(1)}) custom-call(bf16[2,128,704]{2,1,0:T(8,128)(2,1)S(1)} %expert_in.5.refs_0_, bf16[2,128,704]{2,1,0:T(8,128)(2,1)S(1)} %collective-permute-done.40.refs_1_, bf16[704,1024]{1,0:T(8,128)(2,1)S(1)} %copy-done.2, bf16[704,1024]{1,0:T(8,128)(2,1)} %collective-permute-done.17.refs_3_, ...), custom_call_target="tpu_custom_call" | custom-call | flops 738197504 | bytes 5767168 | tf_op jit(solution)/shard_map/expert_out/pallas_call | solution.py:368
  233.7 6.6 %expert_in.7.refs_0_ = bf16[2,64,704]{2,1,0:T(8,128)(2,1)S(1)} custom-call(s32[2]{0:T(128)S(1)} %and_select_fusion.kmap_ref, bf16[2,64,1024]{2,1,0:T(8,128)(2,1)S(1)} %select.55.refs_0_, bf16[2,64,1024]{2,1,0:T(8,128)(2,1)S(1)} %collective-permute-done.48.refs_1_, bf16[1,704,2048]{2,1,0:T(8,128)(2,1)S(1)} %bitcast.60, ...), custom_call_target="tpu_custom_call" | custom-call | flops 738197504 | bytes 11534336 | tf_op jit(solution)/shard_map/expert_in/pallas_call | solution.py:328
  242.7 2.4 collective-permute-start.42
  249.1 3.1 %expert_out.6 = (bf16[2,64,1024]{2,1,0:T(8,128)(2,1)}, bf16[2,64,1024]{2,1,0:T(8,128)(2,1)S(1)}) custom-call(bf16[2,128,704]{2,1,0:T(8,128)(2,1)S(1)} %expert_in.6.refs_0_, bf16[2,128,704]{2,1,0:T(8,128)(2,1)} %collective-permute-done.44.refs_1_, bf16[704,1024]{1,0:T(8,128)(2,1)S(1)} %copy-done.3, bf16[704,1024]{1,0:T(8,128)(2,1)} %collective-permute-done.17.refs_3_, ...), custom_call_target="tpu_custom_call" | custom-call | flops 738197504 | bytes 5767168 | tf_op jit(solution)/shard_map/expert_out/pallas_call | solution.py:368
  252.3 2.1 collective-permute-start.45
  254.4 1.7 collective-permute-start.46
  260.5 2.5 expert_out.7
  263.0 3.0 %collective-permute-start.50 = (bf16[2,64,1024]{2,1,0:T(8,128)(2,1)S(1)}, bf16[2,64,1024]{2,1,0:T(8,128)(2,1)S(1)}, u32[]{:S(2)}, u32[]{:S(2)}) collective-permute-start(bf16[2,64,1024]{2,1,0:T(8,128)(2,1)S(1)} %expert_out.7), channel_id=1, source_target_pairs={{4,24},{6,26},{12,16},{14,18},{20,8},{22,10},{28,0},{30,2},{24,4},... | collective-permute-start | bytes 786440 | tf_op jit(solution)/shard_map/ppermute | solution.py:596
  266.2 6.1 %collective-permute-done.42.refs_4_ = bf16[2,64,1024]{2,1,0:T(8,128)(2,1)} collective-permute-done((bf16[2,64,1024]{2,1,0:T(8,128)(2,1)S(1)}, bf16[2,64,1024]{2,1,0:T(8,128)(2,1)}, u32[]{:S(2)}, u32[]{:S(2)}) %collective-permute-start.42) | collective-permute-done | bytes 262176 | tf_op jit(solution)/shard_map/ppermute | solution.py:596
  272.2 6.4 %collective-permute-done.45.refs_5_ = bf16[2,64,1024]{2,1,0:T(8,128)(2,1)} collective-permute-done((bf16[2,64,1024]{2,1,0:T(8,128)(2,1)}, bf16[2,64,1024]{2,1,0:T(8,128)(2,1)}, u32[]{:S(2)}, u32[]{:S(2)}) %collective-permute-start.45) | collective-permute-done | bytes 262176 | tf_op jit(solution)/shard_map/ppermute | solution.py:596
  278.7 3.5 %combine.2.base_ref = f32[256,1024]{1,0:T(8,128)S(1)} custom-call(bf16[256,1024]{1,0:T(8,128)(2,1)S(1)} %get-tuple-element.50.refs_0_.base_ref, f32[256,128]{1,0:T(8,128)S(1)} %get-tuple-element.52.gate_ref, s32[256,2]{1,0:T(8,128)S(1)} %add.209.code_ref, bf16[2,64,1024]{2,1,0:T(8,128)(2,1)S(1)} %copy-done.16, ...), custom_call_target="tpu_custom_call" | custom-call | flops 939524096 | bytes 1835008 | tf_op jit(solution)/shard_map/combine/pallas_call | solution.py:405
  (191 shorter events, 59.5 us)
Async XLA Ops:
  4.1 49.0 %collective-permute-start.16 = (bf16[1024,1024]{1,0:T(8,128)(2,1)}, bf16[1024,1024]{1,0:T(8,128)(2,1)}, u32[]{:S(2)}, u32[]{:S(2)}) collective-permute-start(bf16[1024,1024]{1,0:T(8,128)(2,1)} %get-tuple-element.74), channel_id=1, source_target_pairs={{0,1},{1,0},{2,3},{3,2},{4,5},{5,4},{6,7},{7,6},{8,9},{9,8},{10,11... | collective-permute-start | bytes 6291464 | tf_op jit(solution)/shard_map/ppermute | solution.py:46
  8.9 15.0 %collective-permute-start.2 = (bf16[2,256,512]{2,1,0:T(8,128)(2,1)}, bf16[2,256,512]{2,1,0:T(8,128)(2,1)}, u32[]{:S(2)}, u32[]{:S(2)}) collective-permute-start(bf16[2,256,512]{2,1,0:T(8,128)(2,1)} %get-tuple-element.40.refs_3_), channel_id=1, source_target_pairs={{4,12},{6,14},{12,20},{14,22},{20,28},{22,30},{28,24},{30,26},{24,... | collective-permute-start | bytes 1572872 | tf_op jit(solution)/shard_map/ppermute | solution.py:490
  10.4 32.2 %collective-permute-start.4 = (bf16[2,256,512]{2,1,0:T(8,128)(2,1)}, bf16[2,256,512]{2,1,0:T(8,128)(2,1)}, u32[]{:S(2)}, u32[]{:S(2)}) collective-permute-start(bf16[2,256,512]{2,1,0:T(8,128)(2,1)} %get-tuple-element.40.refs_3_), channel_id=1, source_target_pairs={{12,4},{14,6},{20,12},{22,14},{28,20},{30,22},{24,28},{26,30},{16,... | collective-permute-start | bytes 1572872 | tf_op jit(solution)/shard_map/ppermute | solution.py:491
  13.7 22.2 %collective-permute-start.5 = (bf16[2,256,512]{2,1,0:T(8,128)(2,1)S(1)}, bf16[2,256,512]{2,1,0:T(8,128)(2,1)}, u32[]{:S(2)}, u32[]{:S(2)}) collective-permute-start(bf16[2,256,512]{2,1,0:T(8,128)(2,1)S(1)} %collective-permute-done.1.refs_4_), channel_id=1, source_target_pairs={{12,4},{14,6},{20,12},{22,14},{28,20},{30,22},{24,28},{26,30},{16,... | collective-permute-start | bytes 1572872 | tf_op jit(solution)/shard_map/ppermute | solution.py:491
  16.3 26.4 %collective-permute-start.3 = (bf16[2,256,512]{2,1,0:T(8,128)(2,1)S(1)}, bf16[2,256,512]{2,1,0:T(8,128)(2,1)}, u32[]{:S(2)}, u32[]{:S(2)}) collective-permute-start(bf16[2,256,512]{2,1,0:T(8,128)(2,1)S(1)} %collective-permute-done.1.refs_4_), channel_id=1, source_target_pairs={{4,12},{6,14},{12,20},{14,22},{20,28},{22,30},{28,24},{30,26},{24,... | collective-permute-start | bytes 1572872 | tf_op jit(solution)/shard_map/ppermute | solution.py:490
  23.9 22.1 %collective-permute-start.6 = (bf16[2,256,512]{2,1,0:T(8,128)(2,1)}, bf16[2,256,512]{2,1,0:T(8,128)(2,1)}, u32[]{:S(2)}, u32[]{:S(2)}) collective-permute-start(bf16[2,256,512]{2,1,0:T(8,128)(2,1)} %collective-permute-done.2.refs_5_), channel_id=1, source_target_pairs={{4,12},{6,14},{12,20},{14,22},{20,28},{22,30},{28,24},{30,26},{24,... | collective-permute-start | bytes 1572872 | tf_op jit(solution)/shard_map/ppermute | solution.py:490
  36.0 15.2 %collective-permute-start.9 = (bf16[2,256,512]{2,1,0:T(8,128)(2,1)}, bf16[2,256,512]{2,1,0:T(8,128)(2,1)}, u32[]{:S(2)}, u32[]{:S(2)}) collective-permute-start(bf16[2,256,512]{2,1,0:T(8,128)(2,1)} %collective-permute-done.5.refs_8_), channel_id=1, source_target_pairs={{12,4},{14,6},{20,12},{22,14},{28,20},{30,22},{24,28},{26,30},{16,... | collective-permute-start | bytes 1572872 | tf_op jit(solution)/shard_map/ppermute | solution.py:491
  42.5 12.4 %collective-permute-start = (bf16[1,256,512]{2,1,0:T(8,128)(2,1)S(1)}, bf16[1,256,512]{2,1,0:T(8,128)(2,1)S(1)}, u32[]{:S(2)}, u32[]{:S(2)}) collective-permute-start(bf16[1,256,512]{2,1,0:T(8,128)(2,1)S(1)} %get-tuple-element.39), channel_id=1, source_target_pairs={{0,2},{2,0},{4,6},{6,4},{8,10},{10,8},{12,14},{14,12},{16,18},{18,... | collective-permute-start | bytes 786440 | tf_op jit(solution)/shard_map/ppermute | solution.py:50
  42.7 19.7 %collective-permute-start.8 = (bf16[2,256,512]{2,1,0:T(8,128)(2,1)}, bf16[2,256,512]{2,1,0:T(8,128)(2,1)}, u32[]{:S(2)}, u32[]{:S(2)}) collective-permute-start(bf16[2,256,512]{2,1,0:T(8,128)(2,1)} %collective-permute-done.4.refs_7_), channel_id=1, source_target_pairs={{12,4},{14,6},{20,12},{22,14},{28,20},{30,22},{24,28},{26,30},{16,... | collective-permute-start | bytes 1572872 | tf_op jit(solution)/shard_map/ppermute | solution.py:491
  46.0 16.9 %collective-permute-start.7 = (bf16[2,256,512]{2,1,0:T(8,128)(2,1)}, bf16[2,256,512]{2,1,0:T(8,128)(2,1)}, u32[]{:S(2)}, u32[]{:S(2)}) collective-permute-start(bf16[2,256,512]{2,1,0:T(8,128)(2,1)} %collective-permute-done.3.refs_6_), channel_id=1, source_target_pairs={{4,12},{6,14},{12,20},{14,22},{20,28},{22,30},{28,24},{30,26},{24,... | collective-permute-start | bytes 1572872 | tf_op jit(solution)/shard_map/ppermute | solution.py:490
  51.1 21.2 %collective-permute-start.10 = (bf16[2,256,512]{2,1,0:T(8,128)(2,1)}, bf16[2,256,512]{2,1,0:T(8,128)(2,1)}, u32[]{:S(2)}, u32[]{:S(2)}) collective-permute-start(bf16[2,256,512]{2,1,0:T(8,128)(2,1)} %collective-permute-done.6.refs_9_), channel_id=1, source_target_pairs={{4,12},{6,14},{12,20},{14,22},{20,28},{22,30},{28,24},{30,26},{24,... | collective-permute-start | bytes 1572872 | tf_op jit(solution)/shard_map/ppermute | solution.py:490
  53.1 20.8 %collective-permute-start.13 = (bf16[2,256,512]{2,1,0:T(8,128)(2,1)}, bf16[2,256,512]{2,1,0:T(8,128)(2,1)}, u32[]{:S(2)}, u32[]{:S(2)}) collective-permute-start(bf16[2,256,512]{2,1,0:T(8,128)(2,1)} %collective-permute-done.9.refs_12_), channel_id=1, source_target_pairs={{12,4},{14,6},{20,12},{22,14},{28,20},{30,22},{24,28},{26,30},{16,... | collective-permute-start | bytes 1572872 | tf_op jit(solution)/shard_map/ppermute | solution.py:491
  54.9 64.0 %collective-permute-start.17 = (bf16[704,1024]{1,0:T(8,128)(2,1)}, bf16[704,1024]{1,0:T(8,128)(2,1)}, u32[]{:S(2)}, u32[]{:S(2)}) collective-permute-start(bf16[704,1024]{1,0:T(8,128)(2,1)} %get-tuple-element.44), channel_id=1, source_target_pairs={{0,1},{1,0},{2,3},{3,2},{4,5},{5,4},{6,7},{7,6},{8,9},{9,8},{10,11... | collective-permute-start | bytes 4325384 | tf_op jit(solution)/shard_map/ppermute | solution.py:46
  62.4 22.5 %collective-permute-start.12 = (bf16[2,256,512]{2,1,0:T(8,128)(2,1)}, bf16[2,256,512]{2,1,0:T(8,128)(2,1)}, u32[]{:S(2)}, u32[]{:S(2)}) collective-permute-start(bf16[2,256,512]{2,1,0:T(8,128)(2,1)} %collective-permute-done.8.refs_11_), channel_id=1, source_target_pairs={{12,4},{14,6},{20,12},{22,14},{28,20},{30,22},{24,28},{26,30},{16,... | collective-permute-start | bytes 1572872 | tf_op jit(solution)/shard_map/ppermute | solution.py:491
  62.9 21.9 %collective-permute-start.11 = (bf16[2,256,512]{2,1,0:T(8,128)(2,1)}, bf16[2,256,512]{2,1,0:T(8,128)(2,1)}, u32[]{:S(2)}, u32[]{:S(2)}) collective-permute-start(bf16[2,256,512]{2,1,0:T(8,128)(2,1)} %collective-permute-done.7.refs_10_), channel_id=1, source_target_pairs={{4,12},{6,14},{12,20},{14,22},{20,28},{22,30},{28,24},{30,26},{24,... | collective-permute-start | bytes 1572872 | tf_op jit(solution)/shard_map/ppermute | solution.py:490
  72.4 21.2 %collective-permute-start.14 = (bf16[2,256,512]{2,1,0:T(8,128)(2,1)}, bf16[2,256,512]{2,1,0:T(8,128)(2,1)}, u32[]{:S(2)}, u32[]{:S(2)}) collective-permute-start(bf16[2,256,512]{2,1,0:T(8,128)(2,1)} %collective-permute-done.10.refs_13_), channel_id=1, source_target_pairs={{4,12},{6,14},{12,20},{14,22},{20,28},{22,30},{28,24},{30,26},{24,... | collective-permute-start | bytes 1572872 | tf_op jit(solution)/shard_map/ppermute | solution.py:493
  73.9 20.6 %collective-permute-start.15 = (bf16[2,256,512]{2,1,0:T(8,128)(2,1)}, bf16[2,256,512]{2,1,0:T(8,128)(2,1)}, u32[]{:S(2)}, u32[]{:S(2)}) collective-permute-start(bf16[2,256,512]{2,1,0:T(8,128)(2,1)} %collective-permute-done.13.refs_16_), channel_id=1, source_target_pairs={{12,4},{14,6},{20,12},{22,14},{28,20},{30,22},{24,28},{26,30},{16,... | collective-permute-start | bytes 1572872 | tf_op jit(solution)/shard_map/ppermute | solution.py:494
  84.8 94.5 %collective-permute-start.30 = (bf16[1,704,2048]{2,1,0:T(8,128)(2,1)}, bf16[1,704,2048]{2,1,0:T(8,128)(2,1)}, u32[]{:S(2)}, u32[]{:S(2)}) collective-permute-start(bf16[1,704,2048]{2,1,0:T(8,128)(2,1)} %bitcast.56), channel_id=1, source_target_pairs={{0,2},{2,0},{4,6},{6,4},{8,10},{10,8},{12,14},{14,12},{16,18},{18,... | collective-permute-start | bytes 8650760 | tf_op jit(solution)/shard_map/ppermute | solution.py:50
  105.1 12.9 %collective-permute-start.21 = (bf16[256,256]{1,0:T(8,128)(2,1)S(1)}, bf16[256,256]{1,0:T(8,128)(2,1)S(1)}, u32[]{:S(2)}, u32[]{:S(2)}) collective-permute-start(bf16[256,256]{1,0:T(8,128)(2,1)S(1)} %get-tuple-element.48), channel_id=1, source_target_pairs={{0,2},{2,0},{4,6},{6,4},{8,10},{10,8},{12,14},{14,12},{16,18},{18,... | collective-permute-start | bytes 393224 | tf_op jit(solution)/shard_map/ppermute | solution.py:50
  105.2 13.4 %collective-permute-start.23 = (bf16[256,256]{1,0:T(8,128)(2,1)S(1)}, bf16[256,256]{1,0:T(8,128)(2,1)S(1)}, u32[]{:S(2)}, u32[]{:S(2)}) collective-permute-start(bf16[256,256]{1,0:T(8,128)(2,1)S(1)} %get-tuple-element.48), channel_id=1, source_target_pairs={{0,3},{1,2},{2,1},{3,0},{4,7},{5,6},{6,5},{7,4},{8,11},{9,10},{10,... | collective-permute-start | bytes 393224 | tf_op jit(solution)/shard_map/ppermute | solution.py:510
  105.9 12.3 %collective-permute-start.22 = (bf16[256,256]{1,0:T(8,128)(2,1)S(1)}, bf16[256,256]{1,0:T(8,128)(2,1)S(1)}, u32[]{:S(2)}, u32[]{:S(2)}) collective-permute-start(bf16[256,256]{1,0:T(8,128)(2,1)S(1)} %get-tuple-element.47.refs_4_), channel_id=1, source_target_pairs={{0,1},{1,0},{2,3},{3,2},{4,5},{5,4},{6,7},{7,6},{8,9},{9,8},{10,11... | collective-permute-start | bytes 393224 | tf_op jit(solution)/shard_map/ppermute | solution.py:46
  118.0 61.9 %collective-permute-start.31 = (bf16[1,704,2048]{2,1,0:T(8,128)(2,1)}, bf16[1,704,2048]{2,1,0:T(8,128)(2,1)}, u32[]{:S(2)}, u32[]{:S(2)}) collective-permute-start(bf16[1,704,2048]{2,1,0:T(8,128)(2,1)} %bitcast.23.refs_3_), channel_id=1, source_target_pairs={{0,2},{2,0},{4,6},{6,4},{8,10},{10,8},{12,14},{14,12},{16,18},{18,... | collective-permute-start | bytes 8650760 | tf_op jit(solution)/shard_map/ppermute | solution.py:50
  118.6 8.6 %collective-permute-start.20 = (bf16[256,256]{1,0:T(8,128)(2,1)S(1)}, bf16[256,256]{1,0:T(8,128)(2,1)S(1)}, u32[]{:S(2)}, u32[]{:S(2)}) collective-permute-start(bf16[256,256]{1,0:T(8,128)(2,1)S(1)} %get-tuple-element.46), channel_id=1, source_target_pairs={{0,3},{1,2},{2,1},{3,0},{4,7},{5,6},{6,5},{7,4},{8,11},{9,10},{10,... | collective-permute-start | bytes 393224 | tf_op jit(solution)/shard_map/ppermute | solution.py:510
  118.8 8.4 %collective-permute-start.19 = (bf16[256,256]{1,0:T(8,128)(2,1)S(1)}, bf16[256,256]{1,0:T(8,128)(2,1)S(1)}, u32[]{:S(2)}, u32[]{:S(2)}) collective-permute-start(bf16[256,256]{1,0:T(8,128)(2,1)S(1)} %get-tuple-element.45.refs_0_), channel_id=1, source_target_pairs={{0,1},{1,0},{2,3},{3,2},{4,5},{5,4},{6,7},{7,6},{8,9},{9,8},{10,11... | collective-permute-start | bytes 393224 | tf_op jit(solution)/shard_map/ppermute | solution.py:46
  138.4 13.6 %collective-permute-start.25 = (bf16[272,1024]{1,0:T(8,128)(2,1)S(1)}, bf16[272,1024]{1,0:T(8,128)(2,1)S(1)}, u32[]{:S(2)}, u32[]{:S(2)}) collective-permute-start(bf16[272,1024]{1,0:T(8,128)(2,1)S(1)} %get-tuple-element.53.refs_0_), channel_id=1, source_target_pairs={{4,12},{6,14},{12,20},{14,22},{20,28},{22,30},{28,24},{30,26},{24,... | collective-permute-start | bytes 1671176 | tf_op jit(solution)/shard_map/ppermute | solution.py:566
  140.0 13.5 %collective-permute-start.27 = (bf16[272,1024]{1,0:T(8,128)(2,1)S(1)}, bf16[272,1024]{1,0:T(8,128)(2,1)S(1)}, u32[]{:S(2)}, u32[]{:S(2)}) collective-permute-start(bf16[272,1024]{1,0:T(8,128)(2,1)S(1)} %get-tuple-element.53.refs_0_), channel_id=1, source_target_pairs={{12,4},{14,6},{20,12},{22,14},{28,20},{30,22},{24,28},{26,30},{16,... | collective-permute-start | bytes 1671176 | tf_op jit(solution)/shard_map/ppermute | solution.py:569
  151.9 12.6 %collective-permute-start.26 = (bf16[272,1024]{1,0:T(8,128)(2,1)S(1)}, bf16[272,1024]{1,0:T(8,128)(2,1)S(1)}, u32[]{:S(2)}, u32[]{:S(2)}) collective-permute-start(bf16[272,1024]{1,0:T(8,128)(2,1)S(1)} %collective-permute-done.25.refs_1_), channel_id=1, source_target_pairs={{4,12},{6,14},{12,20},{14,22},{20,28},{22,30},{28,24},{30,26},{24,... | collective-permute-start | bytes 1671176 | tf_op jit(solution)/shard_map/ppermute | solution.py:566
  153.5 12.3 %collective-permute-start.28 = (bf16[272,1024]{1,0:T(8,128)(2,1)S(1)}, bf16[272,1024]{1,0:T(8,128)(2,1)S(1)}, u32[]{:S(2)}, u32[]{:S(2)}) collective-permute-start(bf16[272,1024]{1,0:T(8,128)(2,1)S(1)} %collective-permute-done.27.refs_2_), channel_id=1, source_target_pairs={{12,4},{14,6},{20,12},{22,14},{28,20},{30,22},{24,28},{26,30},{16,... | collective-permute-start | bytes 1671176 | tf_op jit(solution)/shard_map/ppermute | solution.py:569
  165.8 11.4 %collective-permute-start.37 = (bf16[272,1024]{1,0:T(8,128)(2,1)S(1)}, bf16[272,1024]{1,0:T(8,128)(2,1)S(1)}, u32[]{:S(2)}, u32[]{:S(2)}) collective-permute-start(bf16[272,1024]{1,0:T(8,128)(2,1)S(1)} %collective-permute-done.26.refs_0_), channel_id=1, source_target_pairs={{4,12},{6,14},{12,20},{14,22},{20,28},{22,30},{28,24},{30,26},{24,... | collective-permute-start | bytes 1671176 | tf_op jit(solution)/shard_map/ppermute | solution.py:566
  167.4 11.1 %collective-permute-start.38 = (bf16[272,1024]{1,0:T(8,128)(2,1)S(1)}, bf16[272,1024]{1,0:T(8,128)(2,1)S(1)}, u32[]{:S(2)}, u32[]{:S(2)}) collective-permute-start(bf16[272,1024]{1,0:T(8,128)(2,1)S(1)} %collective-permute-done.28.refs_1_), channel_id=1, source_target_pairs={{12,4},{14,6},{20,12},{22,14},{28,20},{30,22},{24,28},{26,30},{16,... | collective-permute-start | bytes 1671176 | tf_op jit(solution)/shard_map/ppermute | solution.py:569
  167.8 16.7 %collective-permute-start.29 = (bf16[2,192,1024]{2,1,0:T(8,128)(2,1)S(1)}, bf16[2,192,1024]{2,1,0:T(8,128)(2,1)S(1)}, u32[]{:S(2)}, u32[]{:S(2)}) collective-permute-start(bf16[2,192,1024]{2,1,0:T(8,128)(2,1)S(1)} %select.52.refs_0_), channel_id=1, source_target_pairs={{0,1},{1,0},{2,3},{3,2},{4,5},{5,4},{6,7},{7,6},{8,9},{9,8},{10,11... | collective-permute-start | bytes 2359304 | tf_op jit(solution)/shard_map/ppermute | solution.py:46
  177.2 28.3 %collective-permute-start.33 = (bf16[704,1024]{1,0:T(8,128)(2,1)}, bf16[704,1024]{1,0:T(8,128)(2,1)S(1)}, u32[]{:S(2)}, u32[]{:S(2)}) collective-permute-start(bf16[704,1024]{1,0:T(8,128)(2,1)} %get-tuple-element.75.refs_2_), channel_id=1, source_target_pairs={{0,2},{2,0},{4,6},{6,4},{8,10},{10,8},{12,14},{14,12},{16,18},{18,... | collective-permute-start | bytes 4325384 | tf_op jit(solution)/shard_map/ppermute | solution.py:50
  178.5 27.6 %collective-permute-start.34 = (bf16[704,1024]{1,0:T(8,128)(2,1)}, bf16[704,1024]{1,0:T(8,128)(2,1)S(1)}, u32[]{:S(2)}, u32[]{:S(2)}) collective-permute-start(bf16[704,1024]{1,0:T(8,128)(2,1)} %collective-permute-done.17.refs_3_), channel_id=1, source_target_pairs={{0,2},{2,0},{4,6},{6,4},{8,10},{10,8},{12,14},{14,12},{16,18},{18,... | collective-permute-start | bytes 4325384 | tf_op jit(solution)/shard_map/ppermute | solution.py:50
  179.3 16.4 %collective-permute-start.39 = (bf16[2,128,1024]{2,1,0:T(8,128)(2,1)S(1)}, bf16[2,128,1024]{2,1,0:T(8,128)(2,1)S(1)}, u32[]{:S(2)}, u32[]{:S(2)}) collective-permute-start(bf16[2,128,1024]{2,1,0:T(8,128)(2,1)S(1)} %select.53.refs_0_), channel_id=1, source_target_pairs={{0,1},{1,0},{2,3},{3,2},{4,5},{5,4},{6,7},{7,6},{8,9},{9,8},{10,11... | collective-permute-start | bytes 1572872 | tf_op jit(solution)/shard_map/ppermute | solution.py:46
  179.9 23.2 %collective-permute-start.47 = (bf16[272,1024]{1,0:T(8,128)(2,1)S(1)}, bf16[272,1024]{1,0:T(8,128)(2,1)S(1)}, u32[]{:S(2)}, u32[]{:S(2)}) collective-permute-start(bf16[272,1024]{1,0:T(8,128)(2,1)S(1)} %collective-permute-done.37.refs_0_), channel_id=1, source_target_pairs={{4,12},{6,14},{12,20},{14,22},{20,28},{22,30},{28,24},{30,26},{24,... | collective-permute-start | bytes 1671176 | tf_op jit(solution)/shard_map/ppermute | solution.py:566
  191.3 17.1 %collective-permute-start.32 = (bf16[2,192,704]{2,1,0:T(8,128)(2,1)S(1)}, bf16[2,192,704]{2,1,0:T(8,128)(2,1)S(1)}, u32[]{:S(2)}, u32[]{:S(2)}) collective-permute-start(bf16[2,192,704]{2,1,0:T(8,128)(2,1)S(1)} %expert_in.4.refs_0_), channel_id=1, source_target_pairs={{0,1},{1,0},{2,3},{3,2},{4,5},{5,4},{6,7},{7,6},{8,9},{9,8},{10,11... | collective-permute-start | bytes 1622024 | tf_op jit(solution)/shard_map/ppermute | solution.py:46
  195.8 23.9 %collective-permute-start.43 = (bf16[2,128,1024]{2,1,0:T(8,128)(2,1)S(1)}, bf16[2,128,1024]{2,1,0:T(8,128)(2,1)S(1)}, u32[]{:S(2)}, u32[]{:S(2)}) collective-permute-start(bf16[2,128,1024]{2,1,0:T(8,128)(2,1)S(1)} %select.54.refs_0_), channel_id=1, source_target_pairs={{0,1},{1,0},{2,3},{3,2},{4,5},{5,4},{6,7},{7,6},{8,9},{9,8},{10,11... | collective-permute-start | bytes 1572872 | tf_op jit(solution)/shard_map/ppermute | solution.py:46
  203.1 26.1 %collective-permute-start.40 = (bf16[2,128,704]{2,1,0:T(8,128)(2,1)S(1)}, bf16[2,128,704]{2,1,0:T(8,128)(2,1)S(1)}, u32[]{:S(2)}, u32[]{:S(2)}) collective-permute-start(bf16[2,128,704]{2,1,0:T(8,128)(2,1)S(1)} %expert_in.5.refs_0_), channel_id=1, source_target_pairs={{0,1},{1,0},{2,3},{3,2},{4,5},{5,4},{6,7},{7,6},{8,9},{9,8},{10,11... | collective-permute-start | bytes 1081352 | tf_op jit(solution)/shard_map/ppermute | solution.py:46
  205.5 28.2 %collective-permute-start.48 = (bf16[2,64,1024]{2,1,0:T(8,128)(2,1)S(1)}, bf16[2,64,1024]{2,1,0:T(8,128)(2,1)S(1)}, u32[]{:S(2)}, u32[]{:S(2)}) collective-permute-start(bf16[2,64,1024]{2,1,0:T(8,128)(2,1)S(1)} %select.55.refs_0_), channel_id=1, source_target_pairs={{0,1},{1,0},{2,3},{3,2},{4,5},{5,4},{6,7},{7,6},{8,9},{9,8},{10,11... | collective-permute-start | bytes 786440 | tf_op jit(solution)/shard_map/ppermute | solution.py:46
  226.5 16.2 %collective-permute-start.44 = (bf16[2,128,704]{2,1,0:T(8,128)(2,1)S(1)}, bf16[2,128,704]{2,1,0:T(8,128)(2,1)}, u32[]{:S(2)}, u32[]{:S(2)}) collective-permute-start(bf16[2,128,704]{2,1,0:T(8,128)(2,1)S(1)} %expert_in.6.refs_0_), channel_id=1, source_target_pairs={{0,1},{1,0},{2,3},{3,2},{4,5},{5,4},{6,7},{7,6},{8,9},{9,8},{10,11... | collective-permute-start | bytes 1081352 | tf_op jit(solution)/shard_map/ppermute | solution.py:46
  227.2 25.1 %collective-permute-start.35 = (bf16[2,64,1024]{2,1,0:T(8,128)(2,1)}, bf16[2,64,1024]{2,1,0:T(8,128)(2,1)}, u32[]{:S(2)}, u32[]{:S(2)}) collective-permute-start(bf16[2,64,1024]{2,1,0:T(8,128)(2,1)} %get-tuple-element.57), channel_id=1, source_target_pairs={{4,0},{6,2},{12,4},{14,6},{20,12},{22,14},{28,20},{30,22},{24,28},... | collective-permute-start | bytes 786440 | tf_op jit(solution)/shard_map/ppermute | solution.py:596
  227.7 35.3 %collective-permute-start.36 = (bf16[2,64,1024]{2,1,0:T(8,128)(2,1)S(1)}, bf16[2,64,1024]{2,1,0:T(8,128)(2,1)}, u32[]{:S(2)}, u32[]{:S(2)}) collective-permute-start(bf16[2,64,1024]{2,1,0:T(8,128)(2,1)S(1)} %get-tuple-element.58), channel_id=1, source_target_pairs={{4,12},{6,14},{12,20},{14,22},{20,28},{22,30},{28,24},{30,26},{24,... | collective-permute-start | bytes 786440 | tf_op jit(solution)/shard_map/ppermute | solution.py:596
  240.3 14.1 %collective-permute-start.49 = (bf16[2,64,704]{2,1,0:T(8,128)(2,1)S(1)}, bf16[2,64,704]{2,1,0:T(8,128)(2,1)S(1)}, u32[]{:S(2)}, u32[]{:S(2)}) collective-permute-start(bf16[2,64,704]{2,1,0:T(8,128)(2,1)S(1)} %expert_in.7.refs_0_), channel_id=1, source_target_pairs={{0,1},{1,0},{2,3},{3,2},{4,5},{5,4},{6,7},{7,6},{8,9},{9,8},{10,11... | collective-permute-start | bytes 540680 | tf_op jit(solution)/shard_map/ppermute | solution.py:46
  241.6 24.5 %collective-permute-start.41 = (bf16[2,64,1024]{2,1,0:T(8,128)(2,1)}, bf16[2,64,1024]{2,1,0:T(8,128)(2,1)}, u32[]{:S(2)}, u32[]{:S(2)}) collective-permute-start(bf16[2,64,1024]{2,1,0:T(8,128)(2,1)} %get-tuple-element.62), channel_id=1, source_target_pairs={{4,8},{6,10},{12,0},{14,2},{20,4},{22,6},{28,12},{30,14},{24,20},{... | collective-permute-start | bytes 786440 | tf_op jit(solution)/shard_map/ppermute | solution.py:596
  242.7 29.5 %collective-permute-start.42 = (bf16[2,64,1024]{2,1,0:T(8,128)(2,1)S(1)}, bf16[2,64,1024]{2,1,0:T(8,128)(2,1)}, u32[]{:S(2)}, u32[]{:S(2)}) collective-permute-start(bf16[2,64,1024]{2,1,0:T(8,128)(2,1)S(1)} %get-tuple-element.63), channel_id=1, source_target_pairs={{4,20},{6,22},{12,28},{14,30},{20,24},{22,26},{28,16},{30,18},{24,... | collective-permute-start | bytes 786440 | tf_op jit(solution)/shard_map/ppermute | solution.py:596
  252.3 26.4 %collective-permute-start.45 = (bf16[2,64,1024]{2,1,0:T(8,128)(2,1)}, bf16[2,64,1024]{2,1,0:T(8,128)(2,1)}, u32[]{:S(2)}, u32[]{:S(2)}) collective-permute-start(bf16[2,64,1024]{2,1,0:T(8,128)(2,1)} %get-tuple-element.66), channel_id=1, source_target_pairs={{4,16},{6,18},{12,8},{14,10},{20,0},{22,2},{28,4},{30,6},{24,12},{... | collective-permute-start | bytes 786440 | tf_op jit(solution)/shard_map/ppermute | solution.py:596
  254.4 24.3 %collective-permute-start.46 = (bf16[2,64,1024]{2,1,0:T(8,128)(2,1)S(1)}, bf16[2,64,1024]{2,1,0:T(8,128)(2,1)}, u32[]{:S(2)}, u32[]{:S(2)}) collective-permute-start(bf16[2,64,1024]{2,1,0:T(8,128)(2,1)S(1)} %get-tuple-element.67), channel_id=1, source_target_pairs={{4,28},{6,30},{12,24},{14,26},{20,16},{22,18},{28,8},{30,10},{24,0... | collective-permute-start | bytes 786440 | tf_op jit(solution)/shard_map/ppermute | solution.py:596
  263.0 19.2 %collective-permute-start.50 = (bf16[2,64,1024]{2,1,0:T(8,128)(2,1)S(1)}, bf16[2,64,1024]{2,1,0:T(8,128)(2,1)S(1)}, u32[]{:S(2)}, u32[]{:S(2)}) collective-permute-start(bf16[2,64,1024]{2,1,0:T(8,128)(2,1)S(1)} %expert_out.7), channel_id=1, source_target_pairs={{4,24},{6,26},{12,16},{14,18},{20,8},{22,10},{28,0},{30,2},{24,4},... | collective-permute-start | bytes 786440 | tf_op jit(solution)/shard_map/ppermute | solution.py:596
  (33 other events, 439.9 us)

commit v4 on v3

--- a/solution.py
+++ b/solution.py
@@ -177,6 +177,13 @@
 def project(attended, weights, places, residual, gain, router, experts):
     events, width = residual.shape
     tile = 256
+    count = len(attended)
+
+    def weight_map(i):
+        if weights[i].shape[1] > width:
+            return lambda j, m: (m[i], m[count] + j)
+        return lambda j, m: (m[i], j)
+
     return pl.pallas_call(
         functools.partial(project_kernel, len(attended), experts),
         grid_spec=pltpu.PrefetchScalarGridSpec(
@@ -184,7 +191,10 @@
             grid=(width // tile,),
             in_specs=[pl.BlockSpec(part.shape, lambda j, m: (0, 0)) for part in attended]
             + [
-                pl.BlockSpec((part.shape[1], tile), lambda j, m, i=i: (m[i], j))
+                pl.BlockSpec(
+                    (part.shape[1], tile),
+                    weight_map(i),
+                )
                 for i, part in enumerate(attended)
             ]
             + [
@@ -514,7 +524,7 @@
             half = 1 - core if other else core
             places.append(half * (local_heads // (end - first)) + first // (end - first))
     attended[0], fetched = barrier((attended[0], fetched))
-    out_weights = [columns_of(out_proj, my_head)] + fetched[::2]
+    out_weights = [out_proj] + fetched[::2]
     down_weights = [columns_of(w_down[0], my_head)]
     for s in shifts:
         down_weights.append(fetched[2 * s - 1])
@@ -526,7 +536,7 @@
     hidden, stat = project(
         attended,
         [out_weights[s] for s in weight_of],
-        jnp.stack(places),
+        jnp.stack(places + [my_head * (width // 256)]),
         residual_in[0],
         gain,
         wide_router,

time: 284 us -> 289 us (1.018)
    unnamed x61 -> x79, local copies, waits for them, and re-layouts: 12 us -> 12.5 us
  transfers between devices with their start and end apart: 51 -> 51, of which waited for: 25 -> 24; matrix products, arithmetic and copies ran while one was open for 6% -> 7% of each run, Pallas kernels for 27% -> 27%
where the time goes in v4:
time: 289 us; the launch traced here: 288 us
  waiting for transfers between devices  125 us (43%)
  Pallas kernels  77.8 us (27%)
  starting transfers between devices  51.7 us (18%)
  local copies, waits for them, and re-layouts  29 us (10%)
  other arithmetic  4.42 us (2%)
    ppermute x4, waiting for transfers between devices, local(): forth = lax.ppermute(forth, 'track', forward)  29.9 us
    pallas_call x4, Pallas kernels, expert_in(): pl.pallas_call(functools.partial(expert_in_kernel, sources, per_source),...  27.7 us
    ppermute x13, waiting for transfers between devices, shifted(): return lax.ppermute(x, axis, [(i, (i + shift) % size) for i in range(size)])  26.1 us
    ppermute x6, waiting for transfers between devices, local(): back[i] = lax.ppermute(back[i], 'track', backward)  23.4 us
    pallas_call x2, Pallas kernels, attention(): pl.pallas_call(functools.partial(attention_kernel, blocks), grid=(heads,)...  21.6 us
    ppermute x6, waiting for transfers between devices, local(): ahead[i] = lax.ppermute(ahead[i], 'track', forward)  17.6 us
    ppermute x13, starting transfers between devices, shifted(): return lax.ppermute(x, axis, [(i, (i + shift) % size) for i in range(size)])  13.6 us
    ppermute x7, waiting for transfers between devices, local(): returned.append(lax.ppermute(out, 'track', pairs) if hop_length else out)  12.8 us
  transfers between devices with their start and end apart: 51, of which 24 were waited for; matrix products, arithmetic and copies ran while one was open for 7% of the time, Pallas kernels for 27%

profile of v4, /device:TPU:0, one launch (start us, length us, event | category | flops | bytes accessed | tf_op | source)
XLA Modules:
  0.0 288.3 jit_solution(4935193792561399454)
XLA Ops:
  0.0 3.1 %constant_dynamic-slice_fusion = bf16[1024,1024]{1,0:T(8,128)(2,1)} fusion(bf16[1024,2048]{1,0:T(8,128)(2,1)} %refs_13_.1, s32[]{:T(128)S(6)} %select_n.134), kind=kLoop, calls=%fused_computation.58 | loop fusion | bytes 4194308 | tf_op jit(solution)/shard_map/dynamic_slice | solution.py:480
  3.2 3.0 %collective-permute-start.16 = (bf16[1024,1024]{1,0:T(8,128)(2,1)}, bf16[1024,1024]{1,0:T(8,128)(2,1)}, u32[]{:S(2)}, u32[]{:S(2)}) collective-permute-start(bf16[1024,1024]{1,0:T(8,128)(2,1)} %constant_dynamic-slice_fusion), channel_id=1, source_target_pairs={{0,1},{1,0},{2,3},{3,2},{4,5},{5,4},{6,7},{7,6},{8,9},{9,8},{10,11... | collective-permute-start | bytes 6291464 | tf_op jit(solution)/shard_map/ppermute | solution.py:46
  12.6 1.6 collective-permute-start.5
  15.7 7.1 %collective-permute-done.2.refs_5_ = bf16[2,256,512]{2,1,0:T(8,128)(2,1)} collective-permute-done((bf16[2,256,512]{2,1,0:T(8,128)(2,1)}, bf16[2,256,512]{2,1,0:T(8,128)(2,1)}, u32[]{:S(2)}, u32[]{:S(2)}) %collective-permute-start.2) | collective-permute-done | bytes 524320 | tf_op jit(solution)/shard_map/ppermute | solution.py:500
  24.2 10.6 %collective-permute-done.5.refs_8_ = bf16[2,256,512]{2,1,0:T(8,128)(2,1)} collective-permute-done((bf16[2,256,512]{2,1,0:T(8,128)(2,1)}, bf16[2,256,512]{2,1,0:T(8,128)(2,1)}, u32[]{:S(2)}, u32[]{:S(2)}) %collective-permute-start.5) | collective-permute-done | bytes 524320 | tf_op jit(solution)/shard_map/ppermute | solution.py:501
  36.7 3.9 %dynamic-slice_bitcast_fusion = (bf16[704,1024]{1,0:T(8,128)(2,1)}, bf16[704,1024]{1,0:T(8,128)(2,1)}) fusion(bf16[1,704,2048]{2,1,0:T(8,128)(2,1)} %param.30, s32[]{:T(128)S(6)} %select_n.141, s32[]{:T(128)S(6)} %select_n.134), kind=kLoop, calls=%fused_computation.5 | loop fusion | bytes 5767176 | tf_op jit(solution)/shard_map/dynamic_slice | solution.py:480
  40.7 1.6 collective-permute-start.8
  42.4 2.5 collective-permute-done.6.refs_9_
  46.3 3.7 %collective-permute-done.9.refs_12_ = bf16[2,256,512]{2,1,0:T(8,128)(2,1)} collective-permute-done((bf16[2,256,512]{2,1,0:T(8,128)(2,1)}, bf16[2,256,512]{2,1,0:T(8,128)(2,1)}, u32[]{:S(2)}, u32[]{:S(2)}) %collective-permute-start.9) | collective-permute-done | bytes 524320 | tf_op jit(solution)/shard_map/ppermute | solution.py:501
  50.0 1.6 collective-permute-start.10
  52.2 1.8 collective-permute-start.13
  58.5 2.7 collective-permute-done.8.refs_11_
  63.3 8.0 %collective-permute-done.10.refs_13_ = bf16[2,256,512]{2,1,0:T(8,128)(2,1)} collective-permute-done((bf16[2,256,512]{2,1,0:T(8,128)(2,1)}, bf16[2,256,512]{2,1,0:T(8,128)(2,1)}, u32[]{:S(2)}, u32[]{:S(2)}) %collective-permute-start.10) | collective-permute-done | bytes 524320 | tf_op jit(solution)/shard_map/ppermute | solution.py:500
  73.5 1.7 pad.8.refs_18_
  77.2 6.5 %collective-permute-done.12.refs_15_ = bf16[2,256,512]{2,1,0:T(8,128)(2,1)} collective-permute-done((bf16[2,256,512]{2,1,0:T(8,128)(2,1)}, bf16[2,256,512]{2,1,0:T(8,128)(2,1)}, u32[]{:S(2)}, u32[]{:S(2)}) %collective-permute-start.12) | collective-permute-done | bytes 524320 | tf_op jit(solution)/shard_map/ppermute | solution.py:501
  83.7 8.7 %collective-permute-done.14.refs_17_ = bf16[2,256,512]{2,1,0:T(8,128)(2,1)} collective-permute-done((bf16[2,256,512]{2,1,0:T(8,128)(2,1)}, bf16[2,256,512]{2,1,0:T(8,128)(2,1)}, u32[]{:S(2)}, u32[]{:S(2)}) %collective-permute-start.14) | collective-permute-done | bytes 524320 | tf_op jit(solution)/shard_map/ppermute | solution.py:503
  93.3 10.7 %attention.3 = (bf16[256,256]{1,0:T(8,128)(2,1)S(1)}, bf16[256,256]{1,0:T(8,128)(2,1)S(1)}) custom-call(bf16[2,256,512]{2,1,0:T(8,128)(2,1)S(1)} %constant_dynamic-update-slice_fusion.refs_0_, s32[2,256,16]{2,1,0:T(8,128)S(1)} %bitcast_select_fusion.refs_1_, s32[16,256]{1,0:T(8,128)S(1)} %gather_fusion.3, bf16[2,256,512]{2,1,0:T(8,128)(2,1)} %get-tuple-element.40.refs_3_, ...), custom_call_target="tpu_custom_call" | custom-call | flops 2147483648 | bytes 4194304 | tf_op jit(solution)/shard_map/attention/pallas_call | solution.py:126
  106.3 10.8 %attention.2 = (bf16[256,256]{1,0:T(8,128)(2,1)S(1)}, bf16[256,256]{1,0:T(8,128)(2,1)S(1)}) custom-call(bf16[2,256,512]{2,1,0:T(8,128)(2,1)S(1)} %constant_dynamic-update-slice_fusion.refs_0_, s32[2,256,16]{2,1,0:T(8,128)S(1)} %bitcast_select_fusion.refs_1_, s32[16,256]{1,0:T(8,128)S(1)} %gather_fusion.3, bf16[2,256,512]{2,1,0:T(8,128)(2,1)} %get-tuple-element.40.refs_3_, ...), custom_call_target="tpu_custom_call" | custom-call | flops 2147483648 | bytes 4194304 | tf_op jit(solution)/shard_map/attention/pallas_call | solution.py:126
  119.5 2.9 collective-permute-done.18.refs_1_
  122.3 4.0 %collective-permute-done.19.refs_2_ = bf16[256,256]{1,0:T(8,128)(2,1)S(1)} collective-permute-done((bf16[256,256]{1,0:T(8,128)(2,1)S(1)}, bf16[256,256]{1,0:T(8,128)(2,1)S(1)}, u32[]{:S(2)}, u32[]{:S(2)}) %collective-permute-start.19) | collective-permute-done | bytes 131104 | tf_op jit(solution)/shard_map/ppermute | solution.py:46
  126.4 5.3 %project.1 = (bf16[256,1024]{1,0:T(8,128)(2,1)S(1)}, f32[256,128]{1,0:T(8,128)S(1)}) custom-call(s32[9]{0:T(128)S(1)} %stack.66.place_ref, bf16[256,256]{1,0:T(8,128)(2,1)S(1)} %get-tuple-element.45.refs_0_, bf16[256,256]{1,0:T(8,128)(2,1)S(1)} %collective-permute-done.18.refs_1_, bf16[256,256]{1,0:T(8,128)(2,1)S(1)} %collective-permute-done.19.refs_2_, ...), custom_call_target="tpu_custom_call" | custom-call | flops 1073741824 | bytes 4194304 | tf_op jit(solution)/shard_map/project/pallas_call | solution.py:187
  133.4 4.3 %collective-permute-done.24.refs_2_ = f32[256,128]{1,0:T(8,128)S(1)} collective-permute-done((f32[256,128]{1,0:T(8,128)S(1)}, f32[256,128]{1,0:T(8,128)S(1)}, u32[]{:S(2)}, u32[]{:S(2)}) %collective-permute-start.24) | collective-permute-done | bytes 131104 | tf_op jit(solution)/shard_map/ppermute | solution.py:46
  139.9 1.6 collective-permute-start.25
  141.9 11.5 %collective-permute-done.25.refs_1_ = bf16[272,1024]{1,0:T(8,128)(2,1)S(1)} collective-permute-done((bf16[272,1024]{1,0:T(8,128)(2,1)S(1)}, bf16[272,1024]{1,0:T(8,128)(2,1)S(1)}, u32[]{:S(2)}, u32[]{:S(2)}) %collective-permute-start.25) | collective-permute-done | bytes 557088 | tf_op jit(solution)/shard_map/ppermute | solution.py:576
  156.4 9.6 %collective-permute-done.26.refs_0_ = bf16[272,1024]{1,0:T(8,128)(2,1)S(1)} collective-permute-done((bf16[272,1024]{1,0:T(8,128)(2,1)S(1)}, bf16[272,1024]{1,0:T(8,128)(2,1)S(1)}, u32[]{:S(2)}, u32[]{:S(2)}) %collective-permute-start.26) | collective-permute-done | bytes 557088 | tf_op jit(solution)/shard_map/ppermute | solution.py:576
  167.3 1.6 collective-permute-start.37
  169.8 8.8 %collective-permute-done.37.refs_0_ = bf16[272,1024]{1,0:T(8,128)(2,1)S(1)} collective-permute-done((bf16[272,1024]{1,0:T(8,128)(2,1)S(1)}, bf16[272,1024]{1,0:T(8,128)(2,1)S(1)}, u32[]{:S(2)}, u32[]{:S(2)}) %collective-permute-start.37) | collective-permute-done | bytes 557088 | tf_op jit(solution)/shard_map/ppermute | solution.py:576
  181.4 1.6 collective-permute-start.47
  183.0 3.0 %collective-permute-done.29.refs_1_ = bf16[2,192,1024]{2,1,0:T(8,128)(2,1)S(1)} collective-permute-done((bf16[2,192,1024]{2,1,0:T(8,128)(2,1)S(1)}, bf16[2,192,1024]{2,1,0:T(8,128)(2,1)S(1)}, u32[]{:S(2)}, u32[]{:S(2)}) %collective-permute-start.29) | collective-permute-done | bytes 786464 | tf_op jit(solution)/shard_map/ppermute | solution.py:46
  186.0 6.8 %expert_in.4.refs_0_ = bf16[2,192,704]{2,1,0:T(8,128)(2,1)S(1)} custom-call(s32[2]{0:T(128)S(1)} %and_select_fusion.kmap_ref, bf16[2,192,1024]{2,1,0:T(8,128)(2,1)S(1)} %select.52.refs_0_, bf16[2,192,1024]{2,1,0:T(8,128)(2,1)S(1)} %collective-permute-done.29.refs_1_, bf16[1,704,2048]{2,1,0:T(8,128)(2,1)S(1)} %bitcast.58, ...), custom_call_target="tpu_custom_call" | custom-call | flops 2214592512 | bytes 11534336 | tf_op jit(solution)/shard_map/expert_in/pallas_call | solution.py:338
  194.2 3.0 %collective-permute-done.39.refs_1_ = bf16[2,128,1024]{2,1,0:T(8,128)(2,1)S(1)} collective-permute-done((bf16[2,128,1024]{2,1,0:T(8,128)(2,1)S(1)}, bf16[2,128,1024]{2,1,0:T(8,128)(2,1)S(1)}, u32[]{:S(2)}, u32[]{:S(2)}) %collective-permute-start.39) | collective-permute-done | bytes 524320 | tf_op jit(solution)/shard_map/ppermute | solution.py:46
  197.8 6.8 %expert_in.5.refs_0_ = bf16[2,128,704]{2,1,0:T(8,128)(2,1)S(1)} custom-call(s32[2]{0:T(128)S(1)} %and_select_fusion.kmap_ref, bf16[2,128,1024]{2,1,0:T(8,128)(2,1)S(1)} %select.53.refs_0_, bf16[2,128,1024]{2,1,0:T(8,128)(2,1)S(1)} %collective-permute-done.39.refs_1_, bf16[1,704,2048]{2,1,0:T(8,128)(2,1)S(1)} %bitcast.59, ...), custom_call_target="tpu_custom_call" | custom-call | flops 1476395008 | bytes 11534336 | tf_op jit(solution)/shard_map/expert_in/pallas_call | solution.py:338
  204.6 1.6 collective-permute-start.40
  207.6 2.3 collective-permute-done.32.refs_1_
  209.9 3.5 %expert_out.4 = (bf16[2,64,1024]{2,1,0:T(8,128)(2,1)S(1)}, bf16[2,64,1024]{2,1,0:T(8,128)(2,1)}, bf16[2,64,1024]{2,1,0:T(8,128)(2,1)}) custom-call(bf16[2,192,704]{2,1,0:T(8,128)(2,1)S(1)} %expert_in.4.refs_0_, bf16[2,192,704]{2,1,0:T(8,128)(2,1)S(1)} %collective-permute-done.32.refs_1_, bf16[704,1024]{1,0:T(8,128)(2,1)S(1)} %copy-done.3, ...), custom_call_target="tpu_custom_call" | custom-call | flops 1107296256 | bytes 5767168 | tf_op jit(solution)/shard_map/expert_out/pallas_call | solution.py:378
  213.4 7.7 %collective-permute-done.43.refs_1_ = bf16[2,128,1024]{2,1,0:T(8,128)(2,1)S(1)} collective-permute-done((bf16[2,128,1024]{2,1,0:T(8,128)(2,1)S(1)}, bf16[2,128,1024]{2,1,0:T(8,128)(2,1)S(1)}, u32[]{:S(2)}, u32[]{:S(2)}) %collective-permute-start.43) | collective-permute-done | bytes 524320 | tf_op jit(solution)/shard_map/ppermute | solution.py:46
  221.1 6.8 %expert_in.6.refs_0_ = bf16[2,128,704]{2,1,0:T(8,128)(2,1)S(1)} custom-call(s32[2]{0:T(128)S(1)} %and_select_fusion.kmap_ref, bf16[2,128,1024]{2,1,0:T(8,128)(2,1)S(1)} %select.54.refs_0_, bf16[2,128,1024]{2,1,0:T(8,128)(2,1)S(1)} %collective-permute-done.43.refs_1_, bf16[1,704,2048]{2,1,0:T(8,128)(2,1)S(1)} %bitcast.60, ...), custom_call_target="tpu_custom_call" | custom-call | flops 1476395008 | bytes 11534336 | tf_op jit(solution)/shard_map/expert_in/pallas_call | solution.py:338
  229.8 1.6 collective-permute-start.36
  231.4 2.7 expert_out.5
  235.2 7.3 %expert_in.7.refs_0_ = bf16[2,64,704]{2,1,0:T(8,128)(2,1)} custom-call(s32[2]{0:T(128)S(1)} %and_select_fusion.kmap_ref, bf16[2,64,1024]{2,1,0:T(8,128)(2,1)S(1)} %select.55.refs_0_, bf16[2,64,1024]{2,1,0:T(8,128)(2,1)S(1)} %collective-permute-done.48.refs_1_, bf16[1,704,2048]{2,1,0:T(8,128)(2,1)S(1)} %bitcast.61, bf16[1,704,2048]{2,1,0:T(8,128)(2,1)} %bitcast.24.refs_3_, ...), custom_call_target="tpu_custom_call" | custom-call | flops 738197504 | bytes 11534336 | tf_op jit(solution)/shard_map/expert_in/pallas_call | solution.py:338
  245.7 2.4 collective-permute-start.42
  252.1 3.3 %expert_out.6 = (bf16[2,64,1024]{2,1,0:T(8,128)(2,1)}, bf16[2,64,1024]{2,1,0:T(8,128)(2,1)}) custom-call(bf16[2,128,704]{2,1,0:T(8,128)(2,1)S(1)} %expert_in.6.refs_0_, bf16[2,128,704]{2,1,0:T(8,128)(2,1)} %collective-permute-done.44.refs_1_, bf16[704,1024]{1,0:T(8,128)(2,1)S(1)} %copy-done.4, bf16[704,1024]{1,0:T(8,128)(2,1)} %collective-permute-done.17.refs_3_, ...), custom_call_target="tpu_custom_call" | custom-call | flops 738197504 | bytes 5767168 | tf_op jit(solution)/shard_map/expert_out/pallas_call | solution.py:378
  255.5 2.1 collective-permute-start.45
  257.5 1.8 collective-permute-start.46
  261.6 3.2 %expert_out.7 = bf16[2,64,1024]{2,1,0:T(8,128)(2,1)} custom-call(bf16[2,64,704]{2,1,0:T(8,128)(2,1)} %expert_in.7.refs_0_, bf16[2,64,704]{2,1,0:T(8,128)(2,1)} %collective-permute-done.49.refs_1_, bf16[704,1024]{1,0:T(8,128)(2,1)S(1)} %copy-done.5, bf16[704,1024]{1,0:T(8,128)(2,1)} %collective-permute-done.17.refs_3_, bf16[704,1024]{1,0:T(8,128)(2,1)S(1)} %copy-done.8, ...), custom_call_target="tpu_custom_call" | custom-call | flops 369098752 | bytes 5767168 | tf_op jit(solution)/shard_map/expert_out/pallas_call | solution.py:378
  264.9 2.9 %collective-permute-start.50 = (bf16[2,64,1024]{2,1,0:T(8,128)(2,1)}, bf16[2,64,1024]{2,1,0:T(8,128)(2,1)S(1)}, u32[]{:S(2)}, u32[]{:S(2)}) collective-permute-start(bf16[2,64,1024]{2,1,0:T(8,128)(2,1)} %expert_out.7), channel_id=1, source_target_pairs={{4,24},{6,26},{12,16},{14,18},{20,8},{22,10},{28,0},{30,2},{24,4},... | collective-permute-start | bytes 786440 | tf_op jit(solution)/shard_map/ppermute | solution.py:606
  268.9 12.8 %collective-permute-done.45.refs_5_ = bf16[2,64,1024]{2,1,0:T(8,128)(2,1)} collective-permute-done((bf16[2,64,1024]{2,1,0:T(8,128)(2,1)}, bf16[2,64,1024]{2,1,0:T(8,128)(2,1)}, u32[]{:S(2)}, u32[]{:S(2)}) %collective-permute-start.45) | collective-permute-done | bytes 262176 | tf_op jit(solution)/shard_map/ppermute | solution.py:606
  283.5 3.5 %combine.2.base_ref = f32[256,1024]{1,0:T(8,128)S(1)} custom-call(bf16[256,1024]{1,0:T(8,128)(2,1)S(1)} %copy-done.16, f32[256,128]{1,0:T(8,128)S(1)} %copy-done.21, s32[256,2]{1,0:T(8,128)S(1)} %add.207.code_ref, bf16[2,64,1024]{2,1,0:T(8,128)(2,1)S(1)} %copy-done.23, bf16[2,64,1024]{2,1,0:T(8,128)(2,1)} %collective-permute-done.35.refs_1_, ...), custom_call_target="tpu_custom_call" | custom-call | flops 939524096 | bytes 1835008 | tf_op jit(solution)/shard_map/combine/pallas_call | solution.py:415
  (209 shorter events, 62.0 us)
Async XLA Ops:
  3.2 49.0 %collective-permute-start.16 = (bf16[1024,1024]{1,0:T(8,128)(2,1)}, bf16[1024,1024]{1,0:T(8,128)(2,1)}, u32[]{:S(2)}, u32[]{:S(2)}) collective-permute-start(bf16[1024,1024]{1,0:T(8,128)(2,1)} %constant_dynamic-slice_fusion), channel_id=1, source_target_pairs={{0,1},{1,0},{2,3},{3,2},{4,5},{5,4},{6,7},{7,6},{8,9},{9,8},{10,11... | collective-permute-start | bytes 6291464 | tf_op jit(solution)/shard_map/ppermute | solution.py:46
  7.7 15.0 %collective-permute-start.2 = (bf16[2,256,512]{2,1,0:T(8,128)(2,1)}, bf16[2,256,512]{2,1,0:T(8,128)(2,1)}, u32[]{:S(2)}, u32[]{:S(2)}) collective-permute-start(bf16[2,256,512]{2,1,0:T(8,128)(2,1)} %get-tuple-element.40.refs_3_), channel_id=1, source_target_pairs={{4,12},{6,14},{12,20},{14,22},{20,28},{22,30},{28,24},{30,26},{24,... | collective-permute-start | bytes 1572872 | tf_op jit(solution)/shard_map/ppermute | solution.py:500
  9.2 31.3 %collective-permute-start.4 = (bf16[2,256,512]{2,1,0:T(8,128)(2,1)}, bf16[2,256,512]{2,1,0:T(8,128)(2,1)}, u32[]{:S(2)}, u32[]{:S(2)}) collective-permute-start(bf16[2,256,512]{2,1,0:T(8,128)(2,1)} %get-tuple-element.40.refs_3_), channel_id=1, source_target_pairs={{12,4},{14,6},{20,12},{22,14},{28,20},{30,22},{24,28},{26,30},{16,... | collective-permute-start | bytes 1572872 | tf_op jit(solution)/shard_map/ppermute | solution.py:501
  12.6 22.3 %collective-permute-start.5 = (bf16[2,256,512]{2,1,0:T(8,128)(2,1)}, bf16[2,256,512]{2,1,0:T(8,128)(2,1)}, u32[]{:S(2)}, u32[]{:S(2)}) collective-permute-start(bf16[2,256,512]{2,1,0:T(8,128)(2,1)} %collective-permute-done.1.refs_4_), channel_id=1, source_target_pairs={{12,4},{14,6},{20,12},{22,14},{28,20},{30,22},{24,28},{26,30},{16,... | collective-permute-start | bytes 1572872 | tf_op jit(solution)/shard_map/ppermute | solution.py:501
  15.2 25.6 %collective-permute-start.3 = (bf16[2,256,512]{2,1,0:T(8,128)(2,1)}, bf16[2,256,512]{2,1,0:T(8,128)(2,1)}, u32[]{:S(2)}, u32[]{:S(2)}) collective-permute-start(bf16[2,256,512]{2,1,0:T(8,128)(2,1)} %collective-permute-done.1.refs_4_), channel_id=1, source_target_pairs={{4,12},{6,14},{12,20},{14,22},{20,28},{22,30},{28,24},{30,26},{24,... | collective-permute-start | bytes 1572872 | tf_op jit(solution)/shard_map/ppermute | solution.py:500
  22.8 22.1 %collective-permute-start.6 = (bf16[2,256,512]{2,1,0:T(8,128)(2,1)}, bf16[2,256,512]{2,1,0:T(8,128)(2,1)}, u32[]{:S(2)}, u32[]{:S(2)}) collective-permute-start(bf16[2,256,512]{2,1,0:T(8,128)(2,1)} %collective-permute-done.2.refs_5_), channel_id=1, source_target_pairs={{4,12},{6,14},{12,20},{14,22},{20,28},{22,30},{28,24},{30,26},{24,... | collective-permute-start | bytes 1572872 | tf_op jit(solution)/shard_map/ppermute | solution.py:500
  34.8 15.2 %collective-permute-start.9 = (bf16[2,256,512]{2,1,0:T(8,128)(2,1)}, bf16[2,256,512]{2,1,0:T(8,128)(2,1)}, u32[]{:S(2)}, u32[]{:S(2)}) collective-permute-start(bf16[2,256,512]{2,1,0:T(8,128)(2,1)} %collective-permute-done.5.refs_8_), channel_id=1, source_target_pairs={{12,4},{14,6},{20,12},{22,14},{28,20},{30,22},{24,28},{26,30},{16,... | collective-permute-start | bytes 1572872 | tf_op jit(solution)/shard_map/ppermute | solution.py:501
  40.5 13.4 %collective-permute-start = (bf16[1,256,512]{2,1,0:T(8,128)(2,1)S(1)}, bf16[1,256,512]{2,1,0:T(8,128)(2,1)}, u32[]{:S(2)}, u32[]{:S(2)}) collective-permute-start(bf16[1,256,512]{2,1,0:T(8,128)(2,1)S(1)} %get-tuple-element.39), channel_id=1, source_target_pairs={{0,2},{2,0},{4,6},{6,4},{8,10},{10,8},{12,14},{14,12},{16,18},{18,... | collective-permute-start | bytes 786440 | tf_op jit(solution)/shard_map/ppermute | solution.py:50
  40.7 20.5 %collective-permute-start.8 = (bf16[2,256,512]{2,1,0:T(8,128)(2,1)}, bf16[2,256,512]{2,1,0:T(8,128)(2,1)}, u32[]{:S(2)}, u32[]{:S(2)}) collective-permute-start(bf16[2,256,512]{2,1,0:T(8,128)(2,1)} %collective-permute-done.4.refs_7_), channel_id=1, source_target_pairs={{12,4},{14,6},{20,12},{22,14},{28,20},{30,22},{24,28},{26,30},{16,... | collective-permute-start | bytes 1572872 | tf_op jit(solution)/shard_map/ppermute | solution.py:501
  44.8 16.9 %collective-permute-start.7 = (bf16[2,256,512]{2,1,0:T(8,128)(2,1)}, bf16[2,256,512]{2,1,0:T(8,128)(2,1)}, u32[]{:S(2)}, u32[]{:S(2)}) collective-permute-start(bf16[2,256,512]{2,1,0:T(8,128)(2,1)} %collective-permute-done.3.refs_6_), channel_id=1, source_target_pairs={{4,12},{6,14},{12,20},{14,22},{20,28},{22,30},{28,24},{30,26},{24,... | collective-permute-start | bytes 1572872 | tf_op jit(solution)/shard_map/ppermute | solution.py:500
  50.0 21.2 %collective-permute-start.10 = (bf16[2,256,512]{2,1,0:T(8,128)(2,1)}, bf16[2,256,512]{2,1,0:T(8,128)(2,1)}, u32[]{:S(2)}, u32[]{:S(2)}) collective-permute-start(bf16[2,256,512]{2,1,0:T(8,128)(2,1)} %collective-permute-done.6.refs_9_), channel_id=1, source_target_pairs={{4,12},{6,14},{12,20},{14,22},{20,28},{22,30},{28,24},{30,26},{24,... | collective-permute-start | bytes 1572872 | tf_op jit(solution)/shard_map/ppermute | solution.py:500
  52.2 20.5 %collective-permute-start.13 = (bf16[2,256,512]{2,1,0:T(8,128)(2,1)}, bf16[2,256,512]{2,1,0:T(8,128)(2,1)}, u32[]{:S(2)}, u32[]{:S(2)}) collective-permute-start(bf16[2,256,512]{2,1,0:T(8,128)(2,1)} %collective-permute-done.9.refs_12_), channel_id=1, source_target_pairs={{12,4},{14,6},{20,12},{22,14},{28,20},{30,22},{24,28},{26,30},{16,... | collective-permute-start | bytes 1572872 | tf_op jit(solution)/shard_map/ppermute | solution.py:501
  54.0 63.9 %collective-permute-start.17 = (bf16[704,1024]{1,0:T(8,128)(2,1)}, bf16[704,1024]{1,0:T(8,128)(2,1)}, u32[]{:S(2)}, u32[]{:S(2)}) collective-permute-start(bf16[704,1024]{1,0:T(8,128)(2,1)} %get-tuple-element.44), channel_id=1, source_target_pairs={{0,1},{1,0},{2,3},{3,2},{4,5},{5,4},{6,7},{7,6},{8,9},{9,8},{10,11... | collective-permute-start | bytes 4325384 | tf_op jit(solution)/shard_map/ppermute | solution.py:46
  61.2 22.5 %collective-permute-start.12 = (bf16[2,256,512]{2,1,0:T(8,128)(2,1)}, bf16[2,256,512]{2,1,0:T(8,128)(2,1)}, u32[]{:S(2)}, u32[]{:S(2)}) collective-permute-start(bf16[2,256,512]{2,1,0:T(8,128)(2,1)} %collective-permute-done.8.refs_11_), channel_id=1, source_target_pairs={{12,4},{14,6},{20,12},{22,14},{28,20},{30,22},{24,28},{26,30},{16,... | collective-permute-start | bytes 1572872 | tf_op jit(solution)/shard_map/ppermute | solution.py:501
  61.8 21.9 %collective-permute-start.11 = (bf16[2,256,512]{2,1,0:T(8,128)(2,1)}, bf16[2,256,512]{2,1,0:T(8,128)(2,1)}, u32[]{:S(2)}, u32[]{:S(2)}) collective-permute-start(bf16[2,256,512]{2,1,0:T(8,128)(2,1)} %collective-permute-done.7.refs_10_), channel_id=1, source_target_pairs={{4,12},{6,14},{12,20},{14,22},{20,28},{22,30},{28,24},{30,26},{24,... | collective-permute-start | bytes 1572872 | tf_op jit(solution)/shard_map/ppermute | solution.py:500
  71.2 21.2 %collective-permute-start.14 = (bf16[2,256,512]{2,1,0:T(8,128)(2,1)}, bf16[2,256,512]{2,1,0:T(8,128)(2,1)}, u32[]{:S(2)}, u32[]{:S(2)}) collective-permute-start(bf16[2,256,512]{2,1,0:T(8,128)(2,1)} %collective-permute-done.10.refs_13_), channel_id=1, source_target_pairs={{4,12},{6,14},{12,20},{14,22},{20,28},{22,30},{28,24},{30,26},{24,... | collective-permute-start | bytes 1572872 | tf_op jit(solution)/shard_map/ppermute | solution.py:503
  72.7 20.6 %collective-permute-start.15 = (bf16[2,256,512]{2,1,0:T(8,128)(2,1)}, bf16[2,256,512]{2,1,0:T(8,128)(2,1)}, u32[]{:S(2)}, u32[]{:S(2)}) collective-permute-start(bf16[2,256,512]{2,1,0:T(8,128)(2,1)} %collective-permute-done.13.refs_16_), channel_id=1, source_target_pairs={{12,4},{14,6},{20,12},{22,14},{28,20},{30,22},{24,28},{26,30},{16,... | collective-permute-start | bytes 1572872 | tf_op jit(solution)/shard_map/ppermute | solution.py:504
  83.7 97.1 %collective-permute-start.30 = (bf16[1,704,2048]{2,1,0:T(8,128)(2,1)S(1)}, bf16[1,704,2048]{2,1,0:T(8,128)(2,1)}, u32[]{:S(2)}, u32[]{:S(2)}) collective-permute-start(bf16[1,704,2048]{2,1,0:T(8,128)(2,1)S(1)} %bitcast.57), channel_id=1, source_target_pairs={{0,2},{2,0},{4,6},{6,4},{8,10},{10,8},{12,14},{14,12},{16,18},{18,... | collective-permute-start | bytes 8650760 | tf_op jit(solution)/shard_map/ppermute | solution.py:50
  104.1 13.1 %collective-permute-start.21 = (bf16[256,256]{1,0:T(8,128)(2,1)S(1)}, bf16[256,256]{1,0:T(8,128)(2,1)S(1)}, u32[]{:S(2)}, u32[]{:S(2)}) collective-permute-start(bf16[256,256]{1,0:T(8,128)(2,1)S(1)} %get-tuple-element.48), channel_id=1, source_target_pairs={{0,2},{2,0},{4,6},{6,4},{8,10},{10,8},{12,14},{14,12},{16,18},{18,... | collective-permute-start | bytes 393224 | tf_op jit(solution)/shard_map/ppermute | solution.py:50
  104.1 13.6 %collective-permute-start.23 = (bf16[256,256]{1,0:T(8,128)(2,1)S(1)}, bf16[256,256]{1,0:T(8,128)(2,1)S(1)}, u32[]{:S(2)}, u32[]{:S(2)}) collective-permute-start(bf16[256,256]{1,0:T(8,128)(2,1)S(1)} %get-tuple-element.48), channel_id=1, source_target_pairs={{0,3},{1,2},{2,1},{3,0},{4,7},{5,6},{6,5},{7,4},{8,11},{9,10},{10,... | collective-permute-start | bytes 393224 | tf_op jit(solution)/shard_map/ppermute | solution.py:520
  104.8 12.5 %collective-permute-start.22 = (bf16[256,256]{1,0:T(8,128)(2,1)S(1)}, bf16[256,256]{1,0:T(8,128)(2,1)S(1)}, u32[]{:S(2)}, u32[]{:S(2)}) collective-permute-start(bf16[256,256]{1,0:T(8,128)(2,1)S(1)} %get-tuple-element.47.refs_4_), channel_id=1, source_target_pairs={{0,1},{1,0},{2,3},{3,2},{4,5},{5,4},{6,7},{7,6},{8,9},{9,8},{10,11... | collective-permute-start | bytes 393224 | tf_op jit(solution)/shard_map/ppermute | solution.py:46
  117.1 64.3 %collective-permute-start.31 = (bf16[1,704,2048]{2,1,0:T(8,128)(2,1)}, bf16[1,704,2048]{2,1,0:T(8,128)(2,1)}, u32[]{:S(2)}, u32[]{:S(2)}) collective-permute-start(bf16[1,704,2048]{2,1,0:T(8,128)(2,1)} %bitcast.24.refs_3_), channel_id=1, source_target_pairs={{0,2},{2,0},{4,6},{6,4},{8,10},{10,8},{12,14},{14,12},{16,18},{18,... | collective-permute-start | bytes 8650760 | tf_op jit(solution)/shard_map/ppermute | solution.py:50
  117.7 8.6 %collective-permute-start.20 = (bf16[256,256]{1,0:T(8,128)(2,1)S(1)}, bf16[256,256]{1,0:T(8,128)(2,1)S(1)}, u32[]{:S(2)}, u32[]{:S(2)}) collective-permute-start(bf16[256,256]{1,0:T(8,128)(2,1)S(1)} %get-tuple-element.46), channel_id=1, source_target_pairs={{0,3},{1,2},{2,1},{3,0},{4,7},{5,6},{6,5},{7,4},{8,11},{9,10},{10,... | collective-permute-start | bytes 393224 | tf_op jit(solution)/shard_map/ppermute | solution.py:520
  117.9 8.4 %collective-permute-start.19 = (bf16[256,256]{1,0:T(8,128)(2,1)S(1)}, bf16[256,256]{1,0:T(8,128)(2,1)S(1)}, u32[]{:S(2)}, u32[]{:S(2)}) collective-permute-start(bf16[256,256]{1,0:T(8,128)(2,1)S(1)} %get-tuple-element.45.refs_0_), channel_id=1, source_target_pairs={{0,1},{1,0},{2,3},{3,2},{4,5},{5,4},{6,7},{7,6},{8,9},{9,8},{10,11... | collective-permute-start | bytes 393224 | tf_op jit(solution)/shard_map/ppermute | solution.py:46
  139.9 13.5 %collective-permute-start.25 = (bf16[272,1024]{1,0:T(8,128)(2,1)S(1)}, bf16[272,1024]{1,0:T(8,128)(2,1)S(1)}, u32[]{:S(2)}, u32[]{:S(2)}) collective-permute-start(bf16[272,1024]{1,0:T(8,128)(2,1)S(1)} %get-tuple-element.53.refs_0_), channel_id=1, source_target_pairs={{4,12},{6,14},{12,20},{14,22},{20,28},{22,30},{28,24},{30,26},{24,... | collective-permute-start | bytes 1671176 | tf_op jit(solution)/shard_map/ppermute | solution.py:576
  141.5 13.5 %collective-permute-start.27 = (bf16[272,1024]{1,0:T(8,128)(2,1)S(1)}, bf16[272,1024]{1,0:T(8,128)(2,1)S(1)}, u32[]{:S(2)}, u32[]{:S(2)}) collective-permute-start(bf16[272,1024]{1,0:T(8,128)(2,1)S(1)} %get-tuple-element.53.refs_0_), channel_id=1, source_target_pairs={{12,4},{14,6},{20,12},{22,14},{28,20},{30,22},{24,28},{26,30},{16,... | collective-permute-start | bytes 1671176 | tf_op jit(solution)/shard_map/ppermute | solution.py:579
  153.4 12.6 %collective-permute-start.26 = (bf16[272,1024]{1,0:T(8,128)(2,1)S(1)}, bf16[272,1024]{1,0:T(8,128)(2,1)S(1)}, u32[]{:S(2)}, u32[]{:S(2)}) collective-permute-start(bf16[272,1024]{1,0:T(8,128)(2,1)S(1)} %collective-permute-done.25.refs_1_), channel_id=1, source_target_pairs={{4,12},{6,14},{12,20},{14,22},{20,28},{22,30},{28,24},{30,26},{24,... | collective-permute-start | bytes 1671176 | tf_op jit(solution)/shard_map/ppermute | solution.py:576
  155.0 12.3 %collective-permute-start.28 = (bf16[272,1024]{1,0:T(8,128)(2,1)S(1)}, bf16[272,1024]{1,0:T(8,128)(2,1)S(1)}, u32[]{:S(2)}, u32[]{:S(2)}) collective-permute-start(bf16[272,1024]{1,0:T(8,128)(2,1)S(1)} %collective-permute-done.27.refs_2_), channel_id=1, source_target_pairs={{12,4},{14,6},{20,12},{22,14},{28,20},{30,22},{24,28},{26,30},{16,... | collective-permute-start | bytes 1671176 | tf_op jit(solution)/shard_map/ppermute | solution.py:579
  167.3 11.4 %collective-permute-start.37 = (bf16[272,1024]{1,0:T(8,128)(2,1)S(1)}, bf16[272,1024]{1,0:T(8,128)(2,1)S(1)}, u32[]{:S(2)}, u32[]{:S(2)}) collective-permute-start(bf16[272,1024]{1,0:T(8,128)(2,1)S(1)} %collective-permute-done.26.refs_0_), channel_id=1, source_target_pairs={{4,12},{6,14},{12,20},{14,22},{20,28},{22,30},{28,24},{30,26},{24,... | collective-permute-start | bytes 1671176 | tf_op jit(solution)/shard_map/ppermute | solution.py:576
  168.9 11.1 %collective-permute-start.38 = (bf16[272,1024]{1,0:T(8,128)(2,1)S(1)}, bf16[272,1024]{1,0:T(8,128)(2,1)S(1)}, u32[]{:S(2)}, u32[]{:S(2)}) collective-permute-start(bf16[272,1024]{1,0:T(8,128)(2,1)S(1)} %collective-permute-done.28.refs_1_), channel_id=1, source_target_pairs={{12,4},{14,6},{20,12},{22,14},{28,20},{30,22},{24,28},{26,30},{16,... | collective-permute-start | bytes 1671176 | tf_op jit(solution)/shard_map/ppermute | solution.py:579
  169.3 16.7 %collective-permute-start.29 = (bf16[2,192,1024]{2,1,0:T(8,128)(2,1)S(1)}, bf16[2,192,1024]{2,1,0:T(8,128)(2,1)S(1)}, u32[]{:S(2)}, u32[]{:S(2)}) collective-permute-start(bf16[2,192,1024]{2,1,0:T(8,128)(2,1)S(1)} %select.52.refs_0_), channel_id=1, source_target_pairs={{0,1},{1,0},{2,3},{3,2},{4,5},{5,4},{6,7},{7,6},{8,9},{9,8},{10,11... | collective-permute-start | bytes 2359304 | tf_op jit(solution)/shard_map/ppermute | solution.py:46
  178.7 28.3 %collective-permute-start.33 = (bf16[704,1024]{1,0:T(8,128)(2,1)S(1)}, bf16[704,1024]{1,0:T(8,128)(2,1)S(1)}, u32[]{:S(2)}, u32[]{:S(2)}) collective-permute-start(bf16[704,1024]{1,0:T(8,128)(2,1)S(1)} %copy-done.3), channel_id=1, source_target_pairs={{0,2},{2,0},{4,6},{6,4},{8,10},{10,8},{12,14},{14,12},{16,18},{18,... | collective-permute-start | bytes 4325384 | tf_op jit(solution)/shard_map/ppermute | solution.py:50
  180.0 27.6 %collective-permute-start.34 = (bf16[704,1024]{1,0:T(8,128)(2,1)}, bf16[704,1024]{1,0:T(8,128)(2,1)S(1)}, u32[]{:S(2)}, u32[]{:S(2)}) collective-permute-start(bf16[704,1024]{1,0:T(8,128)(2,1)} %collective-permute-done.17.refs_3_), channel_id=1, source_target_pairs={{0,2},{2,0},{4,6},{6,4},{8,10},{10,8},{12,14},{14,12},{16,18},{18,... | collective-permute-start | bytes 4325384 | tf_op jit(solution)/shard_map/ppermute | solution.py:50
  180.8 16.4 %collective-permute-start.39 = (bf16[2,128,1024]{2,1,0:T(8,128)(2,1)S(1)}, bf16[2,128,1024]{2,1,0:T(8,128)(2,1)S(1)}, u32[]{:S(2)}, u32[]{:S(2)}) collective-permute-start(bf16[2,128,1024]{2,1,0:T(8,128)(2,1)S(1)} %select.53.refs_0_), channel_id=1, source_target_pairs={{0,1},{1,0},{2,3},{3,2},{4,5},{5,4},{6,7},{7,6},{8,9},{9,8},{10,11... | collective-permute-start | bytes 1572872 | tf_op jit(solution)/shard_map/ppermute | solution.py:46
  181.4 23.2 %collective-permute-start.47 = (bf16[272,1024]{1,0:T(8,128)(2,1)S(1)}, bf16[272,1024]{1,0:T(8,128)(2,1)S(1)}, u32[]{:S(2)}, u32[]{:S(2)}) collective-permute-start(bf16[272,1024]{1,0:T(8,128)(2,1)S(1)} %collective-permute-done.37.refs_0_), channel_id=1, source_target_pairs={{4,12},{6,14},{12,20},{14,22},{20,28},{22,30},{28,24},{30,26},{24,... | collective-permute-start | bytes 1671176 | tf_op jit(solution)/shard_map/ppermute | solution.py:576
  192.8 17.1 %collective-permute-start.32 = (bf16[2,192,704]{2,1,0:T(8,128)(2,1)S(1)}, bf16[2,192,704]{2,1,0:T(8,128)(2,1)S(1)}, u32[]{:S(2)}, u32[]{:S(2)}) collective-permute-start(bf16[2,192,704]{2,1,0:T(8,128)(2,1)S(1)} %expert_in.4.refs_0_), channel_id=1, source_target_pairs={{0,1},{1,0},{2,3},{3,2},{4,5},{5,4},{6,7},{7,6},{8,9},{9,8},{10,11... | collective-permute-start | bytes 1622024 | tf_op jit(solution)/shard_map/ppermute | solution.py:46
  197.2 23.9 %collective-permute-start.43 = (bf16[2,128,1024]{2,1,0:T(8,128)(2,1)S(1)}, bf16[2,128,1024]{2,1,0:T(8,128)(2,1)S(1)}, u32[]{:S(2)}, u32[]{:S(2)}) collective-permute-start(bf16[2,128,1024]{2,1,0:T(8,128)(2,1)S(1)} %select.54.refs_0_), channel_id=1, source_target_pairs={{0,1},{1,0},{2,3},{3,2},{4,5},{5,4},{6,7},{7,6},{8,9},{9,8},{10,11... | collective-permute-start | bytes 1572872 | tf_op jit(solution)/shard_map/ppermute | solution.py:46
  204.6 26.8 %collective-permute-start.40 = (bf16[2,128,704]{2,1,0:T(8,128)(2,1)S(1)}, bf16[2,128,704]{2,1,0:T(8,128)(2,1)S(1)}, u32[]{:S(2)}, u32[]{:S(2)}) collective-permute-start(bf16[2,128,704]{2,1,0:T(8,128)(2,1)S(1)} %expert_in.5.refs_0_), channel_id=1, source_target_pairs={{0,1},{1,0},{2,3},{3,2},{4,5},{5,4},{6,7},{7,6},{8,9},{9,8},{10,11... | collective-permute-start | bytes 1081352 | tf_op jit(solution)/shard_map/ppermute | solution.py:46
  207.0 28.2 %collective-permute-start.48 = (bf16[2,64,1024]{2,1,0:T(8,128)(2,1)S(1)}, bf16[2,64,1024]{2,1,0:T(8,128)(2,1)S(1)}, u32[]{:S(2)}, u32[]{:S(2)}) collective-permute-start(bf16[2,64,1024]{2,1,0:T(8,128)(2,1)S(1)} %select.55.refs_0_), channel_id=1, source_target_pairs={{0,1},{1,0},{2,3},{3,2},{4,5},{5,4},{6,7},{7,6},{8,9},{9,8},{10,11... | collective-permute-start | bytes 786440 | tf_op jit(solution)/shard_map/ppermute | solution.py:46
  228.0 17.7 %collective-permute-start.44 = (bf16[2,128,704]{2,1,0:T(8,128)(2,1)S(1)}, bf16[2,128,704]{2,1,0:T(8,128)(2,1)}, u32[]{:S(2)}, u32[]{:S(2)}) collective-permute-start(bf16[2,128,704]{2,1,0:T(8,128)(2,1)S(1)} %expert_in.6.refs_0_), channel_id=1, source_target_pairs={{0,1},{1,0},{2,3},{3,2},{4,5},{5,4},{6,7},{7,6},{8,9},{9,8},{10,11... | collective-permute-start | bytes 1081352 | tf_op jit(solution)/shard_map/ppermute | solution.py:46
  229.4 26.1 %collective-permute-start.35 = (bf16[2,64,1024]{2,1,0:T(8,128)(2,1)}, bf16[2,64,1024]{2,1,0:T(8,128)(2,1)}, u32[]{:S(2)}, u32[]{:S(2)}) collective-permute-start(bf16[2,64,1024]{2,1,0:T(8,128)(2,1)} %get-tuple-element.57), channel_id=1, source_target_pairs={{4,0},{6,2},{12,4},{14,6},{20,12},{22,14},{28,20},{30,22},{24,28},... | collective-permute-start | bytes 786440 | tf_op jit(solution)/shard_map/ppermute | solution.py:606
  229.8 35.1 %collective-permute-start.36 = (bf16[2,64,1024]{2,1,0:T(8,128)(2,1)}, bf16[2,64,1024]{2,1,0:T(8,128)(2,1)}, u32[]{:S(2)}, u32[]{:S(2)}) collective-permute-start(bf16[2,64,1024]{2,1,0:T(8,128)(2,1)} %get-tuple-element.58), channel_id=1, source_target_pairs={{4,12},{6,14},{12,20},{14,22},{20,28},{22,30},{28,24},{30,26},{24,... | collective-permute-start | bytes 786440 | tf_op jit(solution)/shard_map/ppermute | solution.py:606
  242.4 15.1 %collective-permute-start.49 = (bf16[2,64,704]{2,1,0:T(8,128)(2,1)}, bf16[2,64,704]{2,1,0:T(8,128)(2,1)}, u32[]{:S(2)}, u32[]{:S(2)}) collective-permute-start(bf16[2,64,704]{2,1,0:T(8,128)(2,1)} %expert_in.7.refs_0_), channel_id=1, source_target_pairs={{0,1},{1,0},{2,3},{3,2},{4,5},{5,4},{6,7},{7,6},{8,9},{9,8},{10,11... | collective-permute-start | bytes 540680 | tf_op jit(solution)/shard_map/ppermute | solution.py:46
  244.6 24.3 %collective-permute-start.41 = (bf16[2,64,1024]{2,1,0:T(8,128)(2,1)}, bf16[2,64,1024]{2,1,0:T(8,128)(2,1)}, u32[]{:S(2)}, u32[]{:S(2)}) collective-permute-start(bf16[2,64,1024]{2,1,0:T(8,128)(2,1)} %copy-done.26), channel_id=1, source_target_pairs={{4,8},{6,10},{12,0},{14,2},{20,4},{22,6},{28,12},{30,14},{24,20},{... | collective-permute-start | bytes 786440 | tf_op jit(solution)/shard_map/ppermute | solution.py:606
  245.7 23.2 %collective-permute-start.42 = (bf16[2,64,1024]{2,1,0:T(8,128)(2,1)}, bf16[2,64,1024]{2,1,0:T(8,128)(2,1)}, u32[]{:S(2)}, u32[]{:S(2)}) collective-permute-start(bf16[2,64,1024]{2,1,0:T(8,128)(2,1)} %copy-done.25), channel_id=1, source_target_pairs={{4,20},{6,22},{12,28},{14,30},{20,24},{22,26},{28,16},{30,18},{24,... | collective-permute-start | bytes 786440 | tf_op jit(solution)/shard_map/ppermute | solution.py:606
  255.5 26.2 %collective-permute-start.45 = (bf16[2,64,1024]{2,1,0:T(8,128)(2,1)}, bf16[2,64,1024]{2,1,0:T(8,128)(2,1)}, u32[]{:S(2)}, u32[]{:S(2)}) collective-permute-start(bf16[2,64,1024]{2,1,0:T(8,128)(2,1)} %get-tuple-element.66), channel_id=1, source_target_pairs={{4,16},{6,18},{12,8},{14,10},{20,0},{22,2},{28,4},{30,6},{24,12},{... | collective-permute-start | bytes 786440 | tf_op jit(solution)/shard_map/ppermute | solution.py:606
  257.5 24.1 %collective-permute-start.46 = (bf16[2,64,1024]{2,1,0:T(8,128)(2,1)}, bf16[2,64,1024]{2,1,0:T(8,128)(2,1)}, u32[]{:S(2)}, u32[]{:S(2)}) collective-permute-start(bf16[2,64,1024]{2,1,0:T(8,128)(2,1)} %get-tuple-element.67), channel_id=1, source_target_pairs={{4,28},{6,30},{12,24},{14,26},{20,16},{22,18},{28,8},{30,10},{24,0... | collective-permute-start | bytes 786440 | tf_op jit(solution)/shard_map/ppermute | solution.py:606
  264.9 22.2 %collective-permute-start.50 = (bf16[2,64,1024]{2,1,0:T(8,128)(2,1)}, bf16[2,64,1024]{2,1,0:T(8,128)(2,1)S(1)}, u32[]{:S(2)}, u32[]{:S(2)}) collective-permute-start(bf16[2,64,1024]{2,1,0:T(8,128)(2,1)} %expert_out.7), channel_id=1, source_target_pairs={{4,24},{6,26},{12,16},{14,18},{20,8},{22,10},{28,0},{30,2},{24,4},... | collective-permute-start | bytes 786440 | tf_op jit(solution)/shard_map/ppermute | solution.py:606
  (42 other events, 571.3 us)
